TPU v7x, 768 devices: a whole 4x8x12 slice. The times are simulated.
768 devices in a mesh: gx: 48 (over x, z_lo, core), gy: 16 (over z_hi, y).
Axes of the slice: x: 4, y: 8, z: 12 (z_hi: 2, z_lo: 6; z = z_hi * 6 + z_lo), core: 2. Of those that a mesh axis runs over, the one named last changes fastest.
Arguments:
- fine_now: float32 [3, 384, 256, 128], P(None, 'gx', 'gy'), may hold values from -6 to 6
- fine_prev: float32 [3, 384, 256, 128], P(None, 'gx', 'gy'), may hold values from -6 to 6
- coarse_now: float32 [3, 192, 128, 128], P(None, 'gx', 'gy'), may hold values from -6 to 6
- coarse_prev: float32 [3, 192, 128, 128], P(None, 'gx', 'gy'), may hold values from -6 to 6
- fine_rho: float32 [384, 256, 128], P('gx', 'gy'), may hold values from 1 to 3
- fine_mu: float32 [384, 256, 128], P('gx', 'gy'), may hold values from 0.3 to 1.5
- fine_lam: float32 [384, 256, 128], P('gx', 'gy'), may hold values from 0.3 to 1.5
- fine_metric: float32 [384, 256, 128], P('gx', 'gy'), may hold values from 0.5 to 2
- coarse_rho: float32 [192, 128, 128], P('gx', 'gy'), may hold values from 1 to 3
- coarse_mu: float32 [192, 128, 128], P('gx', 'gy'), may hold values from 0.3 to 1.5
- coarse_lam: float32 [192, 128, 128], P('gx', 'gy'), may hold values from 0.3 to 1.5
- coarse_metric: float32 [192, 128, 128], P('gx', 'gy'), may hold values from 0.5 to 2
- couple_index: int32 [384, 256, 16], P('gx', 'gy'), may hold values from 0 to 95, as said below
- couple_weight: float32 [384, 256, 16], P('gx', 'gy'), may hold values from 0 to 0.125
Outputs:
- fine_field: float32 [3, 384, 256, 128], P(None, 'gx', 'gy')
- coarse_field: float32 [3, 192, 128, 128], P(None, 'gx', 'gy')
Inputs may be any that keep to these rules, and one draw needn't show every extreme that they name: `couple_index`: the sixteen indices of a fine point are a 4 x 4 patch of neighbouring coarse cells of its block's widened top plane, lying within 2 coarse cells of the point's own coarse cell.
All inputs are finite; a program needn't handle non-finite values.
Results may differ from a plain program's by a relative error of at most 0.0001.
Values sent between devices are 32-bit elements; how exact they have to be, the bound alone decides.
No kernel may reach another device: no remote copies, remote signals or barrier semaphores. Data moves between devices by JAX's collectives and lax.ppermute only.
A program may use at most 32 MiB of HBM per device.

v0:
```python
import jax
import jax.numpy as jnp
import numpy as np
from jax import lax
from jax.sharding import PartitionSpec as P

time_step = 0.25


def padded(shard, sides, width):
    for axis, dim in sides:
        size, length = (lax.axis_size(axis), shard.shape[dim])
        up = [(i, (i + 1) % size) for i in range(size - 1)]
        down = [(j, i) for i, j in up]
        last = lax.slice_in_dim(shard, length - width, length, axis=dim)
        initial = lax.slice_in_dim(shard, 0, width, axis=dim)
        before = lax.ppermute(last, axis, up)
        after = lax.ppermute(initial, axis, down)
        shard = jnp.concatenate([before, shard, after], axis=dim)
    return shard


def vertical_table(layers):
    matrix = np.zeros((layers, layers))
    for centre in range(2, layers - 2):
        matrix[centre, centre - 2] = 1.0 / 12.0
        matrix[centre, centre - 1] = -8.0 / 12.0
        matrix[centre, centre + 1] = 8.0 / 12.0
        matrix[centre, centre + 2] = -1.0 / 12.0
    matrix[0, 0] = -1.5
    matrix[0, 1] = 2.0
    matrix[0, 2] = -0.5
    matrix[1, 0] = -0.5
    matrix[1, 2] = 0.5
    matrix[layers - 2, layers - 3] = -0.5
    matrix[layers - 2, layers - 1] = 0.5
    matrix[layers - 1, layers - 3] = 0.5
    matrix[layers - 1, layers - 2] = -2.0
    matrix[layers - 1, layers - 1] = 1.5
    return jnp.asarray(matrix.T, jnp.float32)


def vertical(values, depth_table):
    return jnp.matmul(values, depth_table, precision=lax.Precision.HIGHEST)


def stencil_sum(source, along, weights):
    extent = source.shape[along] - 4
    running = None
    for offset in range(5):
        if weights[offset] != 0.0:
            contrib = weights[offset] * lax.slice_in_dim(
                source, offset, offset + extent, axis=along
            )
            running = contrib if running is None else running + contrib
    return running


def advance(
    widened, lifted, present, earlier, metric, density, shear, lame_first, depth_table, spacing
):
    first_taps = [c / (12.0 * spacing) for c in (1.0, -8.0, 0.0, 8.0, -1.0)]
    second_taps = [c / (12.0 * spacing * spacing) for c in (-1.0, 16.0, -30.0, 16.0, -1.0)]
    curve_x = stencil_sum(widened[:, :, 2:-2], 1, second_taps)
    curve_y = stencil_sum(widened[:, 2:-2], 2, second_taps)
    cross_one = stencil_sum(stencil_sum(widened[1], 1, first_taps), 0, first_taps)
    cross_zero = stencil_sum(stencil_sum(widened[0], 0, first_taps), 1, first_taps)
    lifted_dx = stencil_sum(lifted[:, 2:-2], 0, first_taps)
    lifted_dy = stencil_sum(lifted[2:-2], 1, first_taps)
    along_x = stencil_sum(widened[0, :, 2:-2], 0, first_taps)
    along_y = stencil_sum(widened[1, 2:-2], 1, first_taps)
    lifted_in = lifted[2:-2, 2:-2]
    slopes = metric * vertical(present[0:2], depth_table)
    stacked = jnp.concatenate([slopes, lifted_in[None], (along_x + along_y + lifted_in)[None]], 0)
    bent_terms = metric * vertical(stacked, depth_table)
    laplace = curve_x + curve_y + bent_terms[0:3]
    grad_div = jnp.stack(
        [curve_x[0] + cross_one + lifted_dx, cross_zero + curve_y[1] + lifted_dy, bent_terms[3]], 0
    )
    acceleration = (shear * laplace + (lame_first + shear) * grad_div) / density
    return 2.0 * present - earlier + time_step * time_step * acceleration


def interpolate(flat_plane, targets, mixing):
    return jnp.sum(flat_plane[:, targets] * mixing, axis=-1)


def on_device(
    fine_now,
    fine_prev,
    coarse_now,
    coarse_prev,
    fine_rho,
    fine_mu,
    fine_lam,
    fine_metric,
    coarse_rho,
    coarse_mu,
    coarse_lam,
    coarse_metric,
    couple_index,
    couple_weight,
):
    depth_table = vertical_table(fine_now.shape[3])
    fine_edge = padded(fine_metric, (("gx", 0), ("gy", 1)), 2)
    coarse_edge = padded(coarse_metric, (("gx", 0), ("gy", 1)), 2)
    for marching in range(2):
        fine_widened = padded(fine_now, (("gx", 1), ("gy", 2)), 2)
        fine_lift = fine_edge * vertical(fine_widened[2], depth_table)
        fine_next = advance(
            fine_widened,
            fine_lift,
            fine_now,
            fine_prev,
            fine_metric,
            fine_rho,
            fine_mu,
            fine_lam,
            depth_table,
            1.0,
        )
        widened = padded(coarse_now, (("gx", 1), ("gy", 2)), 2)
        coarse_lift = coarse_edge * vertical(widened[2], depth_table)
        coarse_next = advance(
            widened,
            coarse_lift,
            coarse_now,
            coarse_prev,
            coarse_metric,
            coarse_rho,
            coarse_mu,
            coarse_lam,
            depth_table,
            2.0,
        )
        top_plane = coarse_next[:, :, :, coarse_next.shape[3] - 1]
        plane_wide = padded(top_plane, (("gx", 1), ("gy", 2)), 2)
        interface_values = interpolate(plane_wide.reshape(3, -1), couple_index, couple_weight)
        fine_next = fine_next.at[:, :, :, 0].set(interface_values)
        fine_prev, fine_now = (fine_now, fine_next)
        coarse_prev, coarse_now = (coarse_now, coarse_next)
    return (fine_now, coarse_now)


def solution(mesh):
    return jax.shard_map(
        on_device,
        mesh=mesh,
        in_specs=(
            P(None, "gx", "gy", None),
            P(None, "gx", "gy", None),
            P(None, "gx", "gy", None),
            P(None, "gx", "gy", None),
            P("gx", "gy", None),
            P("gx", "gy", None),
            P("gx", "gy", None),
            P("gx", "gy", None),
            P("gx", "gy", None),
            P("gx", "gy", None),
            P("gx", "gy", None),
            P("gx", "gy", None),
            P("gx", "gy", None),
            P("gx", "gy", None),
        ),
        out_specs=(P(None, "gx", "gy", None), P(None, "gx", "gy", None)),
        check_vma=False,
    )
```

profile of v0, /device:TPU:58, one launch (start us, length us, event | category | flops | bytes accessed | tf_op | source)
XLA Modules:
  0.0 244.3 jit_solution(4354605459491826448)
XLA Ops:
  0.6 0.8 fusion.263
  1.4 1.9 collective-permute-start.8
  3.3 12.1 %collective-permute-start.9 = (f32[3,2,8,128]{3,2,1,0:T(8,128)S(1)}, f32[3,2,8,128]{3,2,1,0:T(8,128)S(1)}, u32[]{:S(2)}, u32[]{:S(2)}) collective-permute-start(f32[3,2,8,128]{3,2,1,0:T(8,128)S(1)} %get-tuple-element.76), channel_id=1, source_target_pairs={{16,0},{32,16},{48,32},{64,48},{80,64},{96,80},{112,96},{128,112},... | collective-permute-start | bytes 73736 | tf_op jit(solution)/shard_map/ppermute | solution.py:18
  15.5 1.9 collective-permute-start.12
  17.5 9.5 %collective-permute-start.13 = (f32[2,8,128]{2,1,0:T(8,128)S(1)}, f32[2,8,128]{2,1,0:T(8,128)S(1)}, u32[]{:S(2)}, u32[]{:S(2)}) collective-permute-start(f32[2,8,128]{2,1,0:T(8,128)S(1)} %get-tuple-element.88), channel_id=1, source_target_pairs={{16,0},{32,16},{48,32},{64,48},{80,64},{96,80},{112,96},{128,112},... | collective-permute-start | bytes 24584 | tf_op jit(solution)/shard_map/ppermute | solution.py:18
  26.9 0.8 fusion.258
  27.8 2.1 collective-permute-start
  31.8 9.3 %collective-permute-start.1 = (f32[3,2,16,128]{3,2,1,0:T(8,128)S(1)}, f32[3,2,16,128]{3,2,1,0:T(8,128)S(1)}, u32[]{:S(2)}, u32[]{:S(2)}) collective-permute-start(f32[3,2,16,128]{3,2,1,0:T(8,128)S(1)} %get-tuple-element.47), channel_id=1, source_target_pairs={{16,0},{32,16},{48,32},{64,48},{80,64},{96,80},{112,96},{128,112},... | collective-permute-start | bytes 147464 | tf_op jit(solution)/shard_map/ppermute | solution.py:18
  41.2 1.9 collective-permute-start.4
  43.2 8.8 %collective-permute-done.4 = f32[2,16,128]{2,1,0:T(8,128)S(1)} collective-permute-done((f32[2,16,128]{2,1,0:T(8,128)S(1)}, f32[2,16,128]{2,1,0:T(8,128)S(1)}, u32[]{:S(2)}, u32[]{:S(2)}) %collective-permute-start.4) | collective-permute-done | bytes 16416 | tf_op jit(solution)/shard_map/ppermute | solution.py:17
  52.0 1.9 collective-permute-start.5
  53.9 1.4 collective-permute-done.5
  55.3 11.5 %collective-permute-start.14 = (f32[8,2,128]{2,1,0:T(2,128)S(1)}, f32[8,2,128]{2,1,0:T(2,128)S(1)}, u32[]{:S(2)}, u32[]{:S(2)}) collective-permute-start(f32[8,2,128]{2,1,0:T(2,128)S(1)} %get-tuple-element.82), channel_id=1, source_target_pairs={{0,1},{1,2},{2,3},{3,4},{4,5},{5,6},{6,7},{7,8},{8,9},{9,10},{10,1... | collective-permute-start | bytes 24584 | tf_op jit(solution)/shard_map/ppermute | solution.py:17
  67.0 3.5 %collective-permute-start.10 = (f32[3,8,2,128]{3,2,1,0:T(2,128)S(1)}, f32[3,8,2,128]{3,2,1,0:T(2,128)S(1)}, u32[]{:S(2)}, u32[]{:S(2)}) collective-permute-start(f32[3,8,2,128]{3,2,1,0:T(2,128)S(1)} %get-tuple-element.57), channel_id=1, source_target_pairs={{0,1},{1,2},{2,3},{3,4},{4,5},{5,6},{6,7},{7,8},{8,9},{9,10},{10,1... | collective-permute-start | bytes 73736 | tf_op jit(solution)/shard_map/ppermute | solution.py:17
  70.5 2.4 collective-permute-start.11
  72.9 1.9 collective-permute-start.15
  74.8 9.8 %collective-permute-done.11 = f32[3,8,2,128]{3,2,1,0:T(2,128)S(1)} collective-permute-done((f32[3,8,2,128]{3,2,1,0:T(2,128)S(1)}, f32[3,8,2,128]{3,2,1,0:T(2,128)S(1)}, u32[]{:S(2)}, u32[]{:S(2)}) %collective-permute-start.11) | collective-permute-done | bytes 24608 | tf_op jit(solution)/shard_map/ppermute | solution.py:18
  84.6 2.5 %collective-permute-start.6 = (f32[12,2,128]{2,1,0:T(2,128)S(1)}, f32[12,2,128]{2,1,0:T(2,128)S(1)}, u32[]{:S(2)}, u32[]{:S(2)}) collective-permute-start(f32[12,2,128]{2,1,0:T(2,128)S(1)} %get-tuple-element.59), channel_id=1, source_target_pairs={{0,1},{1,2},{2,3},{3,4},{4,5},{5,6},{6,7},{7,8},{8,9},{9,10},{10,1... | collective-permute-start | bytes 36872 | tf_op jit(solution)/shard_map/ppermute | solution.py:17
  87.4 3.3 %collective-permute-start.7 = (f32[12,2,128]{2,1,0:T(2,128)S(1)}, f32[12,2,128]{2,1,0:T(2,128)S(1)}, u32[]{:S(2)}, u32[]{:S(2)}) collective-permute-start(f32[12,2,128]{2,1,0:T(2,128)S(1)} %get-tuple-element.60), channel_id=1, source_target_pairs={{1,0},{2,1},{3,2},{4,3},{5,4},{6,5},{7,6},{8,7},{9,8},{10,9},{11,1... | collective-permute-start | bytes 36872 | tf_op jit(solution)/shard_map/ppermute | solution.py:18
  92.4 1.9 collective-permute-start.16
  94.4 9.3 %collective-permute-start.17 = (f32[3,2,8]{2,1,0:T(2,128)S(1)}, f32[3,2,8]{2,1,0:T(2,128)S(1)}, u32[]{:S(2)}, u32[]{:S(2)}) collective-permute-start(f32[3,2,8]{2,1,0:T(2,128)S(1)} %get-tuple-element.95), channel_id=1, source_target_pairs={{16,0},{32,16},{48,32},{64,48},{80,64},{96,80},{112,96},{128,112},... | collective-permute-start | bytes 584 | tf_op jit(solution)/shard_map/ppermute | solution.py:18
  103.8 1.9 collective-permute-start.24
  105.9 11.0 %collective-permute-start.18 = (f32[3,8,2]{2,1,0:T(8,128)S(1)}, f32[3,8,2]{2,1,0:T(8,128)S(1)}, u32[]{:S(2)}, u32[]{:S(2)}) collective-permute-start(f32[3,8,2]{2,1,0:T(8,128)S(1)} %get-tuple-element.90), channel_id=1, source_target_pairs={{0,1},{1,2},{2,3},{3,4},{4,5},{5,6},{6,7},{7,8},{8,9},{9,10},{10,1... | collective-permute-start | bytes 584 | tf_op jit(solution)/shard_map/ppermute | solution.py:17
  116.9 1.9 collective-permute-start.19
  118.8 8.5 %collective-permute-start.25 = (f32[3,2,8,128]{3,2,1,0:T(8,128)S(1)}, f32[3,2,8,128]{3,2,1,0:T(8,128)S(1)}, u32[]{:S(2)}, u32[]{:S(2)}) collective-permute-start(f32[3,2,8,128]{3,2,1,0:T(8,128)S(1)} %get-tuple-element.70), channel_id=1, source_target_pairs={{16,0},{32,16},{48,32},{64,48},{80,64},{96,80},{112,96},{128,112},... | collective-permute-start | bytes 73736 | tf_op jit(solution)/shard_map/ppermute | solution.py:18
  127.3 3.6 %collective-permute-done.19 = f32[3,8,2]{2,1,0:T(8,128)S(1)} collective-permute-done((f32[3,8,2]{2,1,0:T(8,128)S(1)}, f32[3,8,2]{2,1,0:T(8,128)S(1)}, u32[]{:S(2)}, u32[]{:S(2)}) %collective-permute-start.19) | collective-permute-done | bytes 224 | tf_op jit(solution)/shard_map/ppermute | solution.py:18
  130.9 9.1 %collective-permute-start.2 = (f32[3,12,2,128]{3,2,1,0:T(2,128)S(1)}, f32[3,12,2,128]{3,2,1,0:T(2,128)S(1)}, u32[]{:S(2)}, u32[]{:S(2)}) collective-permute-start(f32[3,12,2,128]{3,2,1,0:T(2,128)S(1)} %get-tuple-element.34), channel_id=1, source_target_pairs={{0,1},{1,2},{2,3},{3,4},{4,5},{5,6},{6,7},{7,8},{8,9},{9,10},{10,1... | collective-permute-start | bytes 110600 | tf_op jit(solution)/shard_map/ppermute | solution.py:17
  140.2 5.5 %gather_fusion = f32[2048,3]{1,0:T(8,128)S(1)} fusion(f32[3,96]{0,1:T(8,128)S(1)} %copy.23, s32[2048]{0:T(1024)S(1)} %broadcast_clamp_fusion), kind=kCustom, calls=%fused_computation | custom fusion | bytes 57344 | tf_op jit(solution)/shard_map/gather | solution.py:85
  145.7 1.9 collective-permute-start.3
  147.7 12.3 %collective-permute-start.26 = (f32[3,8,2,128]{3,2,1,0:T(2,128)S(1)}, f32[3,8,2,128]{3,2,1,0:T(2,128)S(1)}, u32[]{:S(2)}, u32[]{:S(2)}) collective-permute-start(f32[3,8,2,128]{3,2,1,0:T(2,128)S(1)} %get-tuple-element.55), channel_id=1, source_target_pairs={{0,1},{1,2},{2,3},{3,4},{4,5},{5,6},{6,7},{7,8},{8,9},{9,10},{10,1... | collective-permute-start | bytes 73736 | tf_op jit(solution)/shard_map/ppermute | solution.py:17
  160.1 1.9 collective-permute-start.27
  163.2 11.0 %collective-permute-done.27 = f32[3,8,2,128]{3,2,1,0:T(2,128)S(1)} collective-permute-done((f32[3,8,2,128]{3,2,1,0:T(2,128)S(1)}, f32[3,8,2,128]{3,2,1,0:T(2,128)S(1)}, u32[]{:S(2)}, u32[]{:S(2)}) %collective-permute-start.27) | collective-permute-done | bytes 24608 | tf_op jit(solution)/shard_map/ppermute | solution.py:18
  175.1 1.9 collective-permute-start.28
  177.0 9.3 %collective-permute-start.29 = (f32[3,2,8]{2,1,0:T(2,128)S(1)}, f32[3,2,8]{2,1,0:T(2,128)S(1)}, u32[]{:S(2)}, u32[]{:S(2)}) collective-permute-start(f32[3,2,8]{2,1,0:T(2,128)S(1)} %get-tuple-element.97), channel_id=1, source_target_pairs={{16,0},{32,16},{48,32},{64,48},{80,64},{96,80},{112,96},{128,112},... | collective-permute-start | bytes 584 | tf_op jit(solution)/shard_map/ppermute | solution.py:18
  186.5 1.2 collective-permute-done.29
  187.8 1.9 collective-permute-start.30
  189.7 3.9 %collective-permute-start.31 = (f32[3,8,2]{2,1,0:T(8,128)S(1)}, f32[3,8,2]{2,1,0:T(8,128)S(1)}, u32[]{:S(2)}, u32[]{:S(2)}) collective-permute-start(f32[3,8,2]{2,1,0:T(8,128)S(1)} %get-tuple-element.93), channel_id=1, source_target_pairs={{1,0},{2,1},{3,2},{4,3},{5,4},{6,5},{7,6},{8,7},{9,8},{10,9},{11,1... | collective-permute-start | bytes 584 | tf_op jit(solution)/shard_map/ppermute | solution.py:18
  193.7 1.1 fusion.39
  194.7 9.0 %collective-permute-done.31 = f32[3,8,2]{2,1,0:T(8,128)S(1)} collective-permute-done((f32[3,8,2]{2,1,0:T(8,128)S(1)}, f32[3,8,2]{2,1,0:T(8,128)S(1)}, u32[]{:S(2)}, u32[]{:S(2)}) %collective-permute-start.31) | collective-permute-done | bytes 224 | tf_op jit(solution)/shard_map/ppermute | solution.py:18
  204.0 5.5 %gather_fusion.1 = f32[2048,3]{1,0:T(8,128)S(1)} fusion(f32[3,96]{0,1:T(8,128)S(1)} %copy.26, s32[2048]{0:T(1024)S(1)} %broadcast_clamp_fusion), kind=kCustom, calls=%fused_computation.1 | custom fusion | bytes 57344 | tf_op jit(solution)/shard_map/gather | solution.py:85
  209.5 1.3 multiply_reduce_fusion
  210.7 0.9 copy.25
  211.9 1.9 collective-permute-start.20
  213.8 9.5 %collective-permute-start.21 = (f32[3,2,16,128]{3,2,1,0:T(8,128)S(1)}, f32[3,2,16,128]{3,2,1,0:T(8,128)S(1)}, u32[]{:S(2)}, u32[]{:S(2)}) collective-permute-start(f32[3,2,16,128]{3,2,1,0:T(8,128)S(1)} %get-tuple-element.37), channel_id=1, source_target_pairs={{16,0},{32,16},{48,32},{64,48},{80,64},{96,80},{112,96},{128,112},... | collective-permute-start | bytes 147464 | tf_op jit(solution)/shard_map/ppermute | solution.py:18
  223.6 0.9 copy.28
  225.1 1.9 collective-permute-start.22
  227.0 3.9 %collective-permute-start.23 = (f32[3,12,2,128]{3,2,1,0:T(2,128)S(1)}, f32[3,12,2,128]{3,2,1,0:T(2,128)S(1)}, u32[]{:S(2)}, u32[]{:S(2)}) collective-permute-start(f32[3,12,2,128]{3,2,1,0:T(2,128)S(1)} %get-tuple-element.33), channel_id=1, source_target_pairs={{1,0},{2,1},{3,2},{4,3},{5,4},{6,5},{7,6},{8,7},{9,8},{10,9},{11,1... | collective-permute-start | bytes 110600 | tf_op jit(solution)/shard_map/ppermute | solution.py:18
  231.0 10.3 %collective-permute-done.23 = f32[3,12,2,128]{3,2,1,0:T(2,128)S(1)} collective-permute-done((f32[3,12,2,128]{3,2,1,0:T(2,128)S(1)}, f32[3,12,2,128]{3,2,1,0:T(2,128)S(1)}, u32[]{:S(2)}, u32[]{:S(2)}) %collective-permute-start.23) | collective-permute-done | bytes 36896 | tf_op jit(solution)/shard_map/ppermute | solution.py:18
  (161 shorter events, 10.8 us)
Async XLA Ops:
  0.6 14.8 %copy-start.7 = (f32[4,8,128]{2,1,0:T(8,128)S(1)}, f32[4,8,128]{2,1,0:T(8,128)}, u32[]{:S(2)}) copy-start(f32[4,8,128]{2,1,0:T(8,128)} %param.30) | copy-start | bytes 49156
  1.4 65.5 %collective-permute-start.8 = (f32[3,2,8,128]{3,2,1,0:T(8,128)S(1)}, f32[3,2,8,128]{3,2,1,0:T(8,128)S(1)}, u32[]{:S(2)}, u32[]{:S(2)}) collective-permute-start(f32[3,2,8,128]{3,2,1,0:T(8,128)S(1)} %get-tuple-element.77), channel_id=1, source_target_pairs={{0,16},{16,32},{32,48},{48,64},{64,80},{80,96},{96,112},{112,128},... | collective-permute-start | bytes 73736 | tf_op jit(solution)/shard_map/ppermute | solution.py:17
  3.3 63.6 %collective-permute-start.9 = (f32[3,2,8,128]{3,2,1,0:T(8,128)S(1)}, f32[3,2,8,128]{3,2,1,0:T(8,128)S(1)}, u32[]{:S(2)}, u32[]{:S(2)}) collective-permute-start(f32[3,2,8,128]{3,2,1,0:T(8,128)S(1)} %get-tuple-element.76), channel_id=1, source_target_pairs={{16,0},{32,16},{48,32},{64,48},{80,64},{96,80},{112,96},{128,112},... | collective-permute-start | bytes 73736 | tf_op jit(solution)/shard_map/ppermute | solution.py:18
  15.5 14.4 %copy-start.3 = (f32[3,4,8,128]{3,2,1,0:T(8,128)S(1)}, f32[3,4,8,128]{3,2,1,0:T(8,128)}, u32[]{:S(2)}) copy-start(f32[3,4,8,128]{3,2,1,0:T(8,128)} %param.21) | copy-start | bytes 147460
  15.5 16.3 %collective-permute-start.12 = (f32[2,8,128]{2,1,0:T(8,128)S(1)}, f32[2,8,128]{2,1,0:T(8,128)S(1)}, u32[]{:S(2)}, u32[]{:S(2)}) collective-permute-start(f32[2,8,128]{2,1,0:T(8,128)S(1)} %get-tuple-element.89), channel_id=1, source_target_pairs={{0,16},{16,32},{32,48},{48,64},{64,80},{80,96},{96,112},{112,128},... | collective-permute-start | bytes 24584 | tf_op jit(solution)/shard_map/ppermute | solution.py:17
  17.4 12.4 %copy-start.1 = (f32[128,128,1,1]{1,0,3,2:T(8,128)S(1)}, f32[128,128,1,1]{1,0,3,2:T(8,128)}, u32[]{:S(2)}) copy-start(f32[128,128,1,1]{1,0,3,2:T(8,128)} %constant.117) | copy-start | bytes 196612
  17.4 12.6 %copy-start = (f32[3,8,16,128]{3,2,1,0:T(8,128)S(1)}, f32[3,8,16,128]{3,2,1,0:T(8,128)}, u32[]{:S(2)}) copy-start(f32[3,8,16,128]{3,2,1,0:T(8,128)} %param.19) | copy-start | bytes 589828
  17.5 23.8 %collective-permute-start.13 = (f32[2,8,128]{2,1,0:T(8,128)S(1)}, f32[2,8,128]{2,1,0:T(8,128)S(1)}, u32[]{:S(2)}, u32[]{:S(2)}) collective-permute-start(f32[2,8,128]{2,1,0:T(8,128)S(1)} %get-tuple-element.88), channel_id=1, source_target_pairs={{16,0},{32,16},{48,32},{64,48},{80,64},{96,80},{112,96},{128,112},... | collective-permute-start | bytes 24584 | tf_op jit(solution)/shard_map/ppermute | solution.py:18
  27.8 2.3 copy-start.2
  27.8 66.6 %collective-permute-start = (f32[3,2,16,128]{3,2,1,0:T(8,128)S(1)}, f32[3,2,16,128]{3,2,1,0:T(8,128)S(1)}, u32[]{:S(2)}, u32[]{:S(2)}) collective-permute-start(f32[3,2,16,128]{3,2,1,0:T(8,128)S(1)} %get-tuple-element.48), channel_id=1, source_target_pairs={{0,16},{16,32},{32,48},{48,64},{64,80},{80,96},{96,112},{112,128},... | collective-permute-start | bytes 147464 | tf_op jit(solution)/shard_map/ppermute | solution.py:17
  30.9 0.9 copy-start.6
  31.8 72.0 %collective-permute-start.1 = (f32[3,2,16,128]{3,2,1,0:T(8,128)S(1)}, f32[3,2,16,128]{3,2,1,0:T(8,128)S(1)}, u32[]{:S(2)}, u32[]{:S(2)}) collective-permute-start(f32[3,2,16,128]{3,2,1,0:T(8,128)S(1)} %get-tuple-element.47), channel_id=1, source_target_pairs={{16,0},{32,16},{48,32},{64,48},{80,64},{96,80},{112,96},{128,112},... | collective-permute-start | bytes 147464 | tf_op jit(solution)/shard_map/ppermute | solution.py:18
  41.2 10.8 %collective-permute-start.4 = (f32[2,16,128]{2,1,0:T(8,128)S(1)}, f32[2,16,128]{2,1,0:T(8,128)S(1)}, u32[]{:S(2)}, u32[]{:S(2)}) collective-permute-start(f32[2,16,128]{2,1,0:T(8,128)S(1)} %get-tuple-element.68), channel_id=1, source_target_pairs={{0,16},{16,32},{32,48},{48,64},{64,80},{80,96},{96,112},{112,128},... | collective-permute-start | bytes 49160 | tf_op jit(solution)/shard_map/ppermute | solution.py:17
  52.0 3.3 %collective-permute-start.5 = (f32[2,16,128]{2,1,0:T(8,128)S(1)}, f32[2,16,128]{2,1,0:T(8,128)S(1)}, u32[]{:S(2)}, u32[]{:S(2)}) collective-permute-start(f32[2,16,128]{2,1,0:T(8,128)S(1)} %get-tuple-element.67), channel_id=1, source_target_pairs={{16,0},{32,16},{48,32},{64,48},{80,64},{96,80},{112,96},{128,112},... | collective-permute-start | bytes 49160 | tf_op jit(solution)/shard_map/ppermute | solution.py:18
  55.3 32.0 %collective-permute-start.14 = (f32[8,2,128]{2,1,0:T(2,128)S(1)}, f32[8,2,128]{2,1,0:T(2,128)S(1)}, u32[]{:S(2)}, u32[]{:S(2)}) collective-permute-start(f32[8,2,128]{2,1,0:T(2,128)S(1)} %get-tuple-element.82), channel_id=1, source_target_pairs={{0,1},{1,2},{2,3},{3,4},{4,5},{5,6},{6,7},{7,8},{8,9},{9,10},{10,1... | collective-permute-start | bytes 24584 | tf_op jit(solution)/shard_map/ppermute | solution.py:17
  66.9 95.5 %copy-start.8 = (f32[12,16,128]{2,1,0:T(8,128)}, f32[12,16,128]{2,1,0:T(8,128)S(1)}, u32[]{:S(2)}) copy-start(f32[12,16,128]{2,1,0:T(8,128)S(1)} %constant_dynamic-update-slice_fusion.7) | copy-start | bytes 294916
  67.0 5.9 %collective-permute-start.10 = (f32[3,8,2,128]{3,2,1,0:T(2,128)S(1)}, f32[3,8,2,128]{3,2,1,0:T(2,128)S(1)}, u32[]{:S(2)}, u32[]{:S(2)}) collective-permute-start(f32[3,8,2,128]{3,2,1,0:T(2,128)S(1)} %get-tuple-element.57), channel_id=1, source_target_pairs={{0,1},{1,2},{2,3},{3,4},{4,5},{5,6},{6,7},{7,8},{8,9},{9,10},{10,1... | collective-permute-start | bytes 73736 | tf_op jit(solution)/shard_map/ppermute | solution.py:17
  70.5 14.1 %collective-permute-start.11 = (f32[3,8,2,128]{3,2,1,0:T(2,128)S(1)}, f32[3,8,2,128]{3,2,1,0:T(2,128)S(1)}, u32[]{:S(2)}, u32[]{:S(2)}) collective-permute-start(f32[3,8,2,128]{3,2,1,0:T(2,128)S(1)} %get-tuple-element.58), channel_id=1, source_target_pairs={{1,0},{2,1},{3,2},{4,3},{5,4},{6,5},{7,6},{8,7},{9,8},{10,9},{11,1... | collective-permute-start | bytes 73736 | tf_op jit(solution)/shard_map/ppermute | solution.py:18
  72.9 17.8 %collective-permute-start.15 = (f32[8,2,128]{2,1,0:T(2,128)S(1)}, f32[8,2,128]{2,1,0:T(2,128)S(1)}, u32[]{:S(2)}, u32[]{:S(2)}) collective-permute-start(f32[8,2,128]{2,1,0:T(2,128)S(1)} %get-tuple-element.83), channel_id=1, source_target_pairs={{1,0},{2,1},{3,2},{4,3},{5,4},{6,5},{7,6},{8,7},{9,8},{10,9},{11,1... | collective-permute-start | bytes 24584 | tf_op jit(solution)/shard_map/ppermute | solution.py:18
  84.6 77.8 %collective-permute-start.6 = (f32[12,2,128]{2,1,0:T(2,128)S(1)}, f32[12,2,128]{2,1,0:T(2,128)S(1)}, u32[]{:S(2)}, u32[]{:S(2)}) collective-permute-start(f32[12,2,128]{2,1,0:T(2,128)S(1)} %get-tuple-element.59), channel_id=1, source_target_pairs={{0,1},{1,2},{2,3},{3,4},{4,5},{5,6},{6,7},{7,8},{8,9},{9,10},{10,1... | collective-permute-start | bytes 36872 | tf_op jit(solution)/shard_map/ppermute | solution.py:17
  87.3 3.4 %copy-start.5 = (f32[128,128,1]{1,0,2:T(8,128)S(1)}, f32[128,128,1]{1,0,2:T(8,128)}, u32[]{:S(2)}) copy-start(f32[128,128,1]{1,0,2:T(8,128)} %constant.118) | copy-start | bytes 196612
  87.4 75.0 %collective-permute-start.7 = (f32[12,2,128]{2,1,0:T(2,128)S(1)}, f32[12,2,128]{2,1,0:T(2,128)S(1)}, u32[]{:S(2)}, u32[]{:S(2)}) collective-permute-start(f32[12,2,128]{2,1,0:T(2,128)S(1)} %get-tuple-element.60), channel_id=1, source_target_pairs={{1,0},{2,1},{3,2},{4,3},{5,4},{6,5},{7,6},{8,7},{9,8},{10,9},{11,1... | collective-permute-start | bytes 36872 | tf_op jit(solution)/shard_map/ppermute | solution.py:18
  92.4 13.3 %collective-permute-start.16 = (f32[3,2,8]{2,1,0:T(2,128)S(1)}, f32[3,2,8]{2,1,0:T(2,128)S(1)}, u32[]{:S(2)}, u32[]{:S(2)}) collective-permute-start(f32[3,2,8]{2,1,0:T(2,128)S(1)} %get-tuple-element.94), channel_id=1, source_target_pairs={{0,16},{16,32},{32,48},{48,64},{64,80},{80,96},{96,112},{112,128},... | collective-permute-start | bytes 584 | tf_op jit(solution)/shard_map/ppermute | solution.py:17
  94.4 11.4 %collective-permute-start.17 = (f32[3,2,8]{2,1,0:T(2,128)S(1)}, f32[3,2,8]{2,1,0:T(2,128)S(1)}, u32[]{:S(2)}, u32[]{:S(2)}) collective-permute-start(f32[3,2,8]{2,1,0:T(2,128)S(1)} %get-tuple-element.95), channel_id=1, source_target_pairs={{16,0},{32,16},{48,32},{64,48},{80,64},{96,80},{112,96},{128,112},... | collective-permute-start | bytes 584 | tf_op jit(solution)/shard_map/ppermute | solution.py:18
  103.8 41.9 %collective-permute-start.24 = (f32[3,2,8,128]{3,2,1,0:T(8,128)S(1)}, f32[3,2,8,128]{3,2,1,0:T(8,128)S(1)}, u32[]{:S(2)}, u32[]{:S(2)}) collective-permute-start(f32[3,2,8,128]{3,2,1,0:T(8,128)S(1)} %get-tuple-element.69), channel_id=1, source_target_pairs={{0,16},{16,32},{32,48},{48,64},{64,80},{80,96},{96,112},{112,128},... | collective-permute-start | bytes 73736 | tf_op jit(solution)/shard_map/ppermute | solution.py:17
  105.9 12.9 %collective-permute-start.18 = (f32[3,8,2]{2,1,0:T(8,128)S(1)}, f32[3,8,2]{2,1,0:T(8,128)S(1)}, u32[]{:S(2)}, u32[]{:S(2)}) collective-permute-start(f32[3,8,2]{2,1,0:T(8,128)S(1)} %get-tuple-element.90), channel_id=1, source_target_pairs={{0,1},{1,2},{2,3},{3,4},{4,5},{5,6},{6,7},{7,8},{8,9},{9,10},{10,1... | collective-permute-start | bytes 584 | tf_op jit(solution)/shard_map/ppermute | solution.py:17
  116.9 14.0 %collective-permute-start.19 = (f32[3,8,2]{2,1,0:T(8,128)S(1)}, f32[3,8,2]{2,1,0:T(8,128)S(1)}, u32[]{:S(2)}, u32[]{:S(2)}) collective-permute-start(f32[3,8,2]{2,1,0:T(8,128)S(1)} %get-tuple-element.91), channel_id=1, source_target_pairs={{1,0},{2,1},{3,2},{4,3},{5,4},{6,5},{7,6},{8,7},{9,8},{10,9},{11,1... | collective-permute-start | bytes 584 | tf_op jit(solution)/shard_map/ppermute | solution.py:18
  118.8 28.8 %collective-permute-start.25 = (f32[3,2,8,128]{3,2,1,0:T(8,128)S(1)}, f32[3,2,8,128]{3,2,1,0:T(8,128)S(1)}, u32[]{:S(2)}, u32[]{:S(2)}) collective-permute-start(f32[3,2,8,128]{3,2,1,0:T(8,128)S(1)} %get-tuple-element.70), channel_id=1, source_target_pairs={{16,0},{32,16},{48,32},{64,48},{80,64},{96,80},{112,96},{128,112},... | collective-permute-start | bytes 73736 | tf_op jit(solution)/shard_map/ppermute | solution.py:18
  130.9 29.2 %collective-permute-start.2 = (f32[3,12,2,128]{3,2,1,0:T(2,128)S(1)}, f32[3,12,2,128]{3,2,1,0:T(2,128)S(1)}, u32[]{:S(2)}, u32[]{:S(2)}) collective-permute-start(f32[3,12,2,128]{3,2,1,0:T(2,128)S(1)} %get-tuple-element.34), channel_id=1, source_target_pairs={{0,1},{1,2},{2,3},{3,4},{4,5},{5,6},{6,7},{7,8},{8,9},{9,10},{10,1... | collective-permute-start | bytes 110600 | tf_op jit(solution)/shard_map/ppermute | solution.py:17
  145.7 16.3 %collective-permute-start.3 = (f32[3,12,2,128]{3,2,1,0:T(2,128)S(1)}, f32[3,12,2,128]{3,2,1,0:T(2,128)S(1)}, u32[]{:S(2)}, u32[]{:S(2)}) collective-permute-start(f32[3,12,2,128]{3,2,1,0:T(2,128)S(1)} %get-tuple-element.35), channel_id=1, source_target_pairs={{1,0},{2,1},{3,2},{4,3},{5,4},{6,5},{7,6},{8,7},{9,8},{10,9},{11,1... | collective-permute-start | bytes 110600 | tf_op jit(solution)/shard_map/ppermute | solution.py:18
  147.7 15.5 %collective-permute-start.26 = (f32[3,8,2,128]{3,2,1,0:T(2,128)S(1)}, f32[3,8,2,128]{3,2,1,0:T(2,128)S(1)}, u32[]{:S(2)}, u32[]{:S(2)}) collective-permute-start(f32[3,8,2,128]{3,2,1,0:T(2,128)S(1)} %get-tuple-element.55), channel_id=1, source_target_pairs={{0,1},{1,2},{2,3},{3,4},{4,5},{5,6},{6,7},{7,8},{8,9},{9,10},{10,1... | collective-permute-start | bytes 73736 | tf_op jit(solution)/shard_map/ppermute | solution.py:17
  160.1 14.1 %collective-permute-start.27 = (f32[3,8,2,128]{3,2,1,0:T(2,128)S(1)}, f32[3,8,2,128]{3,2,1,0:T(2,128)S(1)}, u32[]{:S(2)}, u32[]{:S(2)}) collective-permute-start(f32[3,8,2,128]{3,2,1,0:T(2,128)S(1)} %get-tuple-element.56), channel_id=1, source_target_pairs={{1,0},{2,1},{3,2},{4,3},{5,4},{6,5},{7,6},{8,7},{9,8},{10,9},{11,1... | collective-permute-start | bytes 73736 | tf_op jit(solution)/shard_map/ppermute | solution.py:18
  163.2 23.3 %copy-start.4 = (f32[4,8,16,128]{3,2,1,0:T(8,128)}, f32[4,8,16,128]{3,2,1,0:T(8,128)S(1)}, u32[]{:S(2)}) copy-start(f32[4,8,16,128]{3,2,1,0:T(8,128)S(1)} %convolution_multiply_fusion.1) | copy-start | bytes 786436
  174.9 11.6 %copy-start.14 = (f32[3,4,8,128]{3,2,1,0:T(8,128)}, f32[3,4,8,128]{3,2,1,0:T(8,128)S(1)}, u32[]{:S(2)}) copy-start(f32[3,4,8,128]{3,2,1,0:T(8,128)S(1)} %fusion.153) | copy-start | bytes 147460
  175.1 11.4 %collective-permute-start.28 = (f32[3,2,8]{2,1,0:T(2,128)S(1)}, f32[3,2,8]{2,1,0:T(2,128)S(1)}, u32[]{:S(2)}, u32[]{:S(2)}) collective-permute-start(f32[3,2,8]{2,1,0:T(2,128)S(1)} %get-tuple-element.96), channel_id=1, source_target_pairs={{0,16},{16,32},{32,48},{48,64},{64,80},{80,96},{96,112},{112,128},... | collective-permute-start | bytes 584 | tf_op jit(solution)/shard_map/ppermute | solution.py:17
  177.0 10.7 %collective-permute-start.29 = (f32[3,2,8]{2,1,0:T(2,128)S(1)}, f32[3,2,8]{2,1,0:T(2,128)S(1)}, u32[]{:S(2)}, u32[]{:S(2)}) collective-permute-start(f32[3,2,8]{2,1,0:T(2,128)S(1)} %get-tuple-element.97), channel_id=1, source_target_pairs={{16,0},{32,16},{48,32},{64,48},{80,64},{96,80},{112,96},{128,112},... | collective-permute-start | bytes 584 | tf_op jit(solution)/shard_map/ppermute | solution.py:18
  186.4 7.2 %copy-start.12 = (f32[3,8,16,128]{3,2,1,0:T(8,128)S(1)}, f32[3,8,16,128]{3,2,1,0:T(8,128)}, u32[]{:S(2)}) copy-start(f32[3,8,16,128]{3,2,1,0:T(8,128)} %param.20) | copy-start | bytes 589828
  186.5 7.1 %copy-start.10 = (f32[8,16,128]{2,1,0:T(8,128)S(1)}, f32[8,16,128]{2,1,0:T(8,128)}, u32[]{:S(2)}) copy-start(f32[8,16,128]{2,1,0:T(8,128)} %param.23) | copy-start | bytes 196612
  186.5 7.1 %slice-start = ((f32[4,8,16,128]{3,2,1,0:T(8,128)}), f32[1,8,16,128]{3,2,1,0:T(8,128)S(1)}, s32[]{:S(2)}) async-start(f32[4,8,16,128]{3,2,1,0:T(8,128)} %copy-done.4), calls=%async_computation | async-start | bytes 131072 | tf_op jit(solution)/shard_map/slice | solution.py:78
  187.8 6.9 %collective-permute-start.30 = (f32[3,8,2]{2,1,0:T(8,128)S(1)}, f32[3,8,2]{2,1,0:T(8,128)S(1)}, u32[]{:S(2)}, u32[]{:S(2)}) collective-permute-start(f32[3,8,2]{2,1,0:T(8,128)S(1)} %get-tuple-element.92), channel_id=1, source_target_pairs={{0,1},{1,2},{2,3},{3,4},{4,5},{5,6},{6,7},{7,8},{8,9},{9,10},{10,1... | collective-permute-start | bytes 584 | tf_op jit(solution)/shard_map/ppermute | solution.py:17
  189.7 14.0 %collective-permute-start.31 = (f32[3,8,2]{2,1,0:T(8,128)S(1)}, f32[3,8,2]{2,1,0:T(8,128)S(1)}, u32[]{:S(2)}, u32[]{:S(2)}) collective-permute-start(f32[3,8,2]{2,1,0:T(8,128)S(1)} %get-tuple-element.93), channel_id=1, source_target_pairs={{1,0},{2,1},{3,2},{4,3},{5,4},{6,5},{7,6},{8,7},{9,8},{10,9},{11,1... | collective-permute-start | bytes 584 | tf_op jit(solution)/shard_map/ppermute | solution.py:18
  204.0 5.5 %copy-start.17 = (f32[8,16,16]{2,1,0:T(8,128)S(1)}, f32[8,16,16]{2,1,0:T(8,128)}, u32[]{:S(2)}) copy-start(f32[8,16,16]{2,1,0:T(8,128)} %param.32) | copy-start | bytes 24580
  211.9 12.6 %collective-permute-start.20 = (f32[3,2,16,128]{3,2,1,0:T(8,128)S(1)}, f32[3,2,16,128]{3,2,1,0:T(8,128)S(1)}, u32[]{:S(2)}, u32[]{:S(2)}) collective-permute-start(f32[3,2,16,128]{3,2,1,0:T(8,128)S(1)} %get-tuple-element.36), channel_id=1, source_target_pairs={{0,16},{16,32},{32,48},{48,64},{64,80},{80,96},{96,112},{112,128},... | collective-permute-start | bytes 147464 | tf_op jit(solution)/shard_map/ppermute | solution.py:17
  213.8 9.8 %copy-start.11 = (f32[8,16,3]{2,1,0:T(8,128)S(1)}, f32[8,16,3]{2,1,0:T(8,128)}, u32[]{:S(2)}) copy-start(f32[8,16,3]{2,1,0:T(8,128)} %get-tuple-element.26) | copy-start | bytes 4612
  213.8 11.2 %collective-permute-start.21 = (f32[3,2,16,128]{3,2,1,0:T(8,128)S(1)}, f32[3,2,16,128]{3,2,1,0:T(8,128)S(1)}, u32[]{:S(2)}, u32[]{:S(2)}) collective-permute-start(f32[3,2,16,128]{3,2,1,0:T(8,128)S(1)} %get-tuple-element.37), channel_id=1, source_target_pairs={{16,0},{32,16},{48,32},{64,48},{80,64},{96,80},{112,96},{128,112},... | collective-permute-start | bytes 147464 | tf_op jit(solution)/shard_map/ppermute | solution.py:18
  225.1 5.9 %collective-permute-start.22 = (f32[3,12,2,128]{3,2,1,0:T(2,128)S(1)}, f32[3,12,2,128]{3,2,1,0:T(2,128)S(1)}, u32[]{:S(2)}, u32[]{:S(2)}) collective-permute-start(f32[3,12,2,128]{3,2,1,0:T(2,128)S(1)} %get-tuple-element.32), channel_id=1, source_target_pairs={{0,1},{1,2},{2,3},{3,4},{4,5},{5,6},{6,7},{7,8},{8,9},{9,10},{10,1... | collective-permute-start | bytes 110600 | tf_op jit(solution)/shard_map/ppermute | solution.py:17
  227.0 14.3 %collective-permute-start.23 = (f32[3,12,2,128]{3,2,1,0:T(2,128)S(1)}, f32[3,12,2,128]{3,2,1,0:T(2,128)S(1)}, u32[]{:S(2)}, u32[]{:S(2)}) collective-permute-start(f32[3,12,2,128]{3,2,1,0:T(2,128)S(1)} %get-tuple-element.33), channel_id=1, source_target_pairs={{1,0},{2,1},{3,2},{4,3},{5,4},{6,5},{7,6},{8,7},{9,8},{10,9},{11,1... | collective-permute-start | bytes 110600 | tf_op jit(solution)/shard_map/ppermute | solution.py:18
  241.5 0.9 copy-start.9
  (7 other events, 5.3 us)
where the time goes:
time: 246 us; the launch traced here: 244 us
  starting transfers between devices  160 us (65%)
  waiting for transfers between devices  55.6 us (23%)
  local copies, waits for them, and re-layouts  19.6 us (8%)
  other arithmetic  4.33 us (2%)
  matrix products  2.98 us (1%)
    ppermute x16, starting transfers between devices, padded(): after = lax.ppermute(initial, axis, down)  90.7 us
    ppermute x16, starting transfers between devices, padded(): before = lax.ppermute(last, axis, up)  69.3 us
    ppermute x16, waiting for transfers between devices, padded(): after = lax.ppermute(initial, axis, down)  46.7 us
    gather x2, local copies, waits for them, and re-layouts, interpolate(): return jnp.sum(flat_plane[:, targets] * mixing, axis=-1)  10.9 us
    ppermute x16, waiting for transfers between devices, padded(): before = lax.ppermute(last, axis, up)  8.85 us
  transfers between devices with their start and end apart: 32, of which 9 were waited for; matrix products, arithmetic and copies ran while one was open for 5% of the time, Pallas kernels for 0%

commit v1 on v0

v1 whole, which is shorter than its diff:
```python
import jax
import jax.numpy as jnp
import numpy as np
from jax import lax
from jax.experimental import pallas as pl
from jax.experimental.pallas import tpu as pltpu
from jax.sharding import PartitionSpec as P


DT2 = 0.0625
NL = 128
Y_ROWS, A_ROWS, C_ROWS, R_ROWS = 400, 736, 528, 160
YB, YC, YD = 128, 224, 320
AB, AC, AD = 256, 448, 576
CB_, CC, CS = 64, 88, 264
F32 = jnp.float32


def vertical_matrix():
    m = np.zeros((NL, NL))
    for k in range(2, NL - 2):
        m[k, k - 2], m[k, k - 1], m[k, k + 1], m[k, k + 2] = 1, -8, 8, -1
    m[0, 0:3] = -18, 24, -6
    m[1, 0], m[1, 2] = -6, 6
    m[NL - 2, NL - 3], m[NL - 2, NL - 1] = -6, 6
    m[NL - 1, NL - 3 :] = 6, -24, 18
    return np.concatenate([m.T, m.T], 0)


def odd(axis):
    return lax.axis_index(axis) % 2


def rows(v):
    return v.reshape(-1, NL)


def pack_own(fn, fp, fr, fm, fl, fj, cn, cp, cr, cm, cl, cj, ix, wt, yn, yf, an, af, fo, co):
    inv = DT2 / fr[...]
    fo[0] = fm[...] * inv
    fo[1] = (fl[...] + fm[...]) * inv
    inv = DT2 / cr[...]
    co[0] = cm[...] * inv
    co[1] = (cl[...] + cm[...]) * inv
    lane = lax.broadcasted_iota(jnp.int32, (128, NL), 1)
    index = ix[...].reshape(128, 16)
    weight = wt[...].reshape(128, 16)
    slot = index + 2 + 4 * ((index * 171) >> 11)
    acc = jnp.zeros((128, NL), F32)
    for k in range(16):
        acc = acc + jnp.where(lane == slot[:, k : k + 1], weight[:, k : k + 1], 0.0)
    fo[2] = acc.reshape(8, 16, NL)

    def fine_u(i, x):
        return fn[i, x] if i < 3 else fj[x] * (1.0 / 12.0)

    def coarse_u(i, x):
        return cn[i, x] if i < 3 else cj[x] * (1.0 / 12.0)

    def y_edge(out, low):
        for i in range(4):
            for x in range(8):
                v = fine_u(i, x)
                out[i * 32 + x * 4 : i * 32 + x * 4 + 4] = v[0:4] if low else v[12:16]
        for i in range(6):
            for x in range(8):
                v = fp[i, x] if i < 3 else fo[i - 3, x]
                v = v[0:2] if low else v[14:16]
                if i == 5:
                    v = pltpu.roll(v, 8 if low else 120, 1)
                out[YB + i * 16 + x * 2 : YB + i * 16 + x * 2 + 2] = v
        for i in range(4):
            for x in range(4):
                v = coarse_u(i, x)
                out[YC + i * 24 + x * 6 : YC + i * 24 + x * 6 + 6] = v[0:6] if low else v[2:8]
        for i in range(5):
            for x in range(4):
                v = cp[i, x] if i < 3 else co[i - 3, x]
                out[YD + i * 16 + x * 4 : YD + i * 16 + x * 4 + 4] = v[0:4] if low else v[4:8]

    def x_edge(out, low):
        x0 = 0 if low else 4
        for i in range(4):
            v = fn[i, x0 : x0 + 4] if i < 3 else fj[x0 : x0 + 4] * (1.0 / 12.0)
            out[i * 64 : i * 64 + 64] = rows(v)
        x0 = 0 if low else 6
        for i in range(6):
            v = fp[i, x0 : x0 + 2] if i < 3 else fo[i - 3, x0 : x0 + 2]
            out[AB + i * 32 : AB + i * 32 + 32] = rows(v)
        for i in range(4):
            v = cn[i] if i < 3 else cj[...] * (1.0 / 12.0)
            out[AC + i * 32 : AC + i * 32 + 32] = rows(v)
        for i in range(5):
            v = cp[i] if i < 3 else co[i - 3]
            out[AD + i * 32 : AD + i * 32 + 32] = rows(v)

    ox, oy = odd("gx"), odd("gy")

    @pl.when(oy == 0)
    def _():
        y_edge(yn, False)
        y_edge(yf, True)

    @pl.when(oy == 1)
    def _():
        y_edge(yn, True)
        y_edge(yf, False)

    @pl.when(ox == 0)
    def _():
        x_edge(an, False)
        x_edge(af, True)

    @pl.when(ox == 1)
    def _():
        x_edge(an, True)
        x_edge(af, False)


def pack_corner(src, out, base, low):
    for i in range(4):
        o = i * 32 + (0 if low else 16)
        out[base + i * 16 : base + i * 16 + 16] = src[o : o + 16]
    for i in range(6):
        o = YB + i * 16 + (0 if low else 12)
        out[base + CB_ + i * 4 : base + CB_ + i * 4 + 4] = src[o : o + 4]
    out[base + CC : base + CS] = src[YC:Y_ROWS]


def pack_near(rn, rf, out):
    ox = odd("gx")

    @pl.when(ox == 0)
    def _():
        pack_corner(rn, out, 0, False)
        pack_corner(rf, out, CS, False)

    @pl.when(ox == 1)
    def _():
        pack_corner(rn, out, 0, True)
        pack_corner(rf, out, CS, True)


def pack_relay(a, c, out, base, x0):
    for i in range(4):
        out[base + i * 16 : base + i * 16 + 16] = a[AC + i * 32 + x0 * 8 : AC + i * 32 + x0 * 8 + 16]
    for s in range(2):
        for i in range(4):
            o = s * CS + CC + i * 24 + x0 * 6
            t = base + 64 + s * 48 + i * 12
            out[t : t + 12] = c[o : o + 12]


def pack_far(rn, rf, a, c, out):
    ox = odd("gx")

    @pl.when(ox == 0)
    def _():
        pack_corner(rn, out, 0, True)
        pack_corner(rf, out, CS, True)
        pack_relay(a, c.at[1], out, C_ROWS, 0)

    @pl.when(ox == 1)
    def _():
        pack_corner(rn, out, 0, False)
        pack_corner(rf, out, CS, False)
        pack_relay(a, c.at[0], out, C_ROWS, 2)


def pack_second(a, c, out):
    ox = odd("gx")

    @pl.when(ox == 0)
    def _():
        pack_relay(a, c, out, 0, 2)

    @pl.when(ox == 1)
    def _():
        pack_relay(a, c, out, 0, 0)


def vertical(v, table):
    hi = v.astype(jnp.bfloat16)
    lo = (v - hi.astype(F32)).astype(jnp.bfloat16)
    return jnp.dot(jnp.concatenate([hi, lo], 1), table, preferred_element_type=F32)


def first(m2, m1, p1, p2, scale):
    return (m2 - p2) * (scale / 12.0) + (p1 - m1) * (scale * 8.0 / 12.0)


def second(m2, m1, c, p1, p2, scale):
    return (m1 + p1) * (scale * 16.0 / 12.0) - (m2 + p2) * (scale / 12.0) - c * (scale * 2.5)


def shifted(v):
    return [pltpu.roll(v, s % 24, 0) for s in (2, 1, -1, -2)]


def advance(n, u, j, prev, a, b, lift, work, table, spacing, store):
    s1, s2 = 1.0 / spacing, 1.0 / (spacing * spacing)
    half = (n + 4) // 2
    for x0 in (0, half):
        g = vertical(rows(u(2, x0, half)), table)
        lift[x0 : x0 + half] = (rows(j(x0, half)) * g).reshape(half, 24, NL)
    for c in range(2):
        g = vertical(rows(u(c, 2, n)), table)
        work[c, 0:n] = (rows(j(2, n)) * g).reshape(n, 24, NL)
    for x in range(n):
        f0 = [u(0, x + k, None) for k in (0, 1, 3, 4)]
        m2, m1, p1, p2 = shifted(u(1, x + 2, None))
        work[3, x] = first(*f0, s1) + first(m2, m1, p1, p2, s1) + lift[x + 2]
    work[2, 0:n] = lift[2 : 2 + n]
    for c in range(4):
        g = vertical(rows(work[c, 0:n]), table)
        work[c, 0:n] = (rows(j(2, n)) * g).reshape(n, 24, NL)
    for x in range(n):
        col = [[u(c, x + k, None) for k in range(5)] for c in range(3)]
        lf = [lift[x + k] for k in range(5)]
        sh = [shifted(col[c][2]) for c in range(3)]
        xx = [second(*col[c], s2) for c in range(3)]
        yy = [second(sh[c][0], sh[c][1], col[c][2], sh[c][2], sh[c][3], s2) for c in range(3)]
        dx0 = first(col[0][0], col[0][1], col[0][3], col[0][4], s1)
        dx1 = first(col[1][0], col[1][1], col[1][3], col[1][4], s1)
        g0 = xx[0] + first(*shifted(dx1), s1) + first(lf[0], lf[1], lf[3], lf[4], s1)
        g1 = yy[1] + first(*shifted(dx0), s1) + first(*shifted(lf[2]), s1)
        g2 = work[3, x]
        av, bv = a(x), b(x)
        for c, g in enumerate((g0, g1, g2)):
            lap = xx[c] + yy[c] + work[c, x]
            store(c, x, 2.0 * col[c][2] - prev(c, x) + av * lap + bv * g)


def main(
    fn, fp, fj, fo, cn, cp, cj, co, yn, yf, an, af, gn, bf, g2, table_ref,
    fine_out, coarse_out, fe, fb, ce, cb, f1, c1, lift, work, tops, face,
):
    ox, oy = odd("gx"), odd("gy")
    ce[:, :, 0:8] = jnp.zeros((4, 16, 8, NL), F32)
    ce[:, :, 16:24] = jnp.zeros((4, 16, 8, NL), F32)
    cb[:, :, 0:8] = jnp.zeros((5, 12, 8, NL), F32)
    cb[:, :, 16:24] = jnp.zeros((5, 12, 8, NL), F32)
    fb[:, :, 0:8] = jnp.zeros((6, 12, 8, NL), F32)
    fb[:, :, 16:24] = jnp.zeros((6, 12, 8, NL), F32)
    for x in range(8):
        for i in range(3):
            fe[i, 4 + x, 4:20] = fn[i, x]
            fb[i, 2 + x, 4:20] = fp[i, x]
            fb[3 + i, 2 + x, 4:20] = fo[i, x]
        fe[3, 4 + x, 4:20] = fj[x] * (1.0 / 12.0)
    for x in range(4):
        for i in range(3):
            ce[i, 6 + x, 8:16] = cn[i, x]
            cb[i, 4 + x, 8:16] = cp[i, x]
        for i in range(2):
            cb[3 + i, 4 + x, 8:16] = co[i, x]
        ce[3, 6 + x, 8:16] = cj[x] * (1.0 / 12.0)
    near, far = ox == 0, ox == 1
    other = 1 - ox
    sides = (
        (an, gn.at[other], g2.at[other], near, 0),
        (af, bf, bf, far, C_ROWS),
    )
    for a, c, r, high, base in sides:
        f4 = jnp.where(high, 12, 0)
        f2 = jnp.where(high, 10, 0)
        c4 = jnp.where(high, 10, 2)
        c2 = jnp.where(high, 14, 0)
        b4 = jnp.where(high, 8, 0)
        for i in range(4):
            for x in range(4):
                fe[i, f4 + x, 4:20] = a[i * 64 + x * 16 : i * 64 + x * 16 + 16]
                ce[i, c4 + x, 8:16] = a[AC + i * 32 + x * 8 : AC + i * 32 + x * 8 + 8]
            for x in range(2):
                ce[i, c2 + x, 8:16] = r[base + i * 16 + x * 8 : base + i * 16 + x * 8 + 8]
        for i in range(6):
            for x in range(2):
                fb[i, f2 + x, 4:20] = a[AB + i * 32 + x * 16 : AB + i * 32 + x * 16 + 16]
        for i in range(5):
            for x in range(4):
                cb[i, b4 + x, 8:16] = a[AD + i * 32 + x * 8 : AD + i * 32 + x * 8 + 8]

    def y_side(src, s, high):
        t4, t2, t6, t3 = (20, 20, 16, 16) if high else (0, 2, 2, 4)
        for i in range(4):
            for x in range(8):
                fe[i, 4 + x, t4 : t4 + 4] = src[i * 32 + x * 4 : i * 32 + x * 4 + 4]
            for x in range(4):
                o = YC + i * 24 + x * 6
                ce[i, 6 + x, t6 : t6 + 6] = src[o : o + 6]
        for i in range(6):
            for x in range(8):
                o = YB + i * 16 + x * 2
                fb[i, 2 + x, t2 : t2 + 2] = src[o : o + 2]
        for i in range(5):
            for x in range(4):
                o = YD + i * 16 + x * 4
                cb[i, 4 + x, t3 : t3 + 4] = src[o : o + 4]
        for a, c, r, hx, base in sides:
            f4 = jnp.where(hx, 12, 0)
            f2 = jnp.where(hx, 10, 0)
            c4 = jnp.where(hx, 10, 2)
            c2 = jnp.where(hx, 14, 0)
            b4 = jnp.where(hx, 8, 0)
            q = s * CS
            for i in range(4):
                for x in range(4):
                    o = q + i * 16 + x * 4
                    fe[i, f4 + x, t4 : t4 + 4] = c[o : o + 4]
                    o = q + CC + i * 24 + x * 6
                    ce[i, c4 + x, t6 : t6 + 6] = c[o : o + 6]
                for x in range(2):
                    o = base + 64 + s * 48 + i * 12 + x * 6
                    ce[i, c2 + x, t6 : t6 + 6] = r[o : o + 6]
            for i in range(6):
                for x in range(2):
                    o = q + CB_ + i * 4 + x * 2
                    fb[i, f2 + x, t2 : t2 + 2] = c[o : o + 2]
            for i in range(5):
                for x in range(4):
                    o = q + CC + 96 + i * 16 + x * 4
                    cb[i, b4 + x, t3 : t3 + 4] = c[o : o + 4]

    @pl.when(oy == 0)
    def _():
        y_side(yn, 0, True)
        y_side(yf, 1, False)

    @pl.when(oy == 1)
    def _():
        y_side(yn, 0, False)
        y_side(yf, 1, True)

    table = table_ref[...]
    lane = lax.broadcasted_iota(jnp.int32, (24, NL), 1)

    def view(ref, i, off):
        def get(x, count):
            return ref[i, x + off] if count is None else ref[i, x + off : x + off + count]

        return get

    def views(ref, off):
        def get(i, x, count=None):
            return view(ref, i, off)(x, count)

        return get

    def gather_top(src, n, t0):
        for x in range(n):
            v = jnp.where(lane == 0, pltpu.roll(src[0, x], 1, 1), 0.0)
            v = jnp.where(lane == 1, pltpu.roll(src[1, x], 2, 1), v)
            v = jnp.where(lane == 2, pltpu.roll(src[2, x], 3, 1), v)
            tops[t0 + x] = v[4:20]

    def mixed(x0, n, t0):
        w = rows(fb[5, x0 : x0 + n])
        plane = tops[t0 : t0 + 8].reshape(128, NL)
        return jnp.dot(w, plane, precision=lax.Precision.HIGHEST, preferred_element_type=F32).reshape(n, 24, NL)

    def with_face(c, x, v):
        return jnp.where(lane == 0, pltpu.roll(face[x], (NL - c) % NL, 1), v)

    tops[0:2] = jnp.zeros((2, 16, NL), F32)
    tops[14:16] = jnp.zeros((2, 16, NL), F32)

    def store_c1(c, x, v):
        c1[c, x] = v

    advance(12, views(ce, 0), view(ce, 3, 0), views(cb, 0), view_row(cb, 3, 0), view_row(cb, 4, 0),
            lift, work, table, 2.0, store_c1)
    gather_top(c1, 12, 2)
    face[0:2] = mixed(0, 2, 0)
    face[2:10] = mixed(2, 8, 4)
    face[10:12] = mixed(10, 2, 8)

    def store_f1(c, x, v):
        f1[c, x] = with_face(c, x, v)

    advance(12, views(fe, 0), view(fe, 3, 0), views(fb, 0), view_row(fb, 3, 0), view_row(fb, 4, 0),
            lift, work, table, 1.0, store_f1)

    def store_c2(c, x, v):
        cb[c, x] = v
        if 2 <= x < 6:
            coarse_out[c, x - 2] = v[8:16]

    advance(8, views(c1, 0), view(ce, 3, 2), views(ce, 4), view_row(cb, 3, 2), view_row(cb, 4, 2),
            lift, work, table, 2.0, store_c2)
    gather_top(cb, 8, 4)
    face[0:8] = mixed(2, 8, 4)

    def store_f2(c, x, v):
        fine_out[c, x] = with_face(c, x, v)[4:20]

    advance(8, views(f1, 0), view(fe, 3, 2), views(fe, 4), view_row(fb, 3, 2), view_row(fb, 4, 2),
            lift, work, table, 1.0, store_f2)


def view_row(ref, i, off):
    def get(x):
        return ref[i, x + off]

    return get


def pairs(size, start):
    out = []
    for i in range(start, size - 1, 2):
        out += [(i, i + 1), (i + 1, i)]
    return out


INTERPRET = False


def call(body, shapes, *operands, scratch=()):
    return pl.pallas_call(
        body,
        out_shape=[jax.ShapeDtypeStruct(s, F32) for s in shapes],
        scratch_shapes=[pltpu.VMEM(s, F32) for s in scratch],
        compiler_params=pltpu.CompilerParams(vmem_limit_bytes=56 << 20),
        interpret=INTERPRET,
    )(*operands)


def on_device(
    fine_now, fine_prev, coarse_now, coarse_prev, fine_rho, fine_mu, fine_lam, fine_metric,
    coarse_rho, coarse_mu, coarse_lam, coarse_metric, couple_index, couple_weight,
):
    gx, gy = lax.axis_size("gx"), lax.axis_size("gy")
    near_x, far_x, near_y, far_y = pairs(gx, 0), pairs(gx, 1), pairs(gy, 0), pairs(gy, 1)
    groups = [[i, i + 1] for i in range(0, gx, 2)]
    table = jnp.asarray(vertical_matrix(), jnp.bfloat16)

    yn, yf, an, af, fo, co = call(
        pack_own,
        [(Y_ROWS, NL)] * 2 + [(A_ROWS, NL)] * 2 + [(3, 8, 16, NL), (2, 4, 8, NL)],
        fine_now, fine_prev, fine_rho, fine_mu, fine_lam, fine_metric,
        coarse_now, coarse_prev, coarse_rho, coarse_mu, coarse_lam, coarse_metric,
        couple_index, couple_weight,
    )
    yn = lax.ppermute(yn, "gy", near_y)
    yf = lax.ppermute(yf, "gy", far_y)
    af = lax.ppermute(af, "gx", far_x)
    an = lax.ppermute(an, "gx", near_x)
    (cn,) = call(pack_near, [(C_ROWS, NL)], yn, yf)
    gn = lax.all_gather(cn, "gx", axis_index_groups=groups)
    (bf,) = call(pack_far, [(C_ROWS + R_ROWS, NL)], yn, yf, an, gn)
    bf = lax.ppermute(bf, "gx", far_x)
    (r2,) = call(pack_second, [(R_ROWS, NL)], af, bf)
    g2 = lax.all_gather(r2, "gx", axis_index_groups=groups)
    return tuple(
        call(
            main,
            [(3, 8, 16, NL), (3, 4, 8, NL)],
            fine_now, fine_prev, fine_metric, fo, coarse_now, coarse_prev, coarse_metric, co,
            yn, yf, an, af, gn, bf, g2, table,
            scratch=[
                (4, 16, 24, NL), (6, 12, 24, NL), (4, 16, 24, NL), (5, 12, 24, NL),
                (3, 12, 24, NL), (3, 12, 24, NL), (16, 24, NL), (4, 12, 24, NL), (16, 16, NL), (12, 24, NL),
            ],
        )
    )


def solution(mesh):
    wide, flat = P(None, "gx", "gy", None), P("gx", "gy", None)
    return jax.shard_map(
        on_device,
        mesh=mesh,
        in_specs=(wide,) * 4 + (flat,) * 10,
        out_specs=(wide, wide),
        check_vma=False,
    )
```

time: 246 us -> 73 us (0.30)
  the two profiles are of different devices: /device:TPU:58 before, /device:TPU:57 now
where the time goes in v1:
time: 73 us; the launch traced here: 72.3 us
  starting transfers between devices  38.2 us (52%)
  Pallas kernels  15.7 us (22%)
  blocking collectives  8.39 us (11%)
  waiting for transfers between devices  7.05 us (10%)
  local copies, waits for them, and re-layouts  2.2 us (3%)
    pallas_call x5, Pallas kernels, call(): pl.pallas_call(body, out_shape=[jax.ShapeDtypeStruct(s, F32) for s in sha...  15.7 us
    ppermute x1, starting transfers between devices, on_device(): bf = lax.ppermute(bf, 'gx', far_x)  14.8 us
    ppermute x1, starting transfers between devices, on_device(): yf = lax.ppermute(yf, 'gy', far_y)  14.3 us
    ppermute x1, waiting for transfers between devices, on_device(): bf = lax.ppermute(bf, 'gx', far_x)  5.2 us
    all_gather x1, blocking collectives, on_device(): gn = lax.all_gather(cn, 'gx', axis_index_groups=groups)  4.97 us
    ppermute x1, starting transfers between devices, on_device(): af = lax.ppermute(af, 'gx', far_x)  3.56 us
    all_gather x1, blocking collectives, on_device(): g2 = lax.all_gather(r2, 'gx', axis_index_groups=groups)  3.43 us
    ppermute x1, starting transfers between devices, on_device(): yn = lax.ppermute(yn, 'gy', near_y)  2.98 us
  transfers between devices with their start and end apart: 5, of which 2 were waited for; matrix products, arithmetic and copies ran while one was open for 0% of the time, Pallas kernels for 5%

profile of v1, /device:TPU:57, one launch (start us, length us, event | category | flops | bytes accessed | tf_op | source)
XLA Modules:
  0.0 72.3 jit_solution(9334584870246744941)
XLA Ops:
  0.6 3.1 %shard_map.158 = (f32[400,128]{1,0:T(8,128)}, f32[400,128]{1,0:T(8,128)}, f32[736,128]{1,0:T(8,128)}, f32[736,128]{1,0:T(8,128)}, f32[3,8,16,128]{3,2,1,0:T(8,128)}, /*index=5*/f32[2,4,8,128]{3,2,1,0:T(8,128)}) custom-call(f32[3,8,16,128]{3,2,1,0:T(8,128)} %fn.3, f32[3,8,16,128]{3,2,1,0:T(8,128)} %fp.3, f32[8,16,128]{2,1,0:T(8,128)} %fr.1, ...), custom_call_target="tpu_custom_call" | custom-call | tf_op jit(solution)/shard_map/pallas_call | solution.py:418
  3.8 2.6 %collective-permute-start.2 = (f32[736,128]{1,0:T(8,128)}, f32[736,128]{1,0:T(8,128)S(1)}, u32[]{:S(2)}, u32[]{:S(2)}) collective-permute-start(f32[736,128]{1,0:T(8,128)} %get-tuple-element.12), channel_id=1, source_target_pairs={{0,16},{16,0},{32,48},{48,32},{64,80},{80,64},{96,112},{112,96},{1... | collective-permute-start | bytes 1130504 | tf_op jit(solution)/shard_map/ppermute | solution.py:446
  6.3 3.0 %collective-permute-start = (f32[400,128]{1,0:T(8,128)}, f32[400,128]{1,0:T(8,128)S(1)}, u32[]{:S(2)}, u32[]{:S(2)}) collective-permute-start(f32[400,128]{1,0:T(8,128)} %get-tuple-element.10), channel_id=1, source_target_pairs={{0,1},{1,0},{2,3},{3,2},{4,5},{5,4},{6,7},{7,6},{8,9},{9,8},{10,11... | collective-permute-start | bytes 614408 | tf_op jit(solution)/shard_map/ppermute | solution.py:443
  9.3 14.3 %collective-permute-start.1 = (f32[400,128]{1,0:T(8,128)}, f32[400,128]{1,0:T(8,128)S(1)}, u32[]{:S(2)}, u32[]{:S(2)}) collective-permute-start(f32[400,128]{1,0:T(8,128)} %get-tuple-element.11), channel_id=1, source_target_pairs={{1,2},{2,1},{3,4},{4,3},{5,6},{6,5},{7,8},{8,7},{9,10},{10,9},{11,... | collective-permute-start | bytes 614408 | tf_op jit(solution)/shard_map/ppermute | solution.py:444
  23.6 3.6 %collective-permute-start.3 = (f32[736,128]{1,0:T(8,128)}, f32[736,128]{1,0:T(8,128)S(1)}, u32[]{:S(2)}, u32[]{:S(2)}) collective-permute-start(f32[736,128]{1,0:T(8,128)} %get-tuple-element.13), channel_id=1, source_target_pairs={{16,32},{32,16},{48,64},{64,48},{80,96},{96,80},{112,128},{128,112... | collective-permute-start | bytes 1130504 | tf_op jit(solution)/shard_map/ppermute | solution.py:445
  27.2 0.0 collective-permute-done.rn.yn
  27.2 0.0 copy-start
  27.2 1.8 %collective-permute-done.1.rf.yf = f32[400,128]{1,0:T(8,128)S(1)} collective-permute-done((f32[400,128]{1,0:T(8,128)}, f32[400,128]{1,0:T(8,128)S(1)}, u32[]{:S(2)}, u32[]{:S(2)}) %collective-permute-start.1) | collective-permute-done | bytes 204832 | tf_op jit(solution)/shard_map/ppermute | solution.py:444
  29.1 0.0 copy-done
  29.1 0.0 copy-start.1
  29.1 0.7 copy-done.1
  29.8 1.7 %shard_map.159 = f32[528,128]{1,0:T(8,128)} custom-call(f32[400,128]{1,0:T(8,128)} %copy-done, f32[400,128]{1,0:T(8,128)} %copy-done.1), custom_call_target="tpu_custom_call" | custom-call | tf_op jit(solution)/shard_map/pallas_call | solution.py:418
  31.5 5.0 %all-gather = f32[1056,128]{1,0:T(8,128)} all-gather(f32[528,128]{1,0:T(8,128)} %shard_map.159), channel_id=2, replica_groups={{0,16},{32,48},{64,80},{96,112},{128,144},{160,176},{192,208},{224,240}..., dimensions={0}, use_global_device_ids=true | all-gather | bytes 811008 | tf_op jit(solution)/shard_map/all_gather | solution.py:448
  36.5 0.0 collective-permute-done.2.a.an
  36.5 0.0 copy-start.2
  36.5 0.7 %copy-done.2 = f32[736,128]{1,0:T(8,128)} copy-done((f32[736,128]{1,0:T(8,128)}, f32[736,128]{1,0:T(8,128)S(1)}, u32[]{:S(2)}) %copy-start.2) | copy-done | bytes 376856
  37.2 2.1 %shard_map.160 = f32[688,128]{1,0:T(8,128)} custom-call(f32[400,128]{1,0:T(8,128)} %copy-done, f32[400,128]{1,0:T(8,128)} %copy-done.1, f32[736,128]{1,0:T(8,128)} %copy-done.2, f32[2,528,128]{2,1,0:T(8,128)} %bitcast.2), custom_call_target="tpu_custom_call" | custom-call | tf_op jit(solution)/shard_map/pallas_call | solution.py:418
  39.4 14.8 %collective-permute-start.4 = (f32[688,128]{1,0:T(8,128)}, f32[688,128]{1,0:T(8,128)S(1)}, u32[]{:S(2)}, u32[]{:S(2)}) collective-permute-start(f32[688,128]{1,0:T(8,128)} %shard_map.160), channel_id=1, source_target_pairs={{16,32},{32,16},{48,64},{64,48},{80,96},{96,80},{112,128},{128,112... | collective-permute-start | bytes 1056776 | tf_op jit(solution)/shard_map/ppermute | solution.py:450
  54.2 0.0 collective-permute-done.3.a.af
  54.2 0.0 copy-start.3
  54.2 5.2 %collective-permute-done.4.c.bf = f32[688,128]{1,0:T(8,128)S(1)} collective-permute-done((f32[688,128]{1,0:T(8,128)}, f32[688,128]{1,0:T(8,128)S(1)}, u32[]{:S(2)}, u32[]{:S(2)}) %collective-permute-start.4) | collective-permute-done | bytes 352288 | tf_op jit(solution)/shard_map/ppermute | solution.py:450
  59.4 0.0 copy-done.3
  59.4 0.0 copy-start.4
  59.4 0.7 %copy-done.4 = f32[688,128]{1,0:T(8,128)} copy-done((f32[688,128]{1,0:T(8,128)}, f32[688,128]{1,0:T(8,128)S(1)}, u32[]{:S(2)}) %copy-start.4) | copy-done | bytes 352280
  60.1 1.7 %shard_map.161 = f32[160,128]{1,0:T(8,128)} custom-call(f32[736,128]{1,0:T(8,128)} %copy-done.3, f32[688,128]{1,0:T(8,128)} %copy-done.4), custom_call_target="tpu_custom_call" | custom-call | tf_op jit(solution)/shard_map/pallas_call | solution.py:418
  61.9 3.4 %all-gather.1 = f32[320,128]{1,0:T(8,128)} all-gather(f32[160,128]{1,0:T(8,128)} %shard_map.161), channel_id=3, replica_groups={{0,16},{32,48},{64,80},{96,112},{128,144},{160,176},{192,208},{224,240}..., dimensions={0}, use_global_device_ids=true | all-gather | bytes 245760 | tf_op jit(solution)/shard_map/all_gather | solution.py:452
  65.3 7.0 %shard_map.162 = (f32[3,8,16,128]{3,2,1,0:T(8,128)}, f32[3,4,8,128]{3,2,1,0:T(8,128)}) custom-call(f32[3,8,16,128]{3,2,1,0:T(8,128)} %fn.3, f32[3,8,16,128]{3,2,1,0:T(8,128)} %fp.3, f32[8,16,128]{2,1,0:T(8,128)} %fj.3, f32[3,8,16,128]{3,2,1,0:T(8,128)} %get-tuple-element.8.fo, f32[3,4,8,128]{3,2,1,0:T(8,128)} %cn.3, f32[3,4,8,128]{3,2,1,0:T(8,128)} %cp.3, ...), custom_call_target="tpu_custom_call" | custom-call | tf_op jit(solution)/shard_map/pallas_call | solution.py:418
Async XLA Ops:
  3.8 32.7 %collective-permute-start.2 = (f32[736,128]{1,0:T(8,128)}, f32[736,128]{1,0:T(8,128)S(1)}, u32[]{:S(2)}, u32[]{:S(2)}) collective-permute-start(f32[736,128]{1,0:T(8,128)} %get-tuple-element.12), channel_id=1, source_target_pairs={{0,16},{16,0},{32,48},{48,32},{64,80},{80,64},{96,112},{112,96},{1... | collective-permute-start | bytes 1130504 | tf_op jit(solution)/shard_map/ppermute | solution.py:446
  6.3 20.9 %collective-permute-start = (f32[400,128]{1,0:T(8,128)}, f32[400,128]{1,0:T(8,128)S(1)}, u32[]{:S(2)}, u32[]{:S(2)}) collective-permute-start(f32[400,128]{1,0:T(8,128)} %get-tuple-element.10), channel_id=1, source_target_pairs={{0,1},{1,0},{2,3},{3,2},{4,5},{5,4},{6,7},{7,6},{8,9},{9,8},{10,11... | collective-permute-start | bytes 614408 | tf_op jit(solution)/shard_map/ppermute | solution.py:443
  9.3 19.7 %collective-permute-start.1 = (f32[400,128]{1,0:T(8,128)}, f32[400,128]{1,0:T(8,128)S(1)}, u32[]{:S(2)}, u32[]{:S(2)}) collective-permute-start(f32[400,128]{1,0:T(8,128)} %get-tuple-element.11), channel_id=1, source_target_pairs={{1,2},{2,1},{3,4},{4,3},{5,6},{6,5},{7,8},{8,7},{9,10},{10,9},{11,... | collective-permute-start | bytes 614408 | tf_op jit(solution)/shard_map/ppermute | solution.py:444
  23.6 30.5 %collective-permute-start.3 = (f32[736,128]{1,0:T(8,128)}, f32[736,128]{1,0:T(8,128)S(1)}, u32[]{:S(2)}, u32[]{:S(2)}) collective-permute-start(f32[736,128]{1,0:T(8,128)} %get-tuple-element.13), channel_id=1, source_target_pairs={{16,32},{32,16},{48,64},{64,48},{80,96},{96,80},{112,128},{128,112... | collective-permute-start | bytes 1130504 | tf_op jit(solution)/shard_map/ppermute | solution.py:445
  27.2 1.9 %copy-start = (f32[400,128]{1,0:T(8,128)}, f32[400,128]{1,0:T(8,128)S(1)}, u32[]{:S(2)}) copy-start(f32[400,128]{1,0:T(8,128)S(1)} %collective-permute-done.rn.yn) | copy-start | bytes 614404
  29.1 0.7 copy-start.1
  36.5 0.7 %copy-start.2 = (f32[736,128]{1,0:T(8,128)}, f32[736,128]{1,0:T(8,128)S(1)}, u32[]{:S(2)}) copy-start(f32[736,128]{1,0:T(8,128)S(1)} %collective-permute-done.2.a.an) | copy-start | bytes 1130500
  39.4 20.0 %collective-permute-start.4 = (f32[688,128]{1,0:T(8,128)}, f32[688,128]{1,0:T(8,128)S(1)}, u32[]{:S(2)}, u32[]{:S(2)}) collective-permute-start(f32[688,128]{1,0:T(8,128)} %shard_map.160), channel_id=1, source_target_pairs={{16,32},{32,16},{48,64},{64,48},{80,96},{96,80},{112,128},{128,112... | collective-permute-start | bytes 1056776 | tf_op jit(solution)/shard_map/ppermute | solution.py:450
  54.2 5.2 %copy-start.3 = (f32[736,128]{1,0:T(8,128)}, f32[736,128]{1,0:T(8,128)S(1)}, u32[]{:S(2)}) copy-start(f32[736,128]{1,0:T(8,128)S(1)} %collective-permute-done.3.a.af) | copy-start | bytes 1130500
  59.4 0.7 %copy-start.4 = (f32[688,128]{1,0:T(8,128)}, f32[688,128]{1,0:T(8,128)S(1)}, u32[]{:S(2)}) copy-start(f32[688,128]{1,0:T(8,128)S(1)} %collective-permute-done.4.c.bf) | copy-start | bytes 1056772

commit v2 on v1

--- a/solution.py
+++ b/solution.py
@@ -9,7 +9,7 @@
 
 DT2 = 0.0625
 NL = 128
-Y_ROWS, A_ROWS, C_ROWS, R_ROWS = 400, 736, 528, 160
+Y_ROWS, A_ROWS, C_ROWS, R_ROWS, O_ROWS = 400, 736, 528, 160, 64
 YB, YC, YD = 128, 224, 320
 AB, AC, AD = 256, 448, 576
 CB_, CC, CS = 64, 88, 264
@@ -35,7 +35,29 @@
     return v.reshape(-1, NL)
 
 
-def pack_own(fn, fp, fr, fm, fl, fj, cn, cp, cr, cm, cl, cj, ix, wt, yn, yf, an, af, fo, co):
+def y_edge(out, low, fn, fp, fj, fo, cn, cp, cj, co):
+    for i in range(4):
+        for x in range(8):
+            v = fn[i, x] if i < 3 else fj[x] * (1.0 / 12.0)
+            out[i * 32 + x * 4 : i * 32 + x * 4 + 4] = v[0:4] if low else v[12:16]
+    for i in range(6):
+        for x in range(8):
+            v = fp[i, x] if i < 3 else fo[i - 3, x]
+            v = v[0:2] if low else v[14:16]
+            if i == 5:
+                v = pltpu.roll(v, 8 if low else 120, 1)
+            out[YB + i * 16 + x * 2 : YB + i * 16 + x * 2 + 2] = v
+    for i in range(4):
+        for x in range(4):
+            v = cn[i, x] if i < 3 else cj[x] * (1.0 / 12.0)
+            out[YC + i * 24 + x * 6 : YC + i * 24 + x * 6 + 6] = v[0:6] if low else v[2:8]
+    for i in range(5):
+        for x in range(4):
+            v = cp[i, x] if i < 3 else co[i - 3, x]
+            out[YD + i * 16 + x * 4 : YD + i * 16 + x * 4 + 4] = v[0:4] if low else v[4:8]
+
+
+def pack_y(fn, fp, fr, fm, fl, fj, cn, cp, cr, cm, cl, cj, ix, wt, yf, yn, ro, fo, co):
     inv = DT2 / fr[...]
     fo[0] = fm[...] * inv
     fo[1] = (fl[...] + fm[...]) * inv
@@ -50,34 +72,25 @@
     for k in range(16):
         acc = acc + jnp.where(lane == slot[:, k : k + 1], weight[:, k : k + 1], 0.0)
     fo[2] = acc.reshape(8, 16, NL)
-
-    def fine_u(i, x):
-        return fn[i, x] if i < 3 else fj[x] * (1.0 / 12.0)
-
-    def coarse_u(i, x):
-        return cn[i, x] if i < 3 else cj[x] * (1.0 / 12.0)
-
-    def y_edge(out, low):
-        for i in range(4):
-            for x in range(8):
-                v = fine_u(i, x)
-                out[i * 32 + x * 4 : i * 32 + x * 4 + 4] = v[0:4] if low else v[12:16]
-        for i in range(6):
-            for x in range(8):
-                v = fp[i, x] if i < 3 else fo[i - 3, x]
-                v = v[0:2] if low else v[14:16]
-                if i == 5:
-                    v = pltpu.roll(v, 8 if low else 120, 1)
-                out[YB + i * 16 + x * 2 : YB + i * 16 + x * 2 + 2] = v
-        for i in range(4):
-            for x in range(4):
-                v = coarse_u(i, x)
-                out[YC + i * 24 + x * 6 : YC + i * 24 + x * 6 + 6] = v[0:6] if low else v[2:8]
-        for i in range(5):
-            for x in range(4):
-                v = cp[i, x] if i < 3 else co[i - 3, x]
-                out[YD + i * 16 + x * 4 : YD + i * 16 + x * 4 + 4] = v[0:4] if low else v[4:8]
-
+    oy = odd("gy")
+
+    @pl.when(oy == 0)
+    def _():
+        y_edge(yf, True, fn, fp, fj, fo, cn, cp, cj, co)
+        y_edge(yn, False, fn, fp, fj, fo, cn, cp, cj, co)
+
+    @pl.when(oy == 1)
+    def _():
+        y_edge(yf, False, fn, fp, fj, fo, cn, cp, cj, co)
+        y_edge(yn, True, fn, fp, fj, fo, cn, cp, cj, co)
+    yf[Y_ROWS:] = jnp.zeros((8, NL), F32)
+    x0 = 2 - 2 * odd("gx")
+    for i in range(4):
+        v = cn[i, pl.ds(x0, 2)] if i < 3 else cj[pl.ds(x0, 2)] * (1.0 / 12.0)
+        ro[i * 16 : i * 16 + 16] = rows(v)
+
+
+def pack_x(fn, fp, fj, fo, cn, cp, cj, co, an, af):
     def x_edge(out, low):
         x0 = 0 if low else 4
         for i in range(4):
@@ -94,17 +107,7 @@
             v = cp[i] if i < 3 else co[i - 3]
             out[AD + i * 32 : AD + i * 32 + 32] = rows(v)
 
-    ox, oy = odd("gx"), odd("gy")
-
-    @pl.when(oy == 0)
-    def _():
-        y_edge(yn, False)
-        y_edge(yf, True)
-
-    @pl.when(oy == 1)
-    def _():
-        y_edge(yn, True)
-        y_edge(yf, False)
+    ox = odd("gx")
 
     @pl.when(ox == 0)
     def _():
@@ -127,7 +130,8 @@
     out[base + CC : base + CS] = src[YC:Y_ROWS]
 
 
-def pack_near(rn, rf, out):
+def pack_near(rn, rf, ro, out):
+    out[C_ROWS : C_ROWS + O_ROWS] = ro[...]
     ox = odd("gx")
 
     @pl.when(ox == 0)
@@ -143,7 +147,8 @@
 
 def pack_relay(a, c, out, base, x0):
     for i in range(4):
-        out[base + i * 16 : base + i * 16 + 16] = a[AC + i * 32 + x0 * 8 : AC + i * 32 + x0 * 8 + 16]
+        o = C_ROWS + i * 16 if a is None else AC + i * 32 + x0 * 8
+        out[base + i * 16 : base + i * 16 + 16] = (c if a is None else a)[o : o + 16]
     for s in range(2):
         for i in range(4):
             o = s * CS + CC + i * 24 + x0 * 6
@@ -151,20 +156,20 @@
             out[t : t + 12] = c[o : o + 12]
 
 
-def pack_far(rn, rf, a, c, out):
+def pack_far(rn, rf, c, out):
     ox = odd("gx")
 
     @pl.when(ox == 0)
     def _():
         pack_corner(rn, out, 0, True)
         pack_corner(rf, out, CS, True)
-        pack_relay(a, c.at[1], out, C_ROWS, 0)
+        pack_relay(None, c.at[1], out, C_ROWS, 0)
 
     @pl.when(ox == 1)
     def _():
         pack_corner(rn, out, 0, False)
         pack_corner(rf, out, CS, False)
-        pack_relay(a, c.at[0], out, C_ROWS, 2)
+        pack_relay(None, c.at[0], out, C_ROWS, 2)
 
 
 def pack_second(a, c, out):
@@ -414,14 +419,21 @@
 INTERPRET = False
 
 
-def call(body, shapes, *operands, scratch=()):
+def call(body, shapes, *operands, scratch=(), local=True):
+    vmem = pl.BlockSpec(memory_space=pltpu.VMEM)
     return pl.pallas_call(
         body,
-        out_shape=[jax.ShapeDtypeStruct(s, F32) for s in shapes],
+        out_shape=[pltpu.VMEM(s, F32) if local else jax.ShapeDtypeStruct(s, F32) for s in shapes],
+        in_specs=[vmem] * len(operands),
+        out_specs=[vmem] * len(shapes),
         scratch_shapes=[pltpu.VMEM(s, F32) for s in scratch],
         compiler_params=pltpu.CompilerParams(vmem_limit_bytes=56 << 20),
         interpret=INTERPRET,
     )(*operands)
+
+
+def keep(v):
+    return v if INTERPRET else pltpu.with_memory_space_constraint(v, pltpu.VMEM)
 
 
 def on_device(
@@ -433,29 +445,36 @@
     groups = [[i, i + 1] for i in range(0, gx, 2)]
     table = jnp.asarray(vertical_matrix(), jnp.bfloat16)
 
-    yn, yf, an, af, fo, co = call(
-        pack_own,
-        [(Y_ROWS, NL)] * 2 + [(A_ROWS, NL)] * 2 + [(3, 8, 16, NL), (2, 4, 8, NL)],
+    yf, yn, ro, fo, co = call(
+        pack_y,
+        [(Y_ROWS + 8, NL), (Y_ROWS, NL), (O_ROWS, NL), (3, 8, 16, NL), (2, 4, 8, NL)],
         fine_now, fine_prev, fine_rho, fine_mu, fine_lam, fine_metric,
         coarse_now, coarse_prev, coarse_rho, coarse_mu, coarse_lam, coarse_metric,
         couple_index, couple_weight,
     )
-    yn = lax.ppermute(yn, "gy", near_y)
-    yf = lax.ppermute(yf, "gy", far_y)
-    af = lax.ppermute(af, "gx", far_x)
-    an = lax.ppermute(an, "gx", near_x)
-    (cn,) = call(pack_near, [(C_ROWS, NL)], yn, yf)
-    gn = lax.all_gather(cn, "gx", axis_index_groups=groups)
-    (bf,) = call(pack_far, [(C_ROWS + R_ROWS, NL)], yn, yf, an, gn)
-    bf = lax.ppermute(bf, "gx", far_x)
+    fo, co, ro = keep(fo), keep(co), keep(ro)
+    yf = keep(lax.ppermute(yf, "gy", far_y))
+    yn = keep(lax.ppermute(yn, "gy", near_y))
+    an, af = call(
+        pack_x,
+        [(A_ROWS, NL)] * 2,
+        fine_now, fine_prev, fine_metric, fo, coarse_now, coarse_prev, coarse_metric, co,
+    )
+    an = keep(lax.ppermute(an, "gx", near_x))
+    af = keep(lax.ppermute(af, "gx", far_x))
+    (cn,) = call(pack_near, [(C_ROWS + O_ROWS, NL)], yn, yf, ro)
+    gn = keep(lax.all_gather(cn, "gx", axis_index_groups=groups))
+    (bf,) = call(pack_far, [(C_ROWS + R_ROWS, NL)], yn, yf, gn)
+    bf = keep(lax.ppermute(bf, "gx", far_x))
     (r2,) = call(pack_second, [(R_ROWS, NL)], af, bf)
-    g2 = lax.all_gather(r2, "gx", axis_index_groups=groups)
+    g2 = keep(lax.all_gather(r2, "gx", axis_index_groups=groups))
     return tuple(
         call(
             main,
             [(3, 8, 16, NL), (3, 4, 8, NL)],
             fine_now, fine_prev, fine_metric, fo, coarse_now, coarse_prev, coarse_metric, co,
             yn, yf, an, af, gn, bf, g2, table,
+            local=False,
             scratch=[
                 (4, 16, 24, NL), (6, 12, 24, NL), (4, 16, 24, NL), (5, 12, 24, NL),
                 (3, 12, 24, NL), (3, 12, 24, NL), (16, 24, NL), (4, 12, 24, NL), (16, 16, NL), (12, 24, NL),

time: 73 us -> 56.3 us (0.77)
  starting transfers between devices: 38.2 us -> 31.5 us
  Pallas kernels: 15.7 us -> 9.37 us
  blocking collectives: 8.39 us -> 5.66 us
  local copies, waits for them, and re-layouts: 2.2 us -> 0 us
  waiting for transfers between devices: 7.05 us -> 8.76 us
    ppermute x5, starting transfers between devices: 38.2 us -> 31.5 us  [the longest x1 14.1 us: on_device(): yf = keep(lax.ppermute(yf, 'gy', far_y))]
    pallas_call x5 -> x6, Pallas kernels: 15.7 us -> 9.37 us  [call(): pl.pallas_call(body, out_shape=[pltpu.VMEM(s, F32) if local else jax.Shap...]
    all_gather x2, blocking collectives: 8.39 us -> 5.66 us  [the longest x1 3.74 us: on_device(): gn = keep(lax.all_gather(cn, 'gx', axis_index_groups=groups))]
    unnamed x10 -> x0, local copies, waits for them, and re-layouts: 2.2 us -> none
    ppermute x5, waiting for transfers between devices: 7.05 us -> 8.76 us  [the longest x1 4.46 us: on_device(): af = keep(lax.ppermute(af, 'gx', far_x))]
  transfers between devices with their start and end apart: 5 -> 5, of which waited for: 2 -> 3; matrix products, arithmetic and copies ran while one was open for 0% -> 0% of each run, Pallas kernels for 5% -> 2%
where the time goes in v2:
time: 56.3 us; the launch traced here: 56 us
  starting transfers between devices  31.5 us (56%)
  Pallas kernels  9.37 us (17%)
  waiting for transfers between devices  8.76 us (16%)
  blocking collectives  5.66 us (10%)
  between operations  0.7 us (1%)
    ppermute x1, starting transfers between devices, on_device(): yf = keep(lax.ppermute(yf, 'gy', far_y))  14.1 us
    ppermute x1, starting transfers between devices, on_device(): bf = keep(lax.ppermute(bf, 'gx', far_x))  9.68 us
    pallas_call x6, Pallas kernels, call(): pl.pallas_call(body, out_shape=[pltpu.VMEM(s, F32) if local else jax.Shap...  9.37 us
    ppermute x1, waiting for transfers between devices, on_device(): af = keep(lax.ppermute(af, 'gx', far_x))  4.46 us
    ppermute x1, starting transfers between devices, on_device(): af = keep(lax.ppermute(af, 'gx', far_x))  3.95 us
    ppermute x1, waiting for transfers between devices, on_device(): bf = keep(lax.ppermute(bf, 'gx', far_x))  3.77 us
    all_gather x1, blocking collectives, on_device(): gn = keep(lax.all_gather(cn, 'gx', axis_index_groups=groups))  3.74 us
    all_gather x1, blocking collectives, on_device(): g2 = keep(lax.all_gather(r2, 'gx', axis_index_groups=groups))  1.92 us
  transfers between devices with their start and end apart: 5, of which 3 were waited for; matrix products, arithmetic and copies ran while one was open for 0% of the time, Pallas kernels for 2%

profile of v2, /device:TPU:57, one launch (start us, length us, event | category | flops | bytes accessed | tf_op | source)
XLA Modules:
  0.0 56.0 jit_solution(11455821608123232201)
XLA Ops:
  0.6 2.0 %shard_map.158 = (f32[408,128]{1,0:T(8,128)S(1)}, f32[400,128]{1,0:T(8,128)S(1)}, f32[64,128]{1,0:T(8,128)S(1)}, f32[3,8,16,128]{3,2,1,0:T(8,128)S(1)}, f32[2,4,8,128]{3,2,1,0:T(8,128)S(1)}) custom-call(f32[3,8,16,128]{3,2,1,0:T(8,128)} %fn.5, f32[3,8,16,128]{3,2,1,0:T(8,128)} %fp.5, f32[8,16,128]{2,1,0:T(8,128)} %fr.1, f32[8,16,128]{2,1,0:T(8,128)} %fm.1, ...), custom_call_target="tpu_custom_call" | custom-call | tf_op jit(solution)/shard_map/pallas_call | solution.py:424
  2.6 14.1 %collective-permute-start.1 = (f32[408,128]{1,0:T(8,128)S(1)}, f32[408,128]{1,0:T(8,128)S(1)}, u32[]{:S(2)}, u32[]{:S(2)}) collective-permute-start(f32[408,128]{1,0:T(8,128)S(1)} %get-tuple-element.12), channel_id=1, source_target_pairs={{1,2},{2,1},{3,4},{4,3},{5,6},{6,5},{7,8},{8,7},{9,10},{10,9},{11,... | collective-permute-start | bytes 626696 | tf_op jit(solution)/shard_map/ppermute | solution.py:456
  16.7 1.9 %collective-permute-start = (f32[400,128]{1,0:T(8,128)S(1)}, f32[400,128]{1,0:T(8,128)S(1)}, u32[]{:S(2)}, u32[]{:S(2)}) collective-permute-start(f32[400,128]{1,0:T(8,128)S(1)} %get-tuple-element.11), channel_id=1, source_target_pairs={{0,1},{1,0},{2,3},{3,2},{4,5},{5,4},{6,7},{7,6},{8,9},{9,8},{10,11... | collective-permute-start | bytes 614408 | tf_op jit(solution)/shard_map/ppermute | solution.py:457
  18.6 1.1 %shard_map.159 = (f32[736,128]{1,0:T(8,128)S(1)}, f32[736,128]{1,0:T(8,128)S(1)}) custom-call(f32[3,8,16,128]{3,2,1,0:T(8,128)} %fn.5, f32[3,8,16,128]{3,2,1,0:T(8,128)} %fp.5, f32[8,16,128]{2,1,0:T(8,128)} %fj.5, f32[3,8,16,128]{3,2,1,0:T(8,128)S(1)} %get-tuple-element.9.fo, f32[3,4,8,128]{3,2,1,0:T(8,128)} %cn.5, f32[3,4,8,128]{3,2,1,0:T(8,128)} %cp.5, ...), custom_call_target="tpu_custom_call" | custom-call | tf_op jit(solution)/shard_map/pallas_call | solution.py:424
  19.7 3.9 %collective-permute-start.3 = (f32[736,128]{1,0:T(8,128)S(1)}, f32[736,128]{1,0:T(8,128)S(1)}, u32[]{:S(2)}, u32[]{:S(2)}) collective-permute-start(f32[736,128]{1,0:T(8,128)S(1)} %get-tuple-element.14), channel_id=1, source_target_pairs={{16,32},{32,16},{48,64},{64,48},{80,96},{96,80},{112,128},{128,112... | collective-permute-start | bytes 1130504 | tf_op jit(solution)/shard_map/ppermute | solution.py:464
  23.7 0.5 collective-permute-done.rn.yn
  24.2 0.0 collective-permute-done.1.rf.yf
  24.3 3.7 %all-gather = f32[1184,128]{1,0:T(8,128)S(1)} all-gather(f32[592,128]{1,0:T(8,128)S(1)} %shard_map.160), channel_id=2, replica_groups={{0,16},{32,48},{64,80},{96,112},{128,144},{160,176},{192,208},{224,240}..., dimensions={0}, use_global_device_ids=true | all-gather | bytes 909312 | tf_op jit(solution)/shard_map/all_gather | solution.py:466
  28.0 9.7 %collective-permute-start.4 = (f32[688,128]{1,0:T(8,128)S(1)}, f32[688,128]{1,0:T(8,128)S(1)}, u32[]{:S(2)}, u32[]{:S(2)}) collective-permute-start(f32[688,128]{1,0:T(8,128)S(1)} %shard_map.161), channel_id=1, source_target_pairs={{16,32},{32,16},{48,64},{64,48},{80,96},{96,80},{112,128},{128,112... | collective-permute-start | bytes 1056776 | tf_op jit(solution)/shard_map/ppermute | solution.py:468
  37.7 1.9 %collective-permute-start.2 = (f32[736,128]{1,0:T(8,128)S(1)}, f32[736,128]{1,0:T(8,128)S(1)}, u32[]{:S(2)}, u32[]{:S(2)}) collective-permute-start(f32[736,128]{1,0:T(8,128)S(1)} %get-tuple-element.13), channel_id=1, source_target_pairs={{0,16},{16,0},{32,48},{48,32},{64,80},{80,64},{96,112},{112,96},{1... | collective-permute-start | bytes 1130504 | tf_op jit(solution)/shard_map/ppermute | solution.py:463
  39.6 4.5 %collective-permute-done.3.a.af = f32[736,128]{1,0:T(8,128)S(1)} collective-permute-done((f32[736,128]{1,0:T(8,128)S(1)}, f32[736,128]{1,0:T(8,128)S(1)}, u32[]{:S(2)}, u32[]{:S(2)}) %collective-permute-start.3) | collective-permute-done | bytes 376864 | tf_op jit(solution)/shard_map/ppermute | solution.py:464
  44.1 3.8 %collective-permute-done.4.c.bf = f32[688,128]{1,0:T(8,128)S(1)} collective-permute-done((f32[688,128]{1,0:T(8,128)S(1)}, f32[688,128]{1,0:T(8,128)S(1)}, u32[]{:S(2)}, u32[]{:S(2)}) %collective-permute-start.4) | collective-permute-done | bytes 352288 | tf_op jit(solution)/shard_map/ppermute | solution.py:468
  47.9 1.9 %all-gather.1 = f32[320,128]{1,0:T(8,128)S(1)} all-gather(f32[160,128]{1,0:T(8,128)S(1)} %shard_map.162), channel_id=3, replica_groups={{0,16},{32,48},{64,80},{96,112},{128,144},{160,176},{192,208},{224,240}..., dimensions={0}, use_global_device_ids=true | all-gather | bytes 245760 | tf_op jit(solution)/shard_map/all_gather | solution.py:470
  49.8 0.0 collective-permute-done.2.an
  49.8 6.2 %shard_map.163 = (f32[3,8,16,128]{3,2,1,0:T(8,128)}, f32[3,4,8,128]{3,2,1,0:T(8,128)}) custom-call(f32[3,8,16,128]{3,2,1,0:T(8,128)} %fn.5, f32[3,8,16,128]{3,2,1,0:T(8,128)} %fp.5, f32[8,16,128]{2,1,0:T(8,128)} %fj.5, f32[3,8,16,128]{3,2,1,0:T(8,128)S(1)} %get-tuple-element.9.fo, f32[3,4,8,128]{3,2,1,0:T(8,128)} %cn.5, f32[3,4,8,128]{3,2,1,0:T(8,128)} %cp.5, ...), custom_call_target="tpu_custom_call" | custom-call | tf_op jit(solution)/shard_map/pallas_call | solution.py:424
  (3 shorter events, 0.1 us)
Async XLA Ops:
  2.6 21.6 %collective-permute-start.1 = (f32[408,128]{1,0:T(8,128)S(1)}, f32[408,128]{1,0:T(8,128)S(1)}, u32[]{:S(2)}, u32[]{:S(2)}) collective-permute-start(f32[408,128]{1,0:T(8,128)S(1)} %get-tuple-element.12), channel_id=1, source_target_pairs={{1,2},{2,1},{3,4},{4,3},{5,6},{6,5},{7,8},{8,7},{9,10},{10,9},{11,... | collective-permute-start | bytes 626696 | tf_op jit(solution)/shard_map/ppermute | solution.py:456
  16.7 7.5 %collective-permute-start = (f32[400,128]{1,0:T(8,128)S(1)}, f32[400,128]{1,0:T(8,128)S(1)}, u32[]{:S(2)}, u32[]{:S(2)}) collective-permute-start(f32[400,128]{1,0:T(8,128)S(1)} %get-tuple-element.11), channel_id=1, source_target_pairs={{0,1},{1,0},{2,3},{3,2},{4,5},{5,4},{6,7},{7,6},{8,9},{9,8},{10,11... | collective-permute-start | bytes 614408 | tf_op jit(solution)/shard_map/ppermute | solution.py:457
  19.7 24.4 %collective-permute-start.3 = (f32[736,128]{1,0:T(8,128)S(1)}, f32[736,128]{1,0:T(8,128)S(1)}, u32[]{:S(2)}, u32[]{:S(2)}) collective-permute-start(f32[736,128]{1,0:T(8,128)S(1)} %get-tuple-element.14), channel_id=1, source_target_pairs={{16,32},{32,16},{48,64},{64,48},{80,96},{96,80},{112,128},{128,112... | collective-permute-start | bytes 1130504 | tf_op jit(solution)/shard_map/ppermute | solution.py:464
  28.0 19.9 %collective-permute-start.4 = (f32[688,128]{1,0:T(8,128)S(1)}, f32[688,128]{1,0:T(8,128)S(1)}, u32[]{:S(2)}, u32[]{:S(2)}) collective-permute-start(f32[688,128]{1,0:T(8,128)S(1)} %shard_map.161), channel_id=1, source_target_pairs={{16,32},{32,16},{48,64},{64,48},{80,96},{96,80},{112,128},{128,112... | collective-permute-start | bytes 1056776 | tf_op jit(solution)/shard_map/ppermute | solution.py:468
  37.7 12.1 %collective-permute-start.2 = (f32[736,128]{1,0:T(8,128)S(1)}, f32[736,128]{1,0:T(8,128)S(1)}, u32[]{:S(2)}, u32[]{:S(2)}) collective-permute-start(f32[736,128]{1,0:T(8,128)S(1)} %get-tuple-element.13), channel_id=1, source_target_pairs={{0,16},{16,0},{32,48},{48,32},{64,80},{80,64},{96,112},{112,96},{1... | collective-permute-start | bytes 1130504 | tf_op jit(solution)/shard_map/ppermute | solution.py:463

commit v3 on v2

--- a/solution.py
+++ b/solution.py
@@ -9,10 +9,10 @@
 
 DT2 = 0.0625
 NL = 128
-Y_ROWS, A_ROWS, C_ROWS, R_ROWS, O_ROWS = 400, 736, 528, 160, 64
-YB, YC, YD = 128, 224, 320
-AB, AC, AD = 256, 448, 576
-CB_, CC, CS = 64, 88, 264
+Y_ROWS, A_ROWS, C_ROWS, R_ROWS, O_ROWS = 336, 664, 400, 24, 8
+YB, YC, YD, YT = 128, 224, 288, 328
+AB, AC, AD, AT = 256, 448, 576, 656
+CB_, CC, CD, CT, CS = 64, 88, 152, 192, 200
 F32 = jnp.float32
 
 
@@ -27,6 +27,24 @@
     return np.concatenate([m.T, m.T], 0)
 
 
+class Joined:
+    def __init__(self, one, two):
+        self.one, self.two = one, two
+
+    def at(self, s):
+        if s.stop <= AB:
+            return self.one, s
+        return self.two, slice(s.start - AB, s.stop - AB)
+
+    def __getitem__(self, s):
+        ref, s = self.at(s)
+        return ref[s]
+
+    def __setitem__(self, s, v):
+        ref, s = self.at(s)
+        ref[s] = v
+
+
 def odd(axis):
     return lax.axis_index(axis) % 2
 
@@ -35,7 +53,20 @@
     return v.reshape(-1, NL)
 
 
-def y_edge(out, low, fn, fp, fj, fo, cn, cp, cj, co):
+def tops_of(groups, first_slot=0):
+    lane = lax.broadcasted_iota(jnp.int32, (8, NL), 1)
+    acc = jnp.zeros((8, NL), F32)
+    for k, v in enumerate(groups, first_slot):
+        acc = jnp.where(lane // 8 == k, pltpu.roll(v, (8 * k + 8) % NL, 1), acc)
+    return acc
+
+
+def top_of(packed, slot):
+    lane = lax.broadcasted_iota(jnp.int32, (8, NL), 1)
+    return jnp.where(lane >= NL - 8, pltpu.roll(packed, (NL - 8 - 8 * slot) % NL, 1), 0.0)
+
+
+def y_edge(out, stage, low, fn, fp, fj, fo, cn, cp, cj, co):
     for i in range(4):
         for x in range(8):
             v = fn[i, x] if i < 3 else fj[x] * (1.0 / 12.0)
@@ -50,14 +81,34 @@
     for i in range(4):
         for x in range(4):
             v = cn[i, x] if i < 3 else cj[x] * (1.0 / 12.0)
-            out[YC + i * 24 + x * 6 : YC + i * 24 + x * 6 + 6] = v[0:6] if low else v[2:8]
+            out[YC + i * 16 + x * 4 : YC + i * 16 + x * 4 + 4] = v[0:4] if low else v[4:8]
+            stage[i * 8 + x * 2 : i * 8 + x * 2 + 2] = v[4:6] if low else v[2:4]
     for i in range(5):
         for x in range(4):
             v = cp[i, x] if i < 3 else co[i - 3, x]
-            out[YD + i * 16 + x * 4 : YD + i * 16 + x * 4 + 4] = v[0:4] if low else v[4:8]
-
-
-def pack_y(fn, fp, fr, fm, fl, fj, cn, cp, cr, cm, cl, cj, ix, wt, yf, yn, ro, fo, co):
+            out[YD + i * 8 + x * 2 : YD + i * 8 + x * 2 + 2] = v[0:2] if low else v[6:8]
+            stage[32 + i * 8 + x * 2 : 32 + i * 8 + x * 2 + 2] = v[2:4] if low else v[4:6]
+    out[YT:Y_ROWS] = tops_of([stage[k * 8 : k * 8 + 8] for k in range(9)])
+
+
+def pack_y(fn, fp, fj, fo, cn, cp, cj, co, yf, yn, ro, stage):
+    oy = odd("gy")
+
+    @pl.when(oy == 0)
+    def _():
+        y_edge(yf, stage, True, fn, fp, fj, fo, cn, cp, cj, co)
+        y_edge(yn, stage, False, fn, fp, fj, fo, cn, cp, cj, co)
+
+    @pl.when(oy == 1)
+    def _():
+        y_edge(yf, stage, False, fn, fp, fj, fo, cn, cp, cj, co)
+        y_edge(yn, stage, True, fn, fp, fj, fo, cn, cp, cj, co)
+    yf[Y_ROWS:] = jnp.zeros((8, NL), F32)
+    x0 = 2 - 2 * odd("gx")
+    ro[...] = tops_of([cn[i, x0 + x] if i < 3 else cj[x0 + x] * (1.0 / 12.0) for i in range(4) for x in range(2)])
+
+
+def pack_x(fn, fp, fr, fm, fl, fj, cn, cp, cr, cm, cl, cj, ix, wt, an, am, af, fo, co):
     inv = DT2 / fr[...]
     fo[0] = fm[...] * inv
     fo[1] = (fl[...] + fm[...]) * inv
@@ -72,25 +123,9 @@
     for k in range(16):
         acc = acc + jnp.where(lane == slot[:, k : k + 1], weight[:, k : k + 1], 0.0)
     fo[2] = acc.reshape(8, 16, NL)
-    oy = odd("gy")
-
-    @pl.when(oy == 0)
-    def _():
-        y_edge(yf, True, fn, fp, fj, fo, cn, cp, cj, co)
-        y_edge(yn, False, fn, fp, fj, fo, cn, cp, cj, co)
-
-    @pl.when(oy == 1)
-    def _():
-        y_edge(yf, False, fn, fp, fj, fo, cn, cp, cj, co)
-        y_edge(yn, True, fn, fp, fj, fo, cn, cp, cj, co)
-    yf[Y_ROWS:] = jnp.zeros((8, NL), F32)
-    x0 = 2 - 2 * odd("gx")
-    for i in range(4):
-        v = cn[i, pl.ds(x0, 2)] if i < 3 else cj[pl.ds(x0, 2)] * (1.0 / 12.0)
-        ro[i * 16 : i * 16 + 16] = rows(v)
-
-
-def pack_x(fn, fp, fj, fo, cn, cp, cj, co, an, af):
+
+    near = Joined(an, am)
+
     def x_edge(out, low):
         x0 = 0 if low else 4
         for i in range(4):
@@ -103,20 +138,22 @@
         for i in range(4):
             v = cn[i] if i < 3 else cj[...] * (1.0 / 12.0)
             out[AC + i * 32 : AC + i * 32 + 32] = rows(v)
+        x0, x1 = (0, 2) if low else (2, 0)
         for i in range(5):
-            v = cp[i] if i < 3 else co[i - 3]
-            out[AD + i * 32 : AD + i * 32 + 32] = rows(v)
+            v = cp[i, x0 : x0 + 2] if i < 3 else co[i - 3, x0 : x0 + 2]
+            out[AD + i * 16 : AD + i * 16 + 16] = rows(v)
+        out[AT:A_ROWS] = tops_of([cp[i, x1 + x] if i < 3 else co[i - 3, x1 + x] for i in range(5) for x in range(2)])
 
     ox = odd("gx")
 
     @pl.when(ox == 0)
     def _():
-        x_edge(an, False)
+        x_edge(near, False)
         x_edge(af, True)
 
     @pl.when(ox == 1)
     def _():
-        x_edge(an, True)
+        x_edge(near, True)
         x_edge(af, False)
 
 
@@ -145,15 +182,11 @@
         pack_corner(rf, out, CS, True)
 
 
-def pack_relay(a, c, out, base, x0):
-    for i in range(4):
-        o = C_ROWS + i * 16 if a is None else AC + i * 32 + x0 * 8
-        out[base + i * 16 : base + i * 16 + 16] = (c if a is None else a)[o : o + 16]
-    for s in range(2):
-        for i in range(4):
-            o = s * CS + CC + i * 24 + x0 * 6
-            t = base + 64 + s * 48 + i * 12
-            out[t : t + 12] = c[o : o + 12]
+def pack_relay(own, c, out, base, x0):
+    corners = [c[o : o + 8] for s in range(2) for i in range(4) for o in [s * CS + CC + i * 16 + x0 * 4]]
+    out[base : base + 8] = own + tops_of(corners, 8)
+    out[base + 8 : base + 16] = c[CT:CS]
+    out[base + 16 : base + 24] = c[CS + CT : 2 * CS]
 
 
 def pack_far(rn, rf, c, out):
@@ -163,25 +196,29 @@
     def _():
         pack_corner(rn, out, 0, True)
         pack_corner(rf, out, CS, True)
-        pack_relay(None, c.at[1], out, C_ROWS, 0)
+        pack_relay(c[1, C_ROWS : C_ROWS + 8], c.at[1], out, C_ROWS, 0)
 
     @pl.when(ox == 1)
     def _():
         pack_corner(rn, out, 0, False)
         pack_corner(rf, out, CS, False)
-        pack_relay(None, c.at[0], out, C_ROWS, 2)
+        pack_relay(c[0, C_ROWS : C_ROWS + 8], c.at[0], out, C_ROWS, 2)
 
 
 def pack_second(a, c, out):
     ox = odd("gx")
 
+    def facing(x0):
+        own = [a[o : o + 8] for i in range(4) for x in range(2) for o in [AC + i * 32 + (x0 + x) * 8]]
+        pack_relay(tops_of(own), c, out, 0, x0)
+
     @pl.when(ox == 0)
     def _():
-        pack_relay(a, c, out, 0, 2)
+        facing(2)
 
     @pl.when(ox == 1)
     def _():
-        pack_relay(a, c, out, 0, 0)
+        facing(0)
 
 
 def vertical(v, table):
@@ -237,7 +274,7 @@
 
 
 def main(
-    fn, fp, fj, fo, cn, cp, cj, co, yn, yf, an, af, gn, bf, g2, table_ref,
+    fn, fp, fj, fo, cn, cp, cj, co, yn, yf, an, am, af, gn, bf, g2, table_ref,
     fine_out, coarse_out, fe, fb, ce, cb, f1, c1, lift, work, tops, face,
 ):
     ox, oy = odd("gx"), odd("gy")
@@ -263,7 +300,7 @@
     near, far = ox == 0, ox == 1
     other = 1 - ox
     sides = (
-        (an, gn.at[other], g2.at[other], near, 0),
+        (Joined(an, am), gn.at[other], g2.at[other], near, 0),
         (af, bf, bf, far, C_ROWS),
     )
     for a, c, r, high, base in sides:
@@ -271,36 +308,45 @@
         f2 = jnp.where(high, 10, 0)
         c4 = jnp.where(high, 10, 2)
         c2 = jnp.where(high, 14, 0)
-        b4 = jnp.where(high, 8, 0)
+        b2 = jnp.where(high, 8, 2)
+        b4 = jnp.where(high, 10, 0)
+        own, top = r[base : base + 8], a[AT:A_ROWS]
         for i in range(4):
             for x in range(4):
                 fe[i, f4 + x, 4:20] = a[i * 64 + x * 16 : i * 64 + x * 16 + 16]
                 ce[i, c4 + x, 8:16] = a[AC + i * 32 + x * 8 : AC + i * 32 + x * 8 + 8]
             for x in range(2):
-                ce[i, c2 + x, 8:16] = r[base + i * 16 + x * 8 : base + i * 16 + x * 8 + 8]
+                ce[i, c2 + x, 8:16] = top_of(own, i * 2 + x)
         for i in range(6):
             for x in range(2):
                 fb[i, f2 + x, 4:20] = a[AB + i * 32 + x * 16 : AB + i * 32 + x * 16 + 16]
         for i in range(5):
-            for x in range(4):
-                cb[i, b4 + x, 8:16] = a[AD + i * 32 + x * 8 : AD + i * 32 + x * 8 + 8]
+            for x in range(2):
+                cb[i, b2 + x, 8:16] = a[AD + i * 16 + x * 8 : AD + i * 16 + x * 8 + 8]
+                cb[i, b4 + x, 8:16] = top_of(top, i * 2 + x)
 
     def y_side(src, s, high):
-        t4, t2, t6, t3 = (20, 20, 16, 16) if high else (0, 2, 2, 4)
+        t4, t2 = (20, 20) if high else (0, 2)
+        k4, k2, k1, k3 = (16, 20, 16, 18) if high else (4, 2, 6, 4)
+        top = src[YT:Y_ROWS]
         for i in range(4):
             for x in range(8):
                 fe[i, 4 + x, t4 : t4 + 4] = src[i * 32 + x * 4 : i * 32 + x * 4 + 4]
+            v = top_of(top, i)
             for x in range(4):
-                o = YC + i * 24 + x * 6
-                ce[i, 6 + x, t6 : t6 + 6] = src[o : o + 6]
+                o = YC + i * 16 + x * 4
+                ce[i, 6 + x, k4 : k4 + 4] = src[o : o + 4]
+                ce[i, 6 + x, k2 : k2 + 2] = v[x * 2 : x * 2 + 2]
         for i in range(6):
             for x in range(8):
                 o = YB + i * 16 + x * 2
                 fb[i, 2 + x, t2 : t2 + 2] = src[o : o + 2]
         for i in range(5):
+            v = top_of(top, 4 + i)
             for x in range(4):
-                o = YD + i * 16 + x * 4
-                cb[i, 4 + x, t3 : t3 + 4] = src[o : o + 4]
+                o = YD + i * 8 + x * 2
+                cb[i, 4 + x, k1 : k1 + 2] = src[o : o + 2]
+                cb[i, 4 + x, k3 : k3 + 2] = v[x * 2 : x * 2 + 2]
         for a, c, r, hx, base in sides:
             f4 = jnp.where(hx, 12, 0)
             f2 = jnp.where(hx, 10, 0)
@@ -308,23 +354,33 @@
             c2 = jnp.where(hx, 14, 0)
             b4 = jnp.where(hx, 8, 0)
             q = s * CS
+            top = c[q + CT : q + CS]
+            beyond = r[base : base + 8]
+            beyond_top = r[base + 8 + s * 8 : base + 16 + s * 8]
             for i in range(4):
+                v = top_of(top, i)
                 for x in range(4):
                     o = q + i * 16 + x * 4
                     fe[i, f4 + x, t4 : t4 + 4] = c[o : o + 4]
-                    o = q + CC + i * 24 + x * 6
-                    ce[i, c4 + x, t6 : t6 + 6] = c[o : o + 6]
+                    o = q + CC + i * 16 + x * 4
+                    ce[i, c4 + x, k4 : k4 + 4] = c[o : o + 4]
+                    ce[i, c4 + x, k2 : k2 + 2] = v[x * 2 : x * 2 + 2]
+                v = top_of(beyond, 8 + s * 4 + i)
+                w = top_of(beyond_top, i)
+                w = jnp.where(hx, w, pltpu.roll(w, 4, 0))
                 for x in range(2):
-                    o = base + 64 + s * 48 + i * 12 + x * 6
-                    ce[i, c2 + x, t6 : t6 + 6] = r[o : o + 6]
+                    ce[i, c2 + x, k4 : k4 + 4] = v[x * 4 : x * 4 + 4]
+                    ce[i, c2 + x, k2 : k2 + 2] = w[x * 2 : x * 2 + 2]
             for i in range(6):
                 for x in range(2):
                     o = q + CB_ + i * 4 + x * 2
                     fb[i, f2 + x, t2 : t2 + 2] = c[o : o + 2]
             for i in range(5):
+                v = top_of(top, 4 + i)
                 for x in range(4):
-                    o = q + CC + 96 + i * 16 + x * 4
-                    cb[i, b4 + x, t3 : t3 + 4] = c[o : o + 4]
+                    o = q + CD + i * 8 + x * 2
+                    cb[i, b4 + x, k1 : k1 + 2] = c[o : o + 2]
+                    cb[i, b4 + x, k3 : k3 + 2] = v[x * 2 : x * 2 + 2]
 
     @pl.when(oy == 0)
     def _():
@@ -445,23 +501,26 @@
     groups = [[i, i + 1] for i in range(0, gx, 2)]
     table = jnp.asarray(vertical_matrix(), jnp.bfloat16)
 
-    yf, yn, ro, fo, co = call(
-        pack_y,
-        [(Y_ROWS + 8, NL), (Y_ROWS, NL), (O_ROWS, NL), (3, 8, 16, NL), (2, 4, 8, NL)],
+    an, am, af, fo, co = call(
+        pack_x,
+        [(AB, NL), (A_ROWS - AB, NL), (A_ROWS, NL)] + [(3, 8, 16, NL), (2, 4, 8, NL)],
         fine_now, fine_prev, fine_rho, fine_mu, fine_lam, fine_metric,
         coarse_now, coarse_prev, coarse_rho, coarse_mu, coarse_lam, coarse_metric,
         couple_index, couple_weight,
     )
-    fo, co, ro = keep(fo), keep(co), keep(ro)
+    fo, co = keep(fo), keep(co)
+    af = keep(lax.ppermute(af, "gx", far_x))
+    yf, yn, ro = call(
+        pack_y,
+        [(Y_ROWS + 8, NL), (Y_ROWS, NL), (O_ROWS, NL)],
+        fine_now, fine_prev, fine_metric, fo, coarse_now, coarse_prev, coarse_metric, co,
+        scratch=[(72, NL)],
+    )
+    ro = keep(ro)
     yf = keep(lax.ppermute(yf, "gy", far_y))
     yn = keep(lax.ppermute(yn, "gy", near_y))
-    an, af = call(
-        pack_x,
-        [(A_ROWS, NL)] * 2,
-        fine_now, fine_prev, fine_metric, fo, coarse_now, coarse_prev, coarse_metric, co,
-    )
     an = keep(lax.ppermute(an, "gx", near_x))
-    af = keep(lax.ppermute(af, "gx", far_x))
+    am = keep(lax.ppermute(am, "gx", near_x))
     (cn,) = call(pack_near, [(C_ROWS + O_ROWS, NL)], yn, yf, ro)
     gn = keep(lax.all_gather(cn, "gx", axis_index_groups=groups))
     (bf,) = call(pack_far, [(C_ROWS + R_ROWS, NL)], yn, yf, gn)
@@ -473,7 +532,7 @@
             main,
             [(3, 8, 16, NL), (3, 4, 8, NL)],
             fine_now, fine_prev, fine_metric, fo, coarse_now, coarse_prev, coarse_metric, co,
-            yn, yf, an, af, gn, bf, g2, table,
+            yn, yf, an, am, af, gn, bf, g2, table,
             local=False,
             scratch=[
                 (4, 16, 24, NL), (6, 12, 24, NL), (4, 16, 24, NL), (5, 12, 24, NL),

time: 56.3 us -> 51.9 us (0.922)
  waiting for transfers between devices: 8.76 us -> 3.66 us
    ppermute x1, waiting for transfers between devices: 4.46 us -> 0.01 us  [on_device(): af = keep(lax.ppermute(af, 'gx', far_x))]
    ppermute x0 -> x1, starting transfers between devices: none -> 1.92 us  [on_device(): am = keep(lax.ppermute(am, 'gx', near_x))]
    ppermute x1, starting transfers between devices: 9.68 us -> 7.79 us  [on_device(): bf = keep(lax.ppermute(bf, 'gx', far_x))]
    ppermute x1, waiting for transfers between devices: 3.77 us -> 2.7 us  [on_device(): bf = keep(lax.ppermute(bf, 'gx', far_x))]
  transfers between devices with their start and end apart: 5 -> 6, of which waited for: 3 -> 2; matrix products, arithmetic and copies ran while one was open for 0% -> 0% of each run, Pallas kernels for 2% -> 0%
where the time goes in v3:
time: 51.9 us; the launch traced here: 51.6 us
  starting transfers between devices  32 us (62%)
  Pallas kernels  9.79 us (19%)
  blocking collectives  5.43 us (10%)
  waiting for transfers between devices  3.66 us (7%)
  between operations  0.71 us (1%)
    ppermute x1, starting transfers between devices, on_device(): yf = keep(lax.ppermute(yf, 'gy', far_y))  14.1 us
    pallas_call x6, Pallas kernels, call(): pl.pallas_call(body, out_shape=[pltpu.VMEM(s, F32) if local else jax.Shap...  9.79 us
    ppermute x1, starting transfers between devices, on_device(): bf = keep(lax.ppermute(bf, 'gx', far_x))  7.79 us
    ppermute x1, starting transfers between devices, on_device(): af = keep(lax.ppermute(af, 'gx', far_x))  3.94 us
    all_gather x1, blocking collectives, on_device(): gn = keep(lax.all_gather(cn, 'gx', axis_index_groups=groups))  3.6 us
    ppermute x1, waiting for transfers between devices, on_device(): bf = keep(lax.ppermute(bf, 'gx', far_x))  2.7 us
    ppermute x1, starting transfers between devices, on_device(): an = keep(lax.ppermute(an, 'gx', near_x))  2.41 us
    ppermute x1, starting transfers between devices, on_device(): yn = keep(lax.ppermute(yn, 'gy', near_y))  1.92 us
  transfers between devices with their start and end apart: 6, of which 2 were waited for; matrix products, arithmetic and copies ran while one was open for 0% of the time, Pallas kernels for 0%

profile of v3, /device:TPU:57, one launch (start us, length us, event | category | flops | bytes accessed | tf_op | source)
XLA Modules:
  0.0 51.6 jit_solution(13768656155586765794)
XLA Ops:
  0.6 2.0 %shard_map.158 = (f32[256,128]{1,0:T(8,128)S(1)}, f32[408,128]{1,0:T(8,128)S(1)}, f32[664,128]{1,0:T(8,128)S(1)}, f32[3,8,16,128]{3,2,1,0:T(8,128)S(1)}, f32[2,4,8,128]{3,2,1,0:T(8,128)S(1)}) custom-call(f32[3,8,16,128]{3,2,1,0:T(8,128)} %fn.5, f32[3,8,16,128]{3,2,1,0:T(8,128)} %fp.5, f32[8,16,128]{2,1,0:T(8,128)} %fr.1, f32[8,16,128]{2,1,0:T(8,128)} %fm.1, ...), custom_call_target="tpu_custom_call" | custom-call | tf_op jit(solution)/shard_map/pallas_call | solution.py:480
  2.6 1.3 %shard_map.159 = (f32[344,128]{1,0:T(8,128)S(1)}, f32[336,128]{1,0:T(8,128)S(1)}, f32[8,128]{1,0:T(8,128)S(1)}) custom-call(f32[3,8,16,128]{3,2,1,0:T(8,128)} %fn.5, f32[3,8,16,128]{3,2,1,0:T(8,128)} %fp.5, f32[8,16,128]{2,1,0:T(8,128)} %fj.5, f32[3,8,16,128]{3,2,1,0:T(8,128)S(1)} %get-tuple-element.10.fo, f32[3,4,8,128]{3,2,1,0:T(8,128)} %cn.5, ...), custom_call_target="tpu_custom_call" | custom-call | tf_op jit(solution)/shard_map/pallas_call | solution.py:480
  3.9 14.1 %collective-permute-start.1 = (f32[344,128]{1,0:T(8,128)S(1)}, f32[344,128]{1,0:T(8,128)S(1)}, u32[]{:S(2)}, u32[]{:S(2)}) collective-permute-start(f32[344,128]{1,0:T(8,128)S(1)} %get-tuple-element.13), channel_id=1, source_target_pairs={{1,2},{2,1},{3,4},{4,3},{5,6},{6,5},{7,8},{8,7},{9,10},{10,9},{11,... | collective-permute-start | bytes 528392 | tf_op jit(solution)/shard_map/ppermute | solution.py:520
  18.0 1.9 %collective-permute-start = (f32[336,128]{1,0:T(8,128)S(1)}, f32[336,128]{1,0:T(8,128)S(1)}, u32[]{:S(2)}, u32[]{:S(2)}) collective-permute-start(f32[336,128]{1,0:T(8,128)S(1)} %get-tuple-element.12), channel_id=1, source_target_pairs={{0,1},{1,0},{2,3},{3,2},{4,5},{5,4},{6,7},{7,6},{8,9},{9,8},{10,11... | collective-permute-start | bytes 516104 | tf_op jit(solution)/shard_map/ppermute | solution.py:521
  19.9 3.9 %collective-permute-start.4 = (f32[664,128]{1,0:T(8,128)S(1)}, f32[664,128]{1,0:T(8,128)S(1)}, u32[]{:S(2)}, u32[]{:S(2)}) collective-permute-start(f32[664,128]{1,0:T(8,128)S(1)} %get-tuple-element.16), channel_id=1, source_target_pairs={{16,32},{32,16},{48,64},{64,48},{80,96},{96,80},{112,128},{128,112... | collective-permute-start | bytes 1019912 | tf_op jit(solution)/shard_map/ppermute | solution.py:512
  23.8 0.9 %collective-permute-done.rn.yn = f32[336,128]{1,0:T(8,128)S(1)} collective-permute-done((f32[336,128]{1,0:T(8,128)S(1)}, f32[336,128]{1,0:T(8,128)S(1)}, u32[]{:S(2)}, u32[]{:S(2)}) %collective-permute-start) | collective-permute-done | bytes 172064 | tf_op jit(solution)/shard_map/ppermute | solution.py:521
  24.8 0.0 collective-permute-done.1.rf.yf
  24.8 3.6 %all-gather = f32[816,128]{1,0:T(8,128)S(1)} all-gather(f32[408,128]{1,0:T(8,128)S(1)} %shard_map.160), channel_id=2, replica_groups={{0,16},{32,48},{64,80},{96,112},{128,144},{160,176},{192,208},{224,240}..., dimensions={0}, use_global_device_ids=true | all-gather | bytes 626688 | tf_op jit(solution)/shard_map/all_gather | solution.py:525
  28.4 0.1 shard_map.161
  28.5 7.8 %collective-permute-start.5 = (f32[424,128]{1,0:T(8,128)S(1)}, f32[424,128]{1,0:T(8,128)S(1)}, u32[]{:S(2)}, u32[]{:S(2)}) collective-permute-start(f32[424,128]{1,0:T(8,128)S(1)} %shard_map.161), channel_id=1, source_target_pairs={{16,32},{32,16},{48,64},{64,48},{80,96},{96,80},{112,128},{128,112... | collective-permute-start | bytes 651272 | tf_op jit(solution)/shard_map/ppermute | solution.py:527
  36.3 1.9 %collective-permute-start.3 = (f32[408,128]{1,0:T(8,128)S(1)}, f32[408,128]{1,0:T(8,128)S(1)}, u32[]{:S(2)}, u32[]{:S(2)}) collective-permute-start(f32[408,128]{1,0:T(8,128)S(1)} %get-tuple-element.15), channel_id=1, source_target_pairs={{0,16},{16,0},{32,48},{48,32},{64,80},{80,64},{96,112},{112,96},{1... | collective-permute-start | bytes 626696 | tf_op jit(solution)/shard_map/ppermute | solution.py:523
  38.2 2.4 %collective-permute-start.2 = (f32[256,128]{1,0:T(8,128)S(1)}, f32[256,128]{1,0:T(8,128)S(1)}, u32[]{:S(2)}, u32[]{:S(2)}) collective-permute-start(f32[256,128]{1,0:T(8,128)S(1)} %get-tuple-element.14), channel_id=1, source_target_pairs={{0,16},{16,0},{32,48},{48,32},{64,80},{80,64},{96,112},{112,96},{1... | collective-permute-start | bytes 393224 | tf_op jit(solution)/shard_map/ppermute | solution.py:522
  40.6 0.0 collective-permute-done.4.a.af
  40.6 2.7 %collective-permute-done.5.c.bf = f32[424,128]{1,0:T(8,128)S(1)} collective-permute-done((f32[424,128]{1,0:T(8,128)S(1)}, f32[424,128]{1,0:T(8,128)S(1)}, u32[]{:S(2)}, u32[]{:S(2)}) %collective-permute-start.5) | collective-permute-done | bytes 217120 | tf_op jit(solution)/shard_map/ppermute | solution.py:527
  43.3 0.1 shard_map.162
  43.4 1.8 %all-gather.1 = f32[48,128]{1,0:T(8,128)S(1)} all-gather(f32[24,128]{1,0:T(8,128)S(1)} %shard_map.162), channel_id=3, replica_groups={{0,16},{32,48},{64,80},{96,112},{128,144},{160,176},{192,208},{224,240}..., dimensions={0}, use_global_device_ids=true | all-gather | bytes 36864 | tf_op jit(solution)/shard_map/all_gather | solution.py:529
  45.3 0.0 collective-permute-done.2.an
  45.3 0.0 collective-permute-done.3.am
  45.3 6.4 %shard_map.163 = (f32[3,8,16,128]{3,2,1,0:T(8,128)}, f32[3,4,8,128]{3,2,1,0:T(8,128)}) custom-call(f32[3,8,16,128]{3,2,1,0:T(8,128)} %fn.5, f32[3,8,16,128]{3,2,1,0:T(8,128)} %fp.5, f32[8,16,128]{2,1,0:T(8,128)} %fj.5, f32[3,8,16,128]{3,2,1,0:T(8,128)S(1)} %get-tuple-element.10.fo, f32[3,4,8,128]{3,2,1,0:T(8,128)} %cn.5, f32[3,4,8,128]{3,2,1,0:T(8,128)} %cp.5, ...), custom_call_target="tpu_custom_call" | custom-call | tf_op jit(solution)/shard_map/pallas_call | solution.py:480
  (1 shorter events, 0.0 us)
Async XLA Ops:
  3.9 20.9 %collective-permute-start.1 = (f32[344,128]{1,0:T(8,128)S(1)}, f32[344,128]{1,0:T(8,128)S(1)}, u32[]{:S(2)}, u32[]{:S(2)}) collective-permute-start(f32[344,128]{1,0:T(8,128)S(1)} %get-tuple-element.13), channel_id=1, source_target_pairs={{1,2},{2,1},{3,4},{4,3},{5,6},{6,5},{7,8},{8,7},{9,10},{10,9},{11,... | collective-permute-start | bytes 528392 | tf_op jit(solution)/shard_map/ppermute | solution.py:520
  18.0 6.8 %collective-permute-start = (f32[336,128]{1,0:T(8,128)S(1)}, f32[336,128]{1,0:T(8,128)S(1)}, u32[]{:S(2)}, u32[]{:S(2)}) collective-permute-start(f32[336,128]{1,0:T(8,128)S(1)} %get-tuple-element.12), channel_id=1, source_target_pairs={{0,1},{1,0},{2,3},{3,2},{4,5},{5,4},{6,7},{7,6},{8,9},{9,8},{10,11... | collective-permute-start | bytes 516104 | tf_op jit(solution)/shard_map/ppermute | solution.py:521
  19.9 20.7 %collective-permute-start.4 = (f32[664,128]{1,0:T(8,128)S(1)}, f32[664,128]{1,0:T(8,128)S(1)}, u32[]{:S(2)}, u32[]{:S(2)}) collective-permute-start(f32[664,128]{1,0:T(8,128)S(1)} %get-tuple-element.16), channel_id=1, source_target_pairs={{16,32},{32,16},{48,64},{64,48},{80,96},{96,80},{112,128},{128,112... | collective-permute-start | bytes 1019912 | tf_op jit(solution)/shard_map/ppermute | solution.py:512
  28.5 14.9 %collective-permute-start.5 = (f32[424,128]{1,0:T(8,128)S(1)}, f32[424,128]{1,0:T(8,128)S(1)}, u32[]{:S(2)}, u32[]{:S(2)}) collective-permute-start(f32[424,128]{1,0:T(8,128)S(1)} %shard_map.161), channel_id=1, source_target_pairs={{16,32},{32,16},{48,64},{64,48},{80,96},{96,80},{112,128},{128,112... | collective-permute-start | bytes 651272 | tf_op jit(solution)/shard_map/ppermute | solution.py:527
  36.3 9.0 %collective-permute-start.3 = (f32[408,128]{1,0:T(8,128)S(1)}, f32[408,128]{1,0:T(8,128)S(1)}, u32[]{:S(2)}, u32[]{:S(2)}) collective-permute-start(f32[408,128]{1,0:T(8,128)S(1)} %get-tuple-element.15), channel_id=1, source_target_pairs={{0,16},{16,0},{32,48},{48,32},{64,80},{80,64},{96,112},{112,96},{1... | collective-permute-start | bytes 626696 | tf_op jit(solution)/shard_map/ppermute | solution.py:523
  38.2 7.0 %collective-permute-start.2 = (f32[256,128]{1,0:T(8,128)S(1)}, f32[256,128]{1,0:T(8,128)S(1)}, u32[]{:S(2)}, u32[]{:S(2)}) collective-permute-start(f32[256,128]{1,0:T(8,128)S(1)} %get-tuple-element.14), channel_id=1, source_target_pairs={{0,16},{16,0},{32,48},{48,32},{64,80},{80,64},{96,112},{112,96},{1... | collective-permute-start | bytes 393224 | tf_op jit(solution)/shard_map/ppermute | solution.py:522

commit v4 on v3

--- a/solution.py
+++ b/solution.py
@@ -91,24 +91,10 @@
     out[YT:Y_ROWS] = tops_of([stage[k * 8 : k * 8 + 8] for k in range(9)])
 
 
-def pack_y(fn, fp, fj, fo, cn, cp, cj, co, yf, yn, ro, stage):
-    oy = odd("gy")
-
-    @pl.when(oy == 0)
-    def _():
-        y_edge(yf, stage, True, fn, fp, fj, fo, cn, cp, cj, co)
-        y_edge(yn, stage, False, fn, fp, fj, fo, cn, cp, cj, co)
-
-    @pl.when(oy == 1)
-    def _():
-        y_edge(yf, stage, False, fn, fp, fj, fo, cn, cp, cj, co)
-        y_edge(yn, stage, True, fn, fp, fj, fo, cn, cp, cj, co)
-    yf[Y_ROWS:] = jnp.zeros((8, NL), F32)
-    x0 = 2 - 2 * odd("gx")
-    ro[...] = tops_of([cn[i, x0 + x] if i < 3 else cj[x0 + x] * (1.0 / 12.0) for i in range(4) for x in range(2)])
-
-
-def pack_x(fn, fp, fr, fm, fl, fj, cn, cp, cr, cm, cl, cj, ix, wt, an, am, af, fo, co):
+def pack_y(
+    fn, fp, fr, fm, fl, fj, cn, cp, cr, cm, cl, cj, ix, wt,
+    fe, fb, ce, cb, yf, yn, ro, stage, fo, co,
+):
     inv = DT2 / fr[...]
     fo[0] = fm[...] * inv
     fo[1] = (fl[...] + fm[...]) * inv
@@ -123,26 +109,56 @@
     for k in range(16):
         acc = acc + jnp.where(lane == slot[:, k : k + 1], weight[:, k : k + 1], 0.0)
     fo[2] = acc.reshape(8, 16, NL)
-
+    oy = odd("gy")
+
+    @pl.when(oy == 0)
+    def _():
+        y_edge(yf, stage, True, fn, fp, fj, fo, cn, cp, cj, co)
+        y_edge(yn, stage, False, fn, fp, fj, fo, cn, cp, cj, co)
+
+    @pl.when(oy == 1)
+    def _():
+        y_edge(yf, stage, False, fn, fp, fj, fo, cn, cp, cj, co)
+        y_edge(yn, stage, True, fn, fp, fj, fo, cn, cp, cj, co)
+
+    yf[Y_ROWS:] = jnp.zeros((8, NL), F32)
+    x0 = 2 - 2 * odd("gx")
+    ro[...] = tops_of([cn[i, x0 + x] if i < 3 else cj[x0 + x] * (1.0 / 12.0) for i in range(4) for x in range(2)])
+    for half in (slice(0, 8), slice(16, 24)):
+        ce[:, :, half] = jnp.zeros((4, 16, 8, NL), F32)
+        cb[:, :, half] = jnp.zeros((5, 12, 8, NL), F32)
+        fb[:, :, half] = jnp.zeros((6, 12, 8, NL), F32)
+    for x in range(8):
+        for i in range(3):
+            fe[i, 4 + x, 4:20] = fn[i, x]
+            fb[i, 2 + x, 4:20] = fp[i, x]
+            fb[3 + i, 2 + x, 4:20] = fo[i, x]
+        fe[3, 4 + x, 4:20] = fj[x] * (1.0 / 12.0)
+    for x in range(4):
+        for i in range(3):
+            ce[i, 6 + x, 8:16] = cn[i, x]
+            cb[i, 4 + x, 8:16] = cp[i, x]
+        for i in range(2):
+            cb[3 + i, 4 + x, 8:16] = co[i, x]
+        ce[3, 6 + x, 8:16] = cj[x] * (1.0 / 12.0)
+
+
+def pack_x(fe, fb, ce, cb, an, am, af):
     near = Joined(an, am)
 
     def x_edge(out, low):
-        x0 = 0 if low else 4
+        x0 = 4 if low else 8
         for i in range(4):
-            v = fn[i, x0 : x0 + 4] if i < 3 else fj[x0 : x0 + 4] * (1.0 / 12.0)
-            out[i * 64 : i * 64 + 64] = rows(v)
-        x0 = 0 if low else 6
+            out[i * 64 : i * 64 + 64] = rows(fe[i, x0 : x0 + 4, 4:20])
+        x0 = 2 if low else 8
         for i in range(6):
-            v = fp[i, x0 : x0 + 2] if i < 3 else fo[i - 3, x0 : x0 + 2]
-            out[AB + i * 32 : AB + i * 32 + 32] = rows(v)
+            out[AB + i * 32 : AB + i * 32 + 32] = rows(fb[i, x0 : x0 + 2, 4:20])
         for i in range(4):
-            v = cn[i] if i < 3 else cj[...] * (1.0 / 12.0)
-            out[AC + i * 32 : AC + i * 32 + 32] = rows(v)
-        x0, x1 = (0, 2) if low else (2, 0)
+            out[AC + i * 32 : AC + i * 32 + 32] = rows(ce[i, 6:10, 8:16])
+        x0, x1 = (4, 6) if low else (6, 4)
         for i in range(5):
-            v = cp[i, x0 : x0 + 2] if i < 3 else co[i - 3, x0 : x0 + 2]
-            out[AD + i * 16 : AD + i * 16 + 16] = rows(v)
-        out[AT:A_ROWS] = tops_of([cp[i, x1 + x] if i < 3 else co[i - 3, x1 + x] for i in range(5) for x in range(2)])
+            out[AD + i * 16 : AD + i * 16 + 16] = rows(cb[i, x0 : x0 + 2, 8:16])
+        out[AT:A_ROWS] = tops_of([cb[i, x1 + x, 8:16] for i in range(5) for x in range(2)])
 
     ox = odd("gx")
 
@@ -273,124 +289,137 @@
             store(c, x, 2.0 * col[c][2] - prev(c, x) + av * lap + bv * g)
 
 
+def bases(high):
+    return (
+        jnp.where(high, 12, 0), jnp.where(high, 10, 0), jnp.where(high, 10, 2), jnp.where(high, 14, 0),
+        jnp.where(high, 8, 0), jnp.where(high, 8, 2), jnp.where(high, 10, 0),
+    )
+
+
+def y_places(high):
+    return (20, 20, 16, 20, 16, 18) if high else (0, 2, 4, 2, 6, 4)
+
+
+def unpack_y(src, high, fe, fb, ce, cb):
+    t4, t2, k4, k2, k1, k3 = y_places(high)
+    top = src[YT:Y_ROWS]
+    for i in range(4):
+        for x in range(8):
+            fe[i, 4 + x, t4 : t4 + 4] = src[i * 32 + x * 4 : i * 32 + x * 4 + 4]
+        v = top_of(top, i)
+        for x in range(4):
+            o = YC + i * 16 + x * 4
+            ce[i, 6 + x, k4 : k4 + 4] = src[o : o + 4]
+            ce[i, 6 + x, k2 : k2 + 2] = v[x * 2 : x * 2 + 2]
+    for i in range(6):
+        for x in range(8):
+            o = YB + i * 16 + x * 2
+            fb[i, 2 + x, t2 : t2 + 2] = src[o : o + 2]
+    for i in range(5):
+        v = top_of(top, 4 + i)
+        for x in range(4):
+            o = YD + i * 8 + x * 2
+            cb[i, 4 + x, k1 : k1 + 2] = src[o : o + 2]
+            cb[i, 4 + x, k3 : k3 + 2] = v[x * 2 : x * 2 + 2]
+
+
+def unpack_corner(c, s, hx, high, fe, fb, ce, cb):
+    t4, t2, k4, k2, k1, k3 = y_places(high)
+    f4, f2, c4, _, b4, _, _ = bases(hx)
+    q = s * CS
+    top = c[q + CT : q + CS]
+    for i in range(4):
+        v = top_of(top, i)
+        for x in range(4):
+            o = q + i * 16 + x * 4
+            fe[i, f4 + x, t4 : t4 + 4] = c[o : o + 4]
+            o = q + CC + i * 16 + x * 4
+            ce[i, c4 + x, k4 : k4 + 4] = c[o : o + 4]
+            ce[i, c4 + x, k2 : k2 + 2] = v[x * 2 : x * 2 + 2]
+    for i in range(6):
+        for x in range(2):
+            o = q + CB_ + i * 4 + x * 2
+            fb[i, f2 + x, t2 : t2 + 2] = c[o : o + 2]
+    for i in range(5):
+        v = top_of(top, 4 + i)
+        for x in range(4):
+            o = q + CD + i * 8 + x * 2
+            cb[i, b4 + x, k1 : k1 + 2] = c[o : o + 2]
+            cb[i, b4 + x, k3 : k3 + 2] = v[x * 2 : x * 2 + 2]
+
+
+def unpack_x(a, hx, fe, fb, ce, cb):
+    f4, f2, c4, _, _, b2, b4 = bases(hx)
+    top = a[AT:A_ROWS]
+    for i in range(4):
+        for x in range(4):
+            fe[i, f4 + x, 4:20] = a[i * 64 + x * 16 : i * 64 + x * 16 + 16]
+            ce[i, c4 + x, 8:16] = a[AC + i * 32 + x * 8 : AC + i * 32 + x * 8 + 8]
+    for i in range(6):
+        for x in range(2):
+            fb[i, f2 + x, 4:20] = a[AB + i * 32 + x * 16 : AB + i * 32 + x * 16 + 16]
+    for i in range(5):
+        for x in range(2):
+            cb[i, b2 + x, 8:16] = a[AD + i * 16 + x * 8 : AD + i * 16 + x * 8 + 8]
+            cb[i, b4 + x, 8:16] = top_of(top, i * 2 + x)
+
+
+def unpack_relay(r, base, hx, near_high, ce):
+    c2 = bases(hx)[3]
+    beyond = r[base : base + 8]
+    for i in range(4):
+        for x in range(2):
+            ce[i, c2 + x, 8:16] = top_of(beyond, i * 2 + x)
+        for s, high in ((0, near_high), (1, not near_high)):
+            _, _, k4, k2, _, _ = y_places(high)
+            v = top_of(beyond, 8 + s * 4 + i)
+            w = top_of(r[base + 8 + s * 8 : base + 16 + s * 8], i)
+            w = jnp.where(hx, w, pltpu.roll(w, 4, 0))
+            for x in range(2):
+                ce[i, c2 + x, k4 : k4 + 4] = v[x * 4 : x * 4 + 4]
+                ce[i, c2 + x, k2 : k2 + 2] = w[x * 2 : x * 2 + 2]
+
+
+def fill(_, __, ___, ____, yn, yf, gn, _____, fe, fb, ce, cb):
+    ox, oy = odd("gx"), odd("gy")
+    c, hx = gn.at[1 - ox], ox == 0
+
+    def sides(near_high):
+        for s, src, high in ((0, yn, near_high), (1, yf, not near_high)):
+            unpack_y(src, high, fe, fb, ce, cb)
+            unpack_corner(c, s, hx, high, fe, fb, ce, cb)
+
+    @pl.when(oy == 0)
+    def _():
+        sides(True)
+
+    @pl.when(oy == 1)
+    def _():
+        sides(False)
+
+
 def main(
-    fn, fp, fj, fo, cn, cp, cj, co, yn, yf, an, am, af, gn, bf, g2, table_ref,
+    _, __, ___, ____, an, am, af, bf, g2, table_ref,
     fine_out, coarse_out, fe, fb, ce, cb, f1, c1, lift, work, tops, face,
 ):
     ox, oy = odd("gx"), odd("gy")
-    ce[:, :, 0:8] = jnp.zeros((4, 16, 8, NL), F32)
-    ce[:, :, 16:24] = jnp.zeros((4, 16, 8, NL), F32)
-    cb[:, :, 0:8] = jnp.zeros((5, 12, 8, NL), F32)
-    cb[:, :, 16:24] = jnp.zeros((5, 12, 8, NL), F32)
-    fb[:, :, 0:8] = jnp.zeros((6, 12, 8, NL), F32)
-    fb[:, :, 16:24] = jnp.zeros((6, 12, 8, NL), F32)
-    for x in range(8):
-        for i in range(3):
-            fe[i, 4 + x, 4:20] = fn[i, x]
-            fb[i, 2 + x, 4:20] = fp[i, x]
-            fb[3 + i, 2 + x, 4:20] = fo[i, x]
-        fe[3, 4 + x, 4:20] = fj[x] * (1.0 / 12.0)
-    for x in range(4):
-        for i in range(3):
-            ce[i, 6 + x, 8:16] = cn[i, x]
-            cb[i, 4 + x, 8:16] = cp[i, x]
-        for i in range(2):
-            cb[3 + i, 4 + x, 8:16] = co[i, x]
-        ce[3, 6 + x, 8:16] = cj[x] * (1.0 / 12.0)
     near, far = ox == 0, ox == 1
-    other = 1 - ox
-    sides = (
-        (Joined(an, am), gn.at[other], g2.at[other], near, 0),
-        (af, bf, bf, far, C_ROWS),
-    )
-    for a, c, r, high, base in sides:
-        f4 = jnp.where(high, 12, 0)
-        f2 = jnp.where(high, 10, 0)
-        c4 = jnp.where(high, 10, 2)
-        c2 = jnp.where(high, 14, 0)
-        b2 = jnp.where(high, 8, 2)
-        b4 = jnp.where(high, 10, 0)
-        own, top = r[base : base + 8], a[AT:A_ROWS]
-        for i in range(4):
-            for x in range(4):
-                fe[i, f4 + x, 4:20] = a[i * 64 + x * 16 : i * 64 + x * 16 + 16]
-                ce[i, c4 + x, 8:16] = a[AC + i * 32 + x * 8 : AC + i * 32 + x * 8 + 8]
-            for x in range(2):
-                ce[i, c2 + x, 8:16] = top_of(own, i * 2 + x)
-        for i in range(6):
-            for x in range(2):
-                fb[i, f2 + x, 4:20] = a[AB + i * 32 + x * 16 : AB + i * 32 + x * 16 + 16]
-        for i in range(5):
-            for x in range(2):
-                cb[i, b2 + x, 8:16] = a[AD + i * 16 + x * 8 : AD + i * 16 + x * 8 + 8]
-                cb[i, b4 + x, 8:16] = top_of(top, i * 2 + x)
-
-    def y_side(src, s, high):
-        t4, t2 = (20, 20) if high else (0, 2)
-        k4, k2, k1, k3 = (16, 20, 16, 18) if high else (4, 2, 6, 4)
-        top = src[YT:Y_ROWS]
-        for i in range(4):
-            for x in range(8):
-                fe[i, 4 + x, t4 : t4 + 4] = src[i * 32 + x * 4 : i * 32 + x * 4 + 4]
-            v = top_of(top, i)
-            for x in range(4):
-                o = YC + i * 16 + x * 4
-                ce[i, 6 + x, k4 : k4 + 4] = src[o : o + 4]
-                ce[i, 6 + x, k2 : k2 + 2] = v[x * 2 : x * 2 + 2]
-        for i in range(6):
-            for x in range(8):
-                o = YB + i * 16 + x * 2
-                fb[i, 2 + x, t2 : t2 + 2] = src[o : o + 2]
-        for i in range(5):
-            v = top_of(top, 4 + i)
-            for x in range(4):
-                o = YD + i * 8 + x * 2
-                cb[i, 4 + x, k1 : k1 + 2] = src[o : o + 2]
-                cb[i, 4 + x, k3 : k3 + 2] = v[x * 2 : x * 2 + 2]
-        for a, c, r, hx, base in sides:
-            f4 = jnp.where(hx, 12, 0)
-            f2 = jnp.where(hx, 10, 0)
-            c4 = jnp.where(hx, 10, 2)
-            c2 = jnp.where(hx, 14, 0)
-            b4 = jnp.where(hx, 8, 0)
-            q = s * CS
-            top = c[q + CT : q + CS]
-            beyond = r[base : base + 8]
-            beyond_top = r[base + 8 + s * 8 : base + 16 + s * 8]
-            for i in range(4):
-                v = top_of(top, i)
-                for x in range(4):
-                    o = q + i * 16 + x * 4
-                    fe[i, f4 + x, t4 : t4 + 4] = c[o : o + 4]
-                    o = q + CC + i * 16 + x * 4
-                    ce[i, c4 + x, k4 : k4 + 4] = c[o : o + 4]
-                    ce[i, c4 + x, k2 : k2 + 2] = v[x * 2 : x * 2 + 2]
-                v = top_of(beyond, 8 + s * 4 + i)
-                w = top_of(beyond_top, i)
-                w = jnp.where(hx, w, pltpu.roll(w, 4, 0))
-                for x in range(2):
-                    ce[i, c2 + x, k4 : k4 + 4] = v[x * 4 : x * 4 + 4]
-                    ce[i, c2 + x, k2 : k2 + 2] = w[x * 2 : x * 2 + 2]
-            for i in range(6):
-                for x in range(2):
-                    o = q + CB_ + i * 4 + x * 2
-                    fb[i, f2 + x, t2 : t2 + 2] = c[o : o + 2]
-            for i in range(5):
-                v = top_of(top, 4 + i)
-                for x in range(4):
-                    o = q + CD + i * 8 + x * 2
-                    cb[i, b4 + x, k1 : k1 + 2] = c[o : o + 2]
-                    cb[i, b4 + x, k3 : k3 + 2] = v[x * 2 : x * 2 + 2]
+    unpack_x(Joined(an, am), near, fe, fb, ce, cb)
+    unpack_x(af, far, fe, fb, ce, cb)
+
+    def sides(near_high):
+        for s, high in ((0, near_high), (1, not near_high)):
+            unpack_corner(bf, s, far, high, fe, fb, ce, cb)
+        unpack_relay(bf, C_ROWS, far, near_high, ce)
+        unpack_relay(g2.at[1 - ox], 0, near, near_high, ce)
 
     @pl.when(oy == 0)
     def _():
-        y_side(yn, 0, True)
-        y_side(yf, 1, False)
+        sides(True)
 
     @pl.when(oy == 1)
     def _():
-        y_side(yn, 0, False)
-        y_side(yf, 1, True)
+        sides(False)
 
     table = table_ref[...]
     lane = lax.broadcasted_iota(jnp.int32, (24, NL), 1)
@@ -475,14 +504,16 @@
 INTERPRET = False
 
 
-def call(body, shapes, *operands, scratch=(), local=True):
+def call(body, shapes, *operands, scratch=(), local=True, alias={}):
     vmem = pl.BlockSpec(memory_space=pltpu.VMEM)
+    away = 0 if local else 2
     return pl.pallas_call(
         body,
-        out_shape=[pltpu.VMEM(s, F32) if local else jax.ShapeDtypeStruct(s, F32) for s in shapes],
+        out_shape=[jax.ShapeDtypeStruct(s, F32) if k < away else pltpu.VMEM(s, F32) for k, s in enumerate(shapes)],
         in_specs=[vmem] * len(operands),
         out_specs=[vmem] * len(shapes),
         scratch_shapes=[pltpu.VMEM(s, F32) for s in scratch],
+        input_output_aliases=alias,
         compiler_params=pltpu.CompilerParams(vmem_limit_bytes=56 << 20),
         interpret=INTERPRET,
     )(*operands)
@@ -501,44 +532,42 @@
     groups = [[i, i + 1] for i in range(0, gx, 2)]
     table = jnp.asarray(vertical_matrix(), jnp.bfloat16)
 
-    an, am, af, fo, co = call(
-        pack_x,
-        [(AB, NL), (A_ROWS - AB, NL), (A_ROWS, NL)] + [(3, 8, 16, NL), (2, 4, 8, NL)],
+    blocks = [(4, 16, 24, NL), (6, 12, 24, NL), (4, 16, 24, NL), (5, 12, 24, NL)]
+    *wide, yf, yn, ro = call(
+        pack_y,
+        blocks + [(Y_ROWS + 8, NL), (Y_ROWS, NL), (O_ROWS, NL)],
         fine_now, fine_prev, fine_rho, fine_mu, fine_lam, fine_metric,
         coarse_now, coarse_prev, coarse_rho, coarse_mu, coarse_lam, coarse_metric,
         couple_index, couple_weight,
+        scratch=[(72, NL), (3, 8, 16, NL), (2, 4, 8, NL)],
     )
-    fo, co = keep(fo), keep(co)
-    af = keep(lax.ppermute(af, "gx", far_x))
-    yf, yn, ro = call(
-        pack_y,
-        [(Y_ROWS + 8, NL), (Y_ROWS, NL), (O_ROWS, NL)],
-        fine_now, fine_prev, fine_metric, fo, coarse_now, coarse_prev, coarse_metric, co,
-        scratch=[(72, NL)],
-    )
-    ro = keep(ro)
+    wide, ro = [keep(w) for w in wide], keep(ro)
     yf = keep(lax.ppermute(yf, "gy", far_y))
     yn = keep(lax.ppermute(yn, "gy", near_y))
+    an, am, af = call(pack_x, [(AB, NL), (A_ROWS - AB, NL), (A_ROWS, NL)], *wide)
+    af = keep(lax.ppermute(af, "gx", far_x))
     an = keep(lax.ppermute(an, "gx", near_x))
     am = keep(lax.ppermute(am, "gx", near_x))
     (cn,) = call(pack_near, [(C_ROWS + O_ROWS, NL)], yn, yf, ro)
     gn = keep(lax.all_gather(cn, "gx", axis_index_groups=groups))
-    (bf,) = call(pack_far, [(C_ROWS + R_ROWS, NL)], yn, yf, gn)
-    bf = keep(lax.ppermute(bf, "gx", far_x))
+    (bp,) = call(pack_far, [(C_ROWS + R_ROWS, NL)], yn, yf, gn)
+    bp = keep(bp)
+    bf = keep(lax.ppermute(bp, "gx", far_x))
+    wide = call(fill, blocks, *wide, yn, yf, gn, bp, alias={0: 0, 1: 1, 2: 2, 3: 3})
+    wide = [keep(w) for w in wide]
     (r2,) = call(pack_second, [(R_ROWS, NL)], af, bf)
     g2 = keep(lax.all_gather(r2, "gx", axis_index_groups=groups))
     return tuple(
         call(
             main,
-            [(3, 8, 16, NL), (3, 4, 8, NL)],
-            fine_now, fine_prev, fine_metric, fo, coarse_now, coarse_prev, coarse_metric, co,
-            yn, yf, an, am, af, gn, bf, g2, table,
+            [(3, 8, 16, NL), (3, 4, 8, NL)] + blocks,
+            *wide, an, am, af, bf, g2, table,
             local=False,
+            alias={0: 2, 1: 3, 2: 4, 3: 5},
             scratch=[
-                (4, 16, 24, NL), (6, 12, 24, NL), (4, 16, 24, NL), (5, 12, 24, NL),
                 (3, 12, 24, NL), (3, 12, 24, NL), (16, 24, NL), (4, 12, 24, NL), (16, 16, NL), (12, 24, NL),
             ],
-        )
+        )[:2]
     )
 
 

time: 51.9 us -> 50.4 us (0.971)
  Pallas kernels: 9.79 us -> 8.53 us
    pallas_call x6 -> x7, Pallas kernels: 9.79 us -> 8.53 us  [call(): pl.pallas_call(body, out_shape=[jax.ShapeDtypeStruct(s, F32) if k < away...]
  transfers between devices with their start and end apart: 6 -> 6, of which waited for: 2 -> 2; matrix products, arithmetic and copies ran while one was open for 0% -> 0% of each run, Pallas kernels for 0% -> 1%
where the time goes in v4:
time: 50.4 us; the launch traced here: 50 us
  starting transfers between devices  32 us (63%)
  Pallas kernels  8.53 us (17%)
  blocking collectives  5.43 us (11%)
  waiting for transfers between devices  3.36 us (7%)
  between operations  0.72 us (1%)
    ppermute x1, starting transfers between devices, on_device(): yf = keep(lax.ppermute(yf, 'gy', far_y))  14 us
    pallas_call x7, Pallas kernels, call(): pl.pallas_call(body, out_shape=[jax.ShapeDtypeStruct(s, F32) if k < away...  8.53 us
    ppermute x1, starting transfers between devices, on_device(): bf = keep(lax.ppermute(bp, 'gx', far_x))  7.78 us
    ppermute x1, starting transfers between devices, on_device(): af = keep(lax.ppermute(af, 'gx', far_x))  3.94 us
    all_gather x1, blocking collectives, on_device(): gn = keep(lax.all_gather(cn, 'gx', axis_index_groups=groups))  3.6 us
    ppermute x1, waiting for transfers between devices, on_device(): bf = keep(lax.ppermute(bp, 'gx', far_x))  2.52 us
    ppermute x1, starting transfers between devices, on_device(): an = keep(lax.ppermute(an, 'gx', near_x))  2.41 us
    ppermute x1, starting transfers between devices, on_device(): yn = keep(lax.ppermute(yn, 'gy', near_y))  1.92 us
  transfers between devices with their start and end apart: 6, of which 2 were waited for; matrix products, arithmetic and copies ran while one was open for 0% of the time, Pallas kernels for 1%

profile of v4, /device:TPU:57, one launch (start us, length us, event | category | flops | bytes accessed | tf_op | source)
XLA Modules:
  0.0 50.0 jit_solution(11169346369165967015)
XLA Ops:
  0.6 2.2 %shard_map.158 = (f32[4,16,24,128]{3,2,1,0:T(8,128)S(1)}, f32[6,12,24,128]{3,2,1,0:T(8,128)S(1)}, f32[4,16,24,128]{3,2,1,0:T(8,128)S(1)}, f32[5,12,24,128]{3,2,1...) custom-call(f32[3,8,16,128]{3,2,1,0:T(8,128)} %fn.1, f32[3,8,16,128]{3,2,1,0:T(8,128)} %fp.1, ...), custom_call_target="tpu_custom_call" | custom-call | tf_op jit(solution)/shard_map/pallas_call | solution.py:510
  2.9 14.0 %collective-permute-start.1 = (f32[344,128]{1,0:T(8,128)S(1)}, f32[344,128]{1,0:T(8,128)S(1)}, u32[]{:S(2)}, u32[]{:S(2)}) collective-permute-start(f32[344,128]{1,0:T(8,128)S(1)} %get-tuple-element.23), channel_id=1, source_target_pairs={{1,2},{2,1},{3,4},{4,3},{5,6},{6,5},{7,8},{8,7},{9,10},{10,9},{11,... | collective-permute-start | bytes 528392 | tf_op jit(solution)/shard_map/ppermute | solution.py:545
  16.9 1.9 %collective-permute-start = (f32[336,128]{1,0:T(8,128)S(1)}, f32[336,128]{1,0:T(8,128)S(1)}, u32[]{:S(2)}, u32[]{:S(2)}) collective-permute-start(f32[336,128]{1,0:T(8,128)S(1)} %get-tuple-element.22), channel_id=1, source_target_pairs={{0,1},{1,0},{2,3},{3,2},{4,5},{5,4},{6,7},{7,6},{8,9},{9,8},{10,11... | collective-permute-start | bytes 516104 | tf_op jit(solution)/shard_map/ppermute | solution.py:546
  18.8 0.1 shard_map.162
  18.9 3.9 %collective-permute-start.4 = (f32[664,128]{1,0:T(8,128)S(1)}, f32[664,128]{1,0:T(8,128)S(1)}, u32[]{:S(2)}, u32[]{:S(2)}) collective-permute-start(f32[664,128]{1,0:T(8,128)S(1)} %get-tuple-element.31), channel_id=1, source_target_pairs={{16,32},{32,16},{48,64},{64,48},{80,96},{96,80},{112,128},{128,112... | collective-permute-start | bytes 1019912 | tf_op jit(solution)/shard_map/ppermute | solution.py:548
  22.9 0.8 %collective-permute-done.rn.yn = f32[336,128]{1,0:T(8,128)S(1)} collective-permute-done((f32[336,128]{1,0:T(8,128)S(1)}, f32[336,128]{1,0:T(8,128)S(1)}, u32[]{:S(2)}, u32[]{:S(2)}) %collective-permute-start) | collective-permute-done | bytes 172064 | tf_op jit(solution)/shard_map/ppermute | solution.py:546
  23.7 0.0 collective-permute-done.1.rf.yf
  23.7 3.6 %all-gather = f32[816,128]{1,0:T(8,128)S(1)} all-gather(f32[408,128]{1,0:T(8,128)S(1)} %shard_map.159), channel_id=2, replica_groups={{0,16},{32,48},{64,80},{96,112},{128,144},{160,176},{192,208},{224,240}..., dimensions={0}, use_global_device_ids=true | all-gather | bytes 626688 | tf_op jit(solution)/shard_map/all_gather | solution.py:552
  27.3 0.1 shard_map.160._____
  27.4 7.8 %collective-permute-start.5 = (f32[424,128]{1,0:T(8,128)S(1)}, f32[424,128]{1,0:T(8,128)S(1)}, u32[]{:S(2)}, u32[]{:S(2)}) collective-permute-start(f32[424,128]{1,0:T(8,128)S(1)} %shard_map.160._____), channel_id=1, source_target_pairs={{16,32},{32,16},{48,64},{64,48},{80,96},{96,80},{112,128},{128,112... | collective-permute-start | bytes 651272 | tf_op jit(solution)/shard_map/ppermute | solution.py:555
  35.2 1.9 %collective-permute-start.3 = (f32[408,128]{1,0:T(8,128)S(1)}, f32[408,128]{1,0:T(8,128)S(1)}, u32[]{:S(2)}, u32[]{:S(2)}) collective-permute-start(f32[408,128]{1,0:T(8,128)S(1)} %get-tuple-element.30), channel_id=1, source_target_pairs={{0,16},{16,0},{32,48},{48,32},{64,80},{80,64},{96,112},{112,96},{1... | collective-permute-start | bytes 626696 | tf_op jit(solution)/shard_map/ppermute | solution.py:550
  37.1 2.4 %collective-permute-start.2 = (f32[256,128]{1,0:T(8,128)S(1)}, f32[256,128]{1,0:T(8,128)S(1)}, u32[]{:S(2)}, u32[]{:S(2)}) collective-permute-start(f32[256,128]{1,0:T(8,128)S(1)} %get-tuple-element.29), channel_id=1, source_target_pairs={{0,16},{16,0},{32,48},{48,32},{64,80},{80,64},{96,112},{112,96},{1... | collective-permute-start | bytes 393224 | tf_op jit(solution)/shard_map/ppermute | solution.py:549
  39.6 0.2 shard_map.161
  39.7 0.0 collective-permute-done.4.a.af
  39.8 2.5 %collective-permute-done.5.c.bf = f32[424,128]{1,0:T(8,128)S(1)} collective-permute-done((f32[424,128]{1,0:T(8,128)S(1)}, f32[424,128]{1,0:T(8,128)S(1)}, u32[]{:S(2)}, u32[]{:S(2)}) %collective-permute-start.5) | collective-permute-done | bytes 217120 | tf_op jit(solution)/shard_map/ppermute | solution.py:555
  42.3 0.1 shard_map.163
  42.4 1.8 %all-gather.1 = f32[48,128]{1,0:T(8,128)S(1)} all-gather(f32[24,128]{1,0:T(8,128)S(1)} %shard_map.163), channel_id=3, replica_groups={{0,16},{32,48},{64,80},{96,112},{128,144},{160,176},{192,208},{224,240}..., dimensions={0}, use_global_device_ids=true | all-gather | bytes 36864 | tf_op jit(solution)/shard_map/all_gather | solution.py:559
  44.2 0.0 collective-permute-done.2.an
  44.2 0.0 collective-permute-done.3.am
  44.2 5.9 %shard_map.164 = (f32[3,8,16,128]{3,2,1,0:T(8,128)}, f32[3,4,8,128]{3,2,1,0:T(8,128)}, f32[4,16,24,128]{3,2,1,0:T(8,128)S(1)}, f32[6,12,24,128]{3,2,1,0:T(8,128)...) custom-call(f32[4,16,24,128]{3,2,1,0:T(8,128)S(1)} %get-tuple-elemen, ...), custom_call_target="tpu_custom_call", output_to_operand_aliasing={{2}: (0, {}), {3}: (1, {}), {4}: (2, {}), {5}: (3, {})} | custom-call | tf_op jit(solution)/shard_map/pallas_call | solution.py:510
  (1 shorter events, 0.0 us)
Async XLA Ops:
  2.9 20.9 %collective-permute-start.1 = (f32[344,128]{1,0:T(8,128)S(1)}, f32[344,128]{1,0:T(8,128)S(1)}, u32[]{:S(2)}, u32[]{:S(2)}) collective-permute-start(f32[344,128]{1,0:T(8,128)S(1)} %get-tuple-element.23), channel_id=1, source_target_pairs={{1,2},{2,1},{3,4},{4,3},{5,6},{6,5},{7,8},{8,7},{9,10},{10,9},{11,... | collective-permute-start | bytes 528392 | tf_op jit(solution)/shard_map/ppermute | solution.py:545
  16.9 6.8 %collective-permute-start = (f32[336,128]{1,0:T(8,128)S(1)}, f32[336,128]{1,0:T(8,128)S(1)}, u32[]{:S(2)}, u32[]{:S(2)}) collective-permute-start(f32[336,128]{1,0:T(8,128)S(1)} %get-tuple-element.22), channel_id=1, source_target_pairs={{0,1},{1,0},{2,3},{3,2},{4,5},{5,4},{6,7},{7,6},{8,9},{9,8},{10,11... | collective-permute-start | bytes 516104 | tf_op jit(solution)/shard_map/ppermute | solution.py:546
  18.9 20.8 %collective-permute-start.4 = (f32[664,128]{1,0:T(8,128)S(1)}, f32[664,128]{1,0:T(8,128)S(1)}, u32[]{:S(2)}, u32[]{:S(2)}) collective-permute-start(f32[664,128]{1,0:T(8,128)S(1)} %get-tuple-element.31), channel_id=1, source_target_pairs={{16,32},{32,16},{48,64},{64,48},{80,96},{96,80},{112,128},{128,112... | collective-permute-start | bytes 1019912 | tf_op jit(solution)/shard_map/ppermute | solution.py:548
  27.4 14.9 %collective-permute-start.5 = (f32[424,128]{1,0:T(8,128)S(1)}, f32[424,128]{1,0:T(8,128)S(1)}, u32[]{:S(2)}, u32[]{:S(2)}) collective-permute-start(f32[424,128]{1,0:T(8,128)S(1)} %shard_map.160._____), channel_id=1, source_target_pairs={{16,32},{32,16},{48,64},{64,48},{80,96},{96,80},{112,128},{128,112... | collective-permute-start | bytes 651272 | tf_op jit(solution)/shard_map/ppermute | solution.py:555
  35.2 9.0 %collective-permute-start.3 = (f32[408,128]{1,0:T(8,128)S(1)}, f32[408,128]{1,0:T(8,128)S(1)}, u32[]{:S(2)}, u32[]{:S(2)}) collective-permute-start(f32[408,128]{1,0:T(8,128)S(1)} %get-tuple-element.30), channel_id=1, source_target_pairs={{0,16},{16,0},{32,48},{48,32},{64,80},{80,64},{96,112},{112,96},{1... | collective-permute-start | bytes 626696 | tf_op jit(solution)/shard_map/ppermute | solution.py:550
  37.1 7.0 %collective-permute-start.2 = (f32[256,128]{1,0:T(8,128)S(1)}, f32[256,128]{1,0:T(8,128)S(1)}, u32[]{:S(2)}, u32[]{:S(2)}) collective-permute-start(f32[256,128]{1,0:T(8,128)S(1)} %get-tuple-element.29), channel_id=1, source_target_pairs={{0,16},{16,0},{32,48},{48,32},{64,80},{80,64},{96,112},{112,96},{1... | collective-permute-start | bytes 393224 | tf_op jit(solution)/shard_map/ppermute | solution.py:549

commit v5 on v4

--- a/solution.py
+++ b/solution.py
@@ -91,17 +91,21 @@
     out[YT:Y_ROWS] = tops_of([stage[k * 8 : k * 8 + 8] for k in range(9)])
 
 
-def pack_y(
-    fn, fp, fr, fm, fl, fj, cn, cp, cr, cm, cl, cj, ix, wt,
-    fe, fb, ce, cb, yf, yn, ro, stage, fo, co,
-):
-    inv = DT2 / fr[...]
-    fo[0] = fm[...] * inv
-    fo[1] = (fl[...] + fm[...]) * inv
-    inv = DT2 / cr[...]
-    co[0] = cm[...] * inv
-    co[1] = (cl[...] + cm[...]) * inv
+def pack_y(*refs):
+    inputs, outputs, rest = refs[:14], refs[14:21], refs[21:]
+    local, sems, (stage, fo, co) = rest[:14], rest[14], rest[15:]
+    copies = [pltpu.make_async_copy(i, v, sems.at[k]) for k, (i, v) in enumerate(zip(inputs, local))]
+    for k in PACK_ORDER:
+        copies[k].start()
+    fn, fp, fr, fm, fl, fj, cn, cp, cr, cm, cl, cj, ix, wt = local
+    fe, fb, ce, cb, yf, yn, ro = outputs
+    for half in (slice(0, 8), slice(16, 24)):
+        ce[:, :, half] = jnp.zeros((4, 16, 8, NL), F32)
+        cb[:, :, half] = jnp.zeros((5, 12, 8, NL), F32)
+        fb[:, :, half] = jnp.zeros((6, 12, 8, NL), F32)
     lane = lax.broadcasted_iota(jnp.int32, (128, NL), 1)
+    for k in PACK_ORDER[:2]:
+        copies[k].wait()
     index = ix[...].reshape(128, 16)
     weight = wt[...].reshape(128, 16)
     slot = index + 2 + 4 * ((index * 171) >> 11)
@@ -109,6 +113,14 @@
     for k in range(16):
         acc = acc + jnp.where(lane == slot[:, k : k + 1], weight[:, k : k + 1], 0.0)
     fo[2] = acc.reshape(8, 16, NL)
+    for k in PACK_ORDER[2:]:
+        copies[k].wait()
+    inv = DT2 / fr[...]
+    fo[0] = fm[...] * inv
+    fo[1] = (fl[...] + fm[...]) * inv
+    inv = DT2 / cr[...]
+    co[0] = cm[...] * inv
+    co[1] = (cl[...] + cm[...]) * inv
     oy = odd("gy")
 
     @pl.when(oy == 0)
@@ -124,10 +136,6 @@
     yf[Y_ROWS:] = jnp.zeros((8, NL), F32)
     x0 = 2 - 2 * odd("gx")
     ro[...] = tops_of([cn[i, x0 + x] if i < 3 else cj[x0 + x] * (1.0 / 12.0) for i in range(4) for x in range(2)])
-    for half in (slice(0, 8), slice(16, 24)):
-        ce[:, :, half] = jnp.zeros((4, 16, 8, NL), F32)
-        cb[:, :, half] = jnp.zeros((5, 12, 8, NL), F32)
-        fb[:, :, half] = jnp.zeros((6, 12, 8, NL), F32)
     for x in range(8):
         for i in range(3):
             fe[i, 4 + x, 4:20] = fn[i, x]
@@ -266,22 +274,28 @@
         work[c, 0:n] = (rows(j(2, n)) * g).reshape(n, 24, NL)
     for x in range(n):
         f0 = [u(0, x + k, None) for k in (0, 1, 3, 4)]
-        m2, m1, p1, p2 = shifted(u(1, x + 2, None))
-        work[3, x] = first(*f0, s1) + first(m2, m1, p1, p2, s1) + lift[x + 2]
+        t = first(*f0, s1) + lift[x + 2]
+        v = u(1, x + 2, None)
+        m2, m1, p1, p2 = shifted(v)
+        work[3, x] = t + first(m2, m1, p1, p2, s1)
+        yy1 = second(m2, m1, v, p1, p2, s2)
+        work[4, x] = yy1
+        work[5, x] = yy1 + first(*shifted(t), s1)
     work[2, 0:n] = lift[2 : 2 + n]
     for c in range(4):
         g = vertical(rows(work[c, 0:n]), table)
         work[c, 0:n] = (rows(j(2, n)) * g).reshape(n, 24, NL)
     for x in range(n):
         col = [[u(c, x + k, None) for k in range(5)] for c in range(3)]
-        lf = [lift[x + k] for k in range(5)]
-        sh = [shifted(col[c][2]) for c in range(3)]
+        lf = [lift[x + k] if k != 2 else None for k in range(5)]
+        sh = [shifted(col[c][2]) if c != 1 else None for c in range(3)]
         xx = [second(*col[c], s2) for c in range(3)]
-        yy = [second(sh[c][0], sh[c][1], col[c][2], sh[c][2], sh[c][3], s2) for c in range(3)]
-        dx0 = first(col[0][0], col[0][1], col[0][3], col[0][4], s1)
+        yy = [
+            second(sh[c][0], sh[c][1], col[c][2], sh[c][2], sh[c][3], s2) if c != 1 else work[4, x] for c in range(3)
+        ]
         dx1 = first(col[1][0], col[1][1], col[1][3], col[1][4], s1)
         g0 = xx[0] + first(*shifted(dx1), s1) + first(lf[0], lf[1], lf[3], lf[4], s1)
-        g1 = yy[1] + first(*shifted(dx0), s1) + first(*shifted(lf[2]), s1)
+        g1 = work[5, x]
         g2 = work[3, x]
         av, bv = a(x), b(x)
         for c, g in enumerate((g0, g1, g2)):
@@ -523,6 +537,38 @@
     return v if INTERPRET else pltpu.with_memory_space_constraint(v, pltpu.VMEM)
 
 
+PACK_ORDER = (12, 13, 0, 1, 5, 2, 3, 4, 6, 7, 11, 8, 9, 10)
+
+
+def pack_call(*operands):
+    blocks = [(4, 16, 24, NL), (6, 12, 24, NL), (4, 16, 24, NL), (5, 12, 24, NL)]
+    shapes = blocks + [(Y_ROWS + 8, NL), (Y_ROWS, NL), (O_ROWS, NL)]
+    return pl.pallas_call(
+        pack_y,
+        out_shape=[pltpu.VMEM(s, F32) for s in shapes],
+        in_specs=[pl.BlockSpec(memory_space=pl.ANY)] * len(operands),
+        out_specs=[pl.BlockSpec(memory_space=pltpu.VMEM)] * len(shapes),
+        scratch_shapes=[pltpu.VMEM(o.shape, o.dtype) for o in operands]
+        + [pltpu.SemaphoreType.DMA((len(operands),))]
+        + [pltpu.VMEM(s, F32) for s in ((72, NL), (3, 8, 16, NL), (2, 4, 8, NL))],
+        compiler_params=pltpu.CompilerParams(vmem_limit_bytes=56 << 20),
+        interpret=INTERPRET,
+    )(*operands)
+
+
+def main_call(*operands):
+    blocks = [(4, 16, 24, NL), (6, 12, 24, NL), (4, 16, 24, NL), (5, 12, 24, NL)]
+    return call(
+        main,
+        [(3, 8, 16, NL), (3, 4, 8, NL)] + blocks,
+        *operands,
+        keep(jnp.asarray(vertical_matrix(), jnp.bfloat16)),
+        local=False,
+        alias={0: 2, 1: 3, 2: 4, 3: 5},
+        scratch=[(3, 12, 24, NL), (3, 12, 24, NL), (16, 24, NL), (6, 12, 24, NL), (16, 16, NL), (12, 24, NL)],
+    )
+
+
 def on_device(
     fine_now, fine_prev, coarse_now, coarse_prev, fine_rho, fine_mu, fine_lam, fine_metric,
     coarse_rho, coarse_mu, coarse_lam, coarse_metric, couple_index, couple_weight,
@@ -530,16 +576,12 @@
     gx, gy = lax.axis_size("gx"), lax.axis_size("gy")
     near_x, far_x, near_y, far_y = pairs(gx, 0), pairs(gx, 1), pairs(gy, 0), pairs(gy, 1)
     groups = [[i, i + 1] for i in range(0, gx, 2)]
-    table = jnp.asarray(vertical_matrix(), jnp.bfloat16)
 
     blocks = [(4, 16, 24, NL), (6, 12, 24, NL), (4, 16, 24, NL), (5, 12, 24, NL)]
-    *wide, yf, yn, ro = call(
-        pack_y,
-        blocks + [(Y_ROWS + 8, NL), (Y_ROWS, NL), (O_ROWS, NL)],
+    *wide, yf, yn, ro = pack_call(
         fine_now, fine_prev, fine_rho, fine_mu, fine_lam, fine_metric,
         coarse_now, coarse_prev, coarse_rho, coarse_mu, coarse_lam, coarse_metric,
         couple_index, couple_weight,
-        scratch=[(72, NL), (3, 8, 16, NL), (2, 4, 8, NL)],
     )
     wide, ro = [keep(w) for w in wide], keep(ro)
     yf = keep(lax.ppermute(yf, "gy", far_y))
@@ -557,18 +599,7 @@
     wide = [keep(w) for w in wide]
     (r2,) = call(pack_second, [(R_ROWS, NL)], af, bf)
     g2 = keep(lax.all_gather(r2, "gx", axis_index_groups=groups))
-    return tuple(
-        call(
-            main,
-            [(3, 8, 16, NL), (3, 4, 8, NL)] + blocks,
-            *wide, an, am, af, bf, g2, table,
-            local=False,
-            alias={0: 2, 1: 3, 2: 4, 3: 5},
-            scratch=[
-                (3, 12, 24, NL), (3, 12, 24, NL), (16, 24, NL), (4, 12, 24, NL), (16, 16, NL), (12, 24, NL),
-            ],
-        )[:2]
-    )
+    return tuple(main_call(*wide, an, am, af, bf, g2)[:2])
 
 
 def solution(mesh):

time: 50.4 us -> 49 us (0.972)
  Pallas kernels: 8.53 us -> 7.19 us
    pallas_call x7 -> x6, Pallas kernels: 8.53 us -> 5.27 us  [call(): pl.pallas_call(body, out_shape=[jax.ShapeDtypeStruct(s, F32) if k < away...]
    pallas_call x0 -> x1, Pallas kernels: none -> 1.92 us  [pack_call(): pl.pallas_call(pack_y, out_shape=[pltpu.VMEM(s, F32) for s in shapes], in...]
where the time goes in v5:
time: 49 us; the launch traced here: 48.7 us
  starting transfers between devices  32.1 us (66%)
  Pallas kernels  7.19 us (15%)
  blocking collectives  5.43 us (11%)
  waiting for transfers between devices  3.26 us (7%)
  between operations  0.73 us (1%)
    ppermute x1, starting transfers between devices, on_device(): yf = keep(lax.ppermute(yf, 'gy', far_y))  14.1 us
    ppermute x1, starting transfers between devices, on_device(): bf = keep(lax.ppermute(bp, 'gx', far_x))  7.88 us
    pallas_call x6, Pallas kernels, call(): pl.pallas_call(body, out_shape=[jax.ShapeDtypeStruct(s, F32) if k < away...  5.27 us
    ppermute x1, starting transfers between devices, on_device(): af = keep(lax.ppermute(af, 'gx', far_x))  3.94 us
    all_gather x1, blocking collectives, on_device(): gn = keep(lax.all_gather(cn, 'gx', axis_index_groups=groups))  3.6 us
    ppermute x1, waiting for transfers between devices, on_device(): bf = keep(lax.ppermute(bp, 'gx', far_x))  2.42 us
    ppermute x1, starting transfers between devices, on_device(): an = keep(lax.ppermute(an, 'gx', near_x))  2.41 us
    pallas_call x1, Pallas kernels, pack_call(): pl.pallas_call(pack_y, out_shape=[pltpu.VMEM(s, F32) for s in shapes], in...  1.92 us
  transfers between devices with their start and end apart: 6, of which 2 were waited for; matrix products, arithmetic and copies ran while one was open for 0% of the time, Pallas kernels for 1%

profile of v5, /device:TPU:57, one launch (start us, length us, event | category | flops | bytes accessed | tf_op | source)
XLA Modules:
  0.0 48.7 jit_solution(11490632059345148008)
XLA Ops:
  0.6 1.9 %shard_map.158 = (f32[4,16,24,128]{3,2,1,0:T(8,128)S(1)}, f32[6,12,24,128]{3,2,1,0:T(8,128)S(1)}, f32[4,16,24,128]{3,2,1,0:T(8,128)S(1)}, f32[5,12,24,128]{3,2,1...) custom-call(f32[3,8,16,128]{3,2,1,0:T(8,128)} %refs_0_.1, ...), custom_call_target="tpu_custom_call" | custom-call | tf_op jit(solution)/shard_map/pallas_call | solution.py:546
  2.6 14.1 %collective-permute-start.1 = (f32[344,128]{1,0:T(8,128)S(1)}, f32[344,128]{1,0:T(8,128)S(1)}, u32[]{:S(2)}, u32[]{:S(2)}) collective-permute-start(f32[344,128]{1,0:T(8,128)S(1)} %get-tuple-element.23), channel_id=1, source_target_pairs={{1,2},{2,1},{3,4},{4,3},{5,6},{6,5},{7,8},{8,7},{9,10},{10,9},{11,... | collective-permute-start | bytes 528392 | tf_op jit(solution)/shard_map/ppermute | solution.py:587
  16.6 1.9 %collective-permute-start = (f32[336,128]{1,0:T(8,128)S(1)}, f32[336,128]{1,0:T(8,128)S(1)}, u32[]{:S(2)}, u32[]{:S(2)}) collective-permute-start(f32[336,128]{1,0:T(8,128)S(1)} %get-tuple-element.22), channel_id=1, source_target_pairs={{0,1},{1,0},{2,3},{3,2},{4,5},{5,4},{6,7},{7,6},{8,9},{9,8},{10,11... | collective-permute-start | bytes 516104 | tf_op jit(solution)/shard_map/ppermute | solution.py:588
  18.6 0.1 shard_map.162
  18.7 3.9 %collective-permute-start.4 = (f32[664,128]{1,0:T(8,128)S(1)}, f32[664,128]{1,0:T(8,128)S(1)}, u32[]{:S(2)}, u32[]{:S(2)}) collective-permute-start(f32[664,128]{1,0:T(8,128)S(1)} %get-tuple-element.31), channel_id=1, source_target_pairs={{16,32},{32,16},{48,64},{64,48},{80,96},{96,80},{112,128},{128,112... | collective-permute-start | bytes 1019912 | tf_op jit(solution)/shard_map/ppermute | solution.py:590
  22.6 0.8 %collective-permute-done.rn.yn = f32[336,128]{1,0:T(8,128)S(1)} collective-permute-done((f32[336,128]{1,0:T(8,128)S(1)}, f32[336,128]{1,0:T(8,128)S(1)}, u32[]{:S(2)}, u32[]{:S(2)}) %collective-permute-start) | collective-permute-done | bytes 172064 | tf_op jit(solution)/shard_map/ppermute | solution.py:588
  23.5 0.0 collective-permute-done.1.rf.yf
  23.5 3.6 %all-gather = f32[816,128]{1,0:T(8,128)S(1)} all-gather(f32[408,128]{1,0:T(8,128)S(1)} %shard_map.159), channel_id=2, replica_groups={{0,16},{32,48},{64,80},{96,112},{128,144},{160,176},{192,208},{224,240}..., dimensions={0}, use_global_device_ids=true | all-gather | bytes 626688 | tf_op jit(solution)/shard_map/all_gather | solution.py:594
  27.1 0.1 shard_map.160._____
  27.2 7.9 %collective-permute-start.5 = (f32[424,128]{1,0:T(8,128)S(1)}, f32[424,128]{1,0:T(8,128)S(1)}, u32[]{:S(2)}, u32[]{:S(2)}) collective-permute-start(f32[424,128]{1,0:T(8,128)S(1)} %shard_map.160._____), channel_id=1, source_target_pairs={{16,32},{32,16},{48,64},{64,48},{80,96},{96,80},{112,128},{128,112... | collective-permute-start | bytes 651272 | tf_op jit(solution)/shard_map/ppermute | solution.py:597
  35.0 1.9 %collective-permute-start.3 = (f32[408,128]{1,0:T(8,128)S(1)}, f32[408,128]{1,0:T(8,128)S(1)}, u32[]{:S(2)}, u32[]{:S(2)}) collective-permute-start(f32[408,128]{1,0:T(8,128)S(1)} %get-tuple-element.30), channel_id=1, source_target_pairs={{0,16},{16,0},{32,48},{48,32},{64,80},{80,64},{96,112},{112,96},{1... | collective-permute-start | bytes 626696 | tf_op jit(solution)/shard_map/ppermute | solution.py:592
  37.0 2.4 %collective-permute-start.2 = (f32[256,128]{1,0:T(8,128)S(1)}, f32[256,128]{1,0:T(8,128)S(1)}, u32[]{:S(2)}, u32[]{:S(2)}) collective-permute-start(f32[256,128]{1,0:T(8,128)S(1)} %get-tuple-element.29), channel_id=1, source_target_pairs={{0,16},{16,0},{32,48},{48,32},{64,80},{80,64},{96,112},{112,96},{1... | collective-permute-start | bytes 393224 | tf_op jit(solution)/shard_map/ppermute | solution.py:591
  39.4 0.2 shard_map.161
  39.6 0.0 collective-permute-done.4.a.af
  39.6 2.4 %collective-permute-done.5.c.bf = f32[424,128]{1,0:T(8,128)S(1)} collective-permute-done((f32[424,128]{1,0:T(8,128)S(1)}, f32[424,128]{1,0:T(8,128)S(1)}, u32[]{:S(2)}, u32[]{:S(2)}) %collective-permute-start.5) | collective-permute-done | bytes 217120 | tf_op jit(solution)/shard_map/ppermute | solution.py:597
  42.0 0.0 copy-start
  42.0 0.1 shard_map.163
  42.1 1.8 %all-gather.1 = f32[48,128]{1,0:T(8,128)S(1)} all-gather(f32[24,128]{1,0:T(8,128)S(1)} %shard_map.163), channel_id=3, replica_groups={{0,16},{32,48},{64,80},{96,112},{128,144},{160,176},{192,208},{224,240}..., dimensions={0}, use_global_device_ids=true | all-gather | bytes 36864 | tf_op jit(solution)/shard_map/all_gather | solution.py:601
  43.9 0.0 collective-permute-done.2.an
  43.9 0.0 collective-permute-done.3.am
  43.9 0.0 copy-done
  43.9 4.8 %shard_map.164 = (f32[3,8,16,128]{3,2,1,0:T(8,128)}, f32[3,4,8,128]{3,2,1,0:T(8,128)}, f32[4,16,24,128]{3,2,1,0:T(8,128)S(1)}, f32[6,12,24,128]{3,2,1,0:T(8,128)...) custom-call(f32[4,16,24,128]{3,2,1,0:T(8,128)S(1)} %get-tuple-elemen, ...), custom_call_target="tpu_custom_call", output_to_operand_aliasing={{2}: (0, {}), {3}: (1, {}), {4}: (2, {}), {5}: (3, {})} | custom-call | tf_op jit(solution)/shard_map/pallas_call | solution.py:524
  (1 shorter events, 0.0 us)
Async XLA Ops:
  2.6 20.9 %collective-permute-start.1 = (f32[344,128]{1,0:T(8,128)S(1)}, f32[344,128]{1,0:T(8,128)S(1)}, u32[]{:S(2)}, u32[]{:S(2)}) collective-permute-start(f32[344,128]{1,0:T(8,128)S(1)} %get-tuple-element.23), channel_id=1, source_target_pairs={{1,2},{2,1},{3,4},{4,3},{5,6},{6,5},{7,8},{8,7},{9,10},{10,9},{11,... | collective-permute-start | bytes 528392 | tf_op jit(solution)/shard_map/ppermute | solution.py:587
  16.6 6.8 %collective-permute-start = (f32[336,128]{1,0:T(8,128)S(1)}, f32[336,128]{1,0:T(8,128)S(1)}, u32[]{:S(2)}, u32[]{:S(2)}) collective-permute-start(f32[336,128]{1,0:T(8,128)S(1)} %get-tuple-element.22), channel_id=1, source_target_pairs={{0,1},{1,0},{2,3},{3,2},{4,5},{5,4},{6,7},{7,6},{8,9},{9,8},{10,11... | collective-permute-start | bytes 516104 | tf_op jit(solution)/shard_map/ppermute | solution.py:588
  18.7 20.9 %collective-permute-start.4 = (f32[664,128]{1,0:T(8,128)S(1)}, f32[664,128]{1,0:T(8,128)S(1)}, u32[]{:S(2)}, u32[]{:S(2)}) collective-permute-start(f32[664,128]{1,0:T(8,128)S(1)} %get-tuple-element.31), channel_id=1, source_target_pairs={{16,32},{32,16},{48,64},{64,48},{80,96},{96,80},{112,128},{128,112... | collective-permute-start | bytes 1019912 | tf_op jit(solution)/shard_map/ppermute | solution.py:590
  27.2 14.9 %collective-permute-start.5 = (f32[424,128]{1,0:T(8,128)S(1)}, f32[424,128]{1,0:T(8,128)S(1)}, u32[]{:S(2)}, u32[]{:S(2)}) collective-permute-start(f32[424,128]{1,0:T(8,128)S(1)} %shard_map.160._____), channel_id=1, source_target_pairs={{16,32},{32,16},{48,64},{64,48},{80,96},{96,80},{112,128},{128,112... | collective-permute-start | bytes 651272 | tf_op jit(solution)/shard_map/ppermute | solution.py:597
  35.0 8.9 %collective-permute-start.3 = (f32[408,128]{1,0:T(8,128)S(1)}, f32[408,128]{1,0:T(8,128)S(1)}, u32[]{:S(2)}, u32[]{:S(2)}) collective-permute-start(f32[408,128]{1,0:T(8,128)S(1)} %get-tuple-element.30), channel_id=1, source_target_pairs={{0,16},{16,0},{32,48},{48,32},{64,80},{80,64},{96,112},{112,96},{1... | collective-permute-start | bytes 626696 | tf_op jit(solution)/shard_map/ppermute | solution.py:592
  37.0 6.9 %collective-permute-start.2 = (f32[256,128]{1,0:T(8,128)S(1)}, f32[256,128]{1,0:T(8,128)S(1)}, u32[]{:S(2)}, u32[]{:S(2)}) collective-permute-start(f32[256,128]{1,0:T(8,128)S(1)} %get-tuple-element.29), channel_id=1, source_target_pairs={{0,16},{16,0},{32,48},{48,32},{64,80},{80,64},{96,112},{112,96},{1... | collective-permute-start | bytes 393224 | tf_op jit(solution)/shard_map/ppermute | solution.py:591
  42.0 1.9 %copy-start = (bf16[256,128]{1,0:T(8,128)(2,1)S(1)}, bf16[256,128]{1,0:T(8,128)(2,1)}, u32[]{:S(2)}) copy-start(bf16[256,128]{1,0:T(8,128)(2,1)} %constant.2.clone.table_ref) | copy-start | bytes 196612

commit v6 on v5

--- a/solution.py
+++ b/solution.py
@@ -92,17 +92,15 @@
 
 
 def pack_y(*refs):
-    inputs, outputs, rest = refs[:14], refs[14:21], refs[21:]
-    local, sems, (stage, fo, co) = rest[:14], rest[14], rest[15:]
+    inputs, kept, (fo, co, yf, yn, ro), rest = refs[:14], refs[14:20], refs[20:25], refs[25:]
+    passing, sems, stage = rest[:8], rest[8], rest[9]
+    local = list(passing)
+    for place, ref in zip(KEPT, kept):
+        local.insert(place, ref)
     copies = [pltpu.make_async_copy(i, v, sems.at[k]) for k, (i, v) in enumerate(zip(inputs, local))]
     for k in PACK_ORDER:
         copies[k].start()
     fn, fp, fr, fm, fl, fj, cn, cp, cr, cm, cl, cj, ix, wt = local
-    fe, fb, ce, cb, yf, yn, ro = outputs
-    for half in (slice(0, 8), slice(16, 24)):
-        ce[:, :, half] = jnp.zeros((4, 16, 8, NL), F32)
-        cb[:, :, half] = jnp.zeros((5, 12, 8, NL), F32)
-        fb[:, :, half] = jnp.zeros((6, 12, 8, NL), F32)
     lane = lax.broadcasted_iota(jnp.int32, (128, NL), 1)
     for k in PACK_ORDER[:2]:
         copies[k].wait()
@@ -136,6 +134,13 @@
     yf[Y_ROWS:] = jnp.zeros((8, NL), F32)
     x0 = 2 - 2 * odd("gx")
     ro[...] = tops_of([cn[i, x0 + x] if i < 3 else cj[x0 + x] * (1.0 / 12.0) for i in range(4) for x in range(2)])
+
+
+def pack_x(fn, fp, fj, cn, cp, cj, fo, co, fe, fb, ce, cb, an, am, af):
+    for half in (slice(0, 8), slice(16, 24)):
+        ce[:, :, half] = jnp.zeros((4, 16, 8, NL), F32)
+        cb[:, :, half] = jnp.zeros((5, 12, 8, NL), F32)
+        fb[:, :, half] = jnp.zeros((6, 12, 8, NL), F32)
     for x in range(8):
         for i in range(3):
             fe[i, 4 + x, 4:20] = fn[i, x]
@@ -149,9 +154,6 @@
         for i in range(2):
             cb[3 + i, 4 + x, 8:16] = co[i, x]
         ce[3, 6 + x, 8:16] = cj[x] * (1.0 / 12.0)
-
-
-def pack_x(fe, fb, ce, cb, an, am, af):
     near = Joined(an, am)
 
     def x_edge(out, low):
@@ -540,27 +542,29 @@
 PACK_ORDER = (12, 13, 0, 1, 5, 2, 3, 4, 6, 7, 11, 8, 9, 10)
 
 
+KEPT = (0, 1, 5, 6, 7, 11)
+BLOCKS = [(4, 16, 24, NL), (6, 12, 24, NL), (4, 16, 24, NL), (5, 12, 24, NL)]
+
+
 def pack_call(*operands):
-    blocks = [(4, 16, 24, NL), (6, 12, 24, NL), (4, 16, 24, NL), (5, 12, 24, NL)]
-    shapes = blocks + [(Y_ROWS + 8, NL), (Y_ROWS, NL), (O_ROWS, NL)]
+    shapes = [operands[k].shape for k in KEPT]
+    shapes += [(3, 8, 16, NL), (2, 4, 8, NL), (Y_ROWS + 8, NL), (Y_ROWS, NL), (O_ROWS, NL)]
     return pl.pallas_call(
         pack_y,
         out_shape=[pltpu.VMEM(s, F32) for s in shapes],
         in_specs=[pl.BlockSpec(memory_space=pl.ANY)] * len(operands),
         out_specs=[pl.BlockSpec(memory_space=pltpu.VMEM)] * len(shapes),
-        scratch_shapes=[pltpu.VMEM(o.shape, o.dtype) for o in operands]
-        + [pltpu.SemaphoreType.DMA((len(operands),))]
-        + [pltpu.VMEM(s, F32) for s in ((72, NL), (3, 8, 16, NL), (2, 4, 8, NL))],
+        scratch_shapes=[pltpu.VMEM(o.shape, o.dtype) for k, o in enumerate(operands) if k not in KEPT]
+        + [pltpu.SemaphoreType.DMA((len(operands),)), pltpu.VMEM((72, NL), F32)],
         compiler_params=pltpu.CompilerParams(vmem_limit_bytes=56 << 20),
         interpret=INTERPRET,
     )(*operands)
 
 
 def main_call(*operands):
-    blocks = [(4, 16, 24, NL), (6, 12, 24, NL), (4, 16, 24, NL), (5, 12, 24, NL)]
     return call(
         main,
-        [(3, 8, 16, NL), (3, 4, 8, NL)] + blocks,
+        [(3, 8, 16, NL), (3, 4, 8, NL)] + BLOCKS,
         *operands,
         keep(jnp.asarray(vertical_matrix(), jnp.bfloat16)),
         local=False,
@@ -577,16 +581,16 @@
     near_x, far_x, near_y, far_y = pairs(gx, 0), pairs(gx, 1), pairs(gy, 0), pairs(gy, 1)
     groups = [[i, i + 1] for i in range(0, gx, 2)]
 
-    blocks = [(4, 16, 24, NL), (6, 12, 24, NL), (4, 16, 24, NL), (5, 12, 24, NL)]
-    *wide, yf, yn, ro = pack_call(
+    *own, yf, yn, ro = pack_call(
         fine_now, fine_prev, fine_rho, fine_mu, fine_lam, fine_metric,
         coarse_now, coarse_prev, coarse_rho, coarse_mu, coarse_lam, coarse_metric,
         couple_index, couple_weight,
     )
-    wide, ro = [keep(w) for w in wide], keep(ro)
+    own, ro = [keep(w) for w in own], keep(ro)
     yf = keep(lax.ppermute(yf, "gy", far_y))
     yn = keep(lax.ppermute(yn, "gy", near_y))
-    an, am, af = call(pack_x, [(AB, NL), (A_ROWS - AB, NL), (A_ROWS, NL)], *wide)
+    *wide, an, am, af = call(pack_x, BLOCKS + [(AB, NL), (A_ROWS - AB, NL), (A_ROWS, NL)], *own)
+    wide = [keep(w) for w in wide]
     af = keep(lax.ppermute(af, "gx", far_x))
     an = keep(lax.ppermute(an, "gx", near_x))
     am = keep(lax.ppermute(am, "gx", near_x))
@@ -595,7 +599,7 @@
     (bp,) = call(pack_far, [(C_ROWS + R_ROWS, NL)], yn, yf, gn)
     bp = keep(bp)
     bf = keep(lax.ppermute(bp, "gx", far_x))
-    wide = call(fill, blocks, *wide, yn, yf, gn, bp, alias={0: 0, 1: 1, 2: 2, 3: 3})
+    wide = call(fill, BLOCKS, *wide, yn, yf, gn, bp, alias={0: 0, 1: 1, 2: 2, 3: 3})
     wide = [keep(w) for w in wide]
     (r2,) = call(pack_second, [(R_ROWS, NL)], af, bf)
     g2 = keep(lax.all_gather(r2, "gx", axis_index_groups=groups))

time: 49 us -> 49.1 us (level)
  no operation moved by 1% of the time
where the time goes in v6:
time: 49.1 us; the launch traced here: 48.8 us
  starting transfers between devices  32 us (65%)
  Pallas kernels  7.34 us (15%)
  blocking collectives  5.43 us (11%)
  waiting for transfers between devices  3.21 us (7%)
  between operations  0.73 us (1%)
    ppermute x1, starting transfers between devices, on_device(): yf = keep(lax.ppermute(yf, 'gy', far_y))  14.1 us
    ppermute x1, starting transfers between devices, on_device(): bf = keep(lax.ppermute(bp, 'gx', far_x))  7.78 us
    pallas_call x6, Pallas kernels, call(): pl.pallas_call(body, out_shape=[jax.ShapeDtypeStruct(s, F32) if k < away...  5.43 us
    ppermute x1, starting transfers between devices, on_device(): af = keep(lax.ppermute(af, 'gx', far_x))  3.95 us
    all_gather x1, blocking collectives, on_device(): gn = keep(lax.all_gather(cn, 'gx', axis_index_groups=groups))  3.6 us
    ppermute x1, waiting for transfers between devices, on_device(): bf = keep(lax.ppermute(bp, 'gx', far_x))  2.53 us
    ppermute x1, starting transfers between devices, on_device(): an = keep(lax.ppermute(an, 'gx', near_x))  2.41 us
    ppermute x1, starting transfers between devices, on_device(): am = keep(lax.ppermute(am, 'gx', near_x))  1.92 us
  transfers between devices with their start and end apart: 6, of which 2 were waited for; matrix products, arithmetic and copies ran while one was open for 0% of the time, Pallas kernels for 1%

profile of v6, /device:TPU:57, one launch (start us, length us, event | category | flops | bytes accessed | tf_op | source)
XLA Modules:
  0.0 48.8 jit_solution(17268128652212823850)
XLA Ops:
  0.6 1.9 %shard_map.158 = (f32[3,8,16,128]{3,2,1,0:T(8,128)S(1)}, f32[3,8,16,128]{3,2,1,0:T(8,128)S(1)}, f32[8,16,128]{2,1,0:T(8,128)S(1)}, f32[3,4,8,128]{3,2,1,0:T(8,12...) custom-call(f32[3,8,16,128]{3,2,1,0:T(8,128)} %refs_0_.1, ...), custom_call_target="tpu_custom_call" | custom-call | tf_op jit(solution)/shard_map/pallas_call | solution.py:552
  2.6 14.1 %collective-permute-start.1 = (f32[344,128]{1,0:T(8,128)S(1)}, f32[344,128]{1,0:T(8,128)S(1)}, u32[]{:S(2)}, u32[]{:S(2)}) collective-permute-start(f32[344,128]{1,0:T(8,128)S(1)} %get-tuple-element.39), channel_id=1, source_target_pairs={{1,2},{2,1},{3,4},{4,3},{5,6},{6,5},{7,8},{8,7},{9,10},{10,9},{11,... | collective-permute-start | bytes 528392 | tf_op jit(solution)/shard_map/ppermute | solution.py:590
  16.6 1.9 %collective-permute-start = (f32[336,128]{1,0:T(8,128)S(1)}, f32[336,128]{1,0:T(8,128)S(1)}, u32[]{:S(2)}, u32[]{:S(2)}) collective-permute-start(f32[336,128]{1,0:T(8,128)S(1)} %get-tuple-element.38), channel_id=1, source_target_pairs={{0,1},{1,0},{2,3},{3,2},{4,5},{5,4},{6,7},{7,6},{8,9},{9,8},{10,11... | collective-permute-start | bytes 516104 | tf_op jit(solution)/shard_map/ppermute | solution.py:591
  18.6 0.3 shard_map.159
  18.8 4.0 %collective-permute-start.4 = (f32[664,128]{1,0:T(8,128)S(1)}, f32[664,128]{1,0:T(8,128)S(1)}, u32[]{:S(2)}, u32[]{:S(2)}) collective-permute-start(f32[664,128]{1,0:T(8,128)S(1)} %get-tuple-element.47), channel_id=1, source_target_pairs={{16,32},{32,16},{48,64},{64,48},{80,96},{96,80},{112,128},{128,112... | collective-permute-start | bytes 1019912 | tf_op jit(solution)/shard_map/ppermute | solution.py:594
  22.8 0.7 %collective-permute-done.rn.yn = f32[336,128]{1,0:T(8,128)S(1)} collective-permute-done((f32[336,128]{1,0:T(8,128)S(1)}, f32[336,128]{1,0:T(8,128)S(1)}, u32[]{:S(2)}, u32[]{:S(2)}) %collective-permute-start) | collective-permute-done | bytes 172064 | tf_op jit(solution)/shard_map/ppermute | solution.py:591
  23.4 0.0 collective-permute-done.1.rf.yf
  23.5 3.6 %all-gather = f32[816,128]{1,0:T(8,128)S(1)} all-gather(f32[408,128]{1,0:T(8,128)S(1)} %shard_map.160), channel_id=2, replica_groups={{0,16},{32,48},{64,80},{96,112},{128,144},{160,176},{192,208},{224,240}..., dimensions={0}, use_global_device_ids=true | all-gather | bytes 626688 | tf_op jit(solution)/shard_map/all_gather | solution.py:598
  27.1 0.1 shard_map.161._____
  27.2 7.8 %collective-permute-start.5 = (f32[424,128]{1,0:T(8,128)S(1)}, f32[424,128]{1,0:T(8,128)S(1)}, u32[]{:S(2)}, u32[]{:S(2)}) collective-permute-start(f32[424,128]{1,0:T(8,128)S(1)} %shard_map.161._____), channel_id=1, source_target_pairs={{16,32},{32,16},{48,64},{64,48},{80,96},{96,80},{112,128},{128,112... | collective-permute-start | bytes 651272 | tf_op jit(solution)/shard_map/ppermute | solution.py:601
  34.9 1.9 %collective-permute-start.3 = (f32[408,128]{1,0:T(8,128)S(1)}, f32[408,128]{1,0:T(8,128)S(1)}, u32[]{:S(2)}, u32[]{:S(2)}) collective-permute-start(f32[408,128]{1,0:T(8,128)S(1)} %get-tuple-element.46), channel_id=1, source_target_pairs={{0,16},{16,0},{32,48},{48,32},{64,80},{80,64},{96,112},{112,96},{1... | collective-permute-start | bytes 626696 | tf_op jit(solution)/shard_map/ppermute | solution.py:596
  36.9 2.4 %collective-permute-start.2 = (f32[256,128]{1,0:T(8,128)S(1)}, f32[256,128]{1,0:T(8,128)S(1)}, u32[]{:S(2)}, u32[]{:S(2)}) collective-permute-start(f32[256,128]{1,0:T(8,128)S(1)} %get-tuple-element.45), channel_id=1, source_target_pairs={{0,16},{16,0},{32,48},{48,32},{64,80},{80,64},{96,112},{112,96},{1... | collective-permute-start | bytes 393224 | tf_op jit(solution)/shard_map/ppermute | solution.py:595
  39.3 0.2 shard_map.162
  39.5 0.0 collective-permute-done.4.a.af
  39.5 2.5 %collective-permute-done.5.c.bf = f32[424,128]{1,0:T(8,128)S(1)} collective-permute-done((f32[424,128]{1,0:T(8,128)S(1)}, f32[424,128]{1,0:T(8,128)S(1)}, u32[]{:S(2)}, u32[]{:S(2)}) %collective-permute-start.5) | collective-permute-done | bytes 217120 | tf_op jit(solution)/shard_map/ppermute | solution.py:601
  42.0 0.0 copy-start
  42.0 0.1 shard_map.163
  42.1 1.8 %all-gather.1 = f32[48,128]{1,0:T(8,128)S(1)} all-gather(f32[24,128]{1,0:T(8,128)S(1)} %shard_map.163), channel_id=3, replica_groups={{0,16},{32,48},{64,80},{96,112},{128,144},{160,176},{192,208},{224,240}..., dimensions={0}, use_global_device_ids=true | all-gather | bytes 36864 | tf_op jit(solution)/shard_map/all_gather | solution.py:605
  43.9 0.0 collective-permute-done.2.an
  43.9 0.0 collective-permute-done.3.am
  43.9 0.0 copy-done
  43.9 4.8 %shard_map.164 = (f32[3,8,16,128]{3,2,1,0:T(8,128)}, f32[3,4,8,128]{3,2,1,0:T(8,128)}, f32[4,16,24,128]{3,2,1,0:T(8,128)S(1)}, f32[6,12,24,128]{3,2,1,0:T(8,128)...) custom-call(f32[4,16,24,128]{3,2,1,0:T(8,128)S(1)} %get-tuple-elemen, ...), custom_call_target="tpu_custom_call", output_to_operand_aliasing={{2}: (0, {}), {3}: (1, {}), {4}: (2, {}), {5}: (3, {})} | custom-call | tf_op jit(solution)/shard_map/pallas_call | solution.py:526
  (1 shorter events, 0.0 us)
Async XLA Ops:
  2.6 20.9 %collective-permute-start.1 = (f32[344,128]{1,0:T(8,128)S(1)}, f32[344,128]{1,0:T(8,128)S(1)}, u32[]{:S(2)}, u32[]{:S(2)}) collective-permute-start(f32[344,128]{1,0:T(8,128)S(1)} %get-tuple-element.39), channel_id=1, source_target_pairs={{1,2},{2,1},{3,4},{4,3},{5,6},{6,5},{7,8},{8,7},{9,10},{10,9},{11,... | collective-permute-start | bytes 528392 | tf_op jit(solution)/shard_map/ppermute | solution.py:590
  16.6 6.8 %collective-permute-start = (f32[336,128]{1,0:T(8,128)S(1)}, f32[336,128]{1,0:T(8,128)S(1)}, u32[]{:S(2)}, u32[]{:S(2)}) collective-permute-start(f32[336,128]{1,0:T(8,128)S(1)} %get-tuple-element.38), channel_id=1, source_target_pairs={{0,1},{1,0},{2,3},{3,2},{4,5},{5,4},{6,7},{7,6},{8,9},{9,8},{10,11... | collective-permute-start | bytes 516104 | tf_op jit(solution)/shard_map/ppermute | solution.py:591
  18.8 20.7 %collective-permute-start.4 = (f32[664,128]{1,0:T(8,128)S(1)}, f32[664,128]{1,0:T(8,128)S(1)}, u32[]{:S(2)}, u32[]{:S(2)}) collective-permute-start(f32[664,128]{1,0:T(8,128)S(1)} %get-tuple-element.47), channel_id=1, source_target_pairs={{16,32},{32,16},{48,64},{64,48},{80,96},{96,80},{112,128},{128,112... | collective-permute-start | bytes 1019912 | tf_op jit(solution)/shard_map/ppermute | solution.py:594
  27.2 14.9 %collective-permute-start.5 = (f32[424,128]{1,0:T(8,128)S(1)}, f32[424,128]{1,0:T(8,128)S(1)}, u32[]{:S(2)}, u32[]{:S(2)}) collective-permute-start(f32[424,128]{1,0:T(8,128)S(1)} %shard_map.161._____), channel_id=1, source_target_pairs={{16,32},{32,16},{48,64},{64,48},{80,96},{96,80},{112,128},{128,112... | collective-permute-start | bytes 651272 | tf_op jit(solution)/shard_map/ppermute | solution.py:601
  34.9 9.0 %collective-permute-start.3 = (f32[408,128]{1,0:T(8,128)S(1)}, f32[408,128]{1,0:T(8,128)S(1)}, u32[]{:S(2)}, u32[]{:S(2)}) collective-permute-start(f32[408,128]{1,0:T(8,128)S(1)} %get-tuple-element.46), channel_id=1, source_target_pairs={{0,16},{16,0},{32,48},{48,32},{64,80},{80,64},{96,112},{112,96},{1... | collective-permute-start | bytes 626696 | tf_op jit(solution)/shard_map/ppermute | solution.py:596
  36.9 7.1 %collective-permute-start.2 = (f32[256,128]{1,0:T(8,128)S(1)}, f32[256,128]{1,0:T(8,128)S(1)}, u32[]{:S(2)}, u32[]{:S(2)}) collective-permute-start(f32[256,128]{1,0:T(8,128)S(1)} %get-tuple-element.45), channel_id=1, source_target_pairs={{0,16},{16,0},{32,48},{48,32},{64,80},{80,64},{96,112},{112,96},{1... | collective-permute-start | bytes 393224 | tf_op jit(solution)/shard_map/ppermute | solution.py:595
  42.0 1.9 %copy-start = (bf16[256,128]{1,0:T(8,128)(2,1)S(1)}, bf16[256,128]{1,0:T(8,128)(2,1)}, u32[]{:S(2)}) copy-start(bf16[256,128]{1,0:T(8,128)(2,1)} %constant.2.clone.table_ref) | copy-start | bytes 196612

commit v7 on v6

--- a/solution.py
+++ b/solution.py
@@ -66,16 +66,27 @@
     return jnp.where(lane >= NL - 8, pltpu.roll(packed, (NL - 8 - 8 * slot) % NL, 1), 0.0)
 
 
-def y_edge(out, stage, low, fn, fp, fj, fo, cn, cp, cj, co):
+def one_hot_rows(index, weight):
+    lane = lax.broadcasted_iota(jnp.int32, (index.shape[0], NL), 1)
+    slot = index + 2 + 4 * ((index * 171) >> 11)
+    acc = jnp.zeros((index.shape[0], NL), F32)
+    for k in range(16):
+        acc = acc + jnp.where(lane == slot[:, k : k + 1], weight[:, k : k + 1], 0.0)
+    return acc
+
+
+def y_edge(out, stage, low, fn, fp, fj, fo, cn, cp, cj, co, edge):
     for i in range(4):
         for x in range(8):
             v = fn[i, x] if i < 3 else fj[x] * (1.0 / 12.0)
             out[i * 32 + x * 4 : i * 32 + x * 4 + 4] = v[0:4] if low else v[12:16]
     for i in range(6):
         for x in range(8):
-            v = fp[i, x] if i < 3 else fo[i - 3, x]
-            v = v[0:2] if low else v[14:16]
-            if i == 5:
+            if i < 5:
+                v = fp[i, x] if i < 3 else fo[i - 3, x]
+                v = v[0:2] if low else v[14:16]
+            else:
+                v = edge[x * 4 : x * 4 + 2] if low else edge[x * 4 + 2 : x * 4 + 4]
                 v = pltpu.roll(v, 8 if low else 120, 1)
             out[YB + i * 16 + x * 2 : YB + i * 16 + x * 2 + 2] = v
     for i in range(4):
@@ -92,8 +103,8 @@
 
 
 def pack_y(*refs):
-    inputs, kept, (fo, co, yf, yn, ro), rest = refs[:14], refs[14:20], refs[20:25], refs[25:]
-    passing, sems, stage = rest[:8], rest[8], rest[9]
+    inputs, kept, (fo, co, yf, yn, ro), rest = refs[:14], refs[14:22], refs[22:27], refs[27:]
+    passing, (sems, stage, edge, edge_index, edge_weight) = rest[:6], rest[6:]
     local = list(passing)
     for place, ref in zip(KEPT, kept):
         local.insert(place, ref)
@@ -101,16 +112,13 @@
     for k in PACK_ORDER:
         copies[k].start()
     fn, fp, fr, fm, fl, fj, cn, cp, cr, cm, cl, cj, ix, wt = local
-    lane = lax.broadcasted_iota(jnp.int32, (128, NL), 1)
     for k in PACK_ORDER[:2]:
         copies[k].wait()
-    index = ix[...].reshape(128, 16)
-    weight = wt[...].reshape(128, 16)
-    slot = index + 2 + 4 * ((index * 171) >> 11)
-    acc = jnp.zeros((128, NL), F32)
-    for k in range(16):
-        acc = acc + jnp.where(lane == slot[:, k : k + 1], weight[:, k : k + 1], 0.0)
-    fo[2] = acc.reshape(8, 16, NL)
+    for x in range(8):
+        for o, y in ((0, 0), (2, 14)):
+            edge_index[x * 4 + o : x * 4 + o + 2] = ix[x, y : y + 2]
+            edge_weight[x * 4 + o : x * 4 + o + 2] = wt[x, y : y + 2]
+    edge[...] = one_hot_rows(edge_index[...], edge_weight[...])
     for k in PACK_ORDER[2:]:
         copies[k].wait()
     inv = DT2 / fr[...]
@@ -123,28 +131,32 @@
 
     @pl.when(oy == 0)
     def _():
-        y_edge(yf, stage, True, fn, fp, fj, fo, cn, cp, cj, co)
-        y_edge(yn, stage, False, fn, fp, fj, fo, cn, cp, cj, co)
+        y_edge(yf, stage, True, fn, fp, fj, fo, cn, cp, cj, co, edge)
+        y_edge(yn, stage, False, fn, fp, fj, fo, cn, cp, cj, co, edge)
 
     @pl.when(oy == 1)
     def _():
-        y_edge(yf, stage, False, fn, fp, fj, fo, cn, cp, cj, co)
-        y_edge(yn, stage, True, fn, fp, fj, fo, cn, cp, cj, co)
+        y_edge(yf, stage, False, fn, fp, fj, fo, cn, cp, cj, co, edge)
+        y_edge(yn, stage, True, fn, fp, fj, fo, cn, cp, cj, co, edge)
 
     yf[Y_ROWS:] = jnp.zeros((8, NL), F32)
     x0 = 2 - 2 * odd("gx")
     ro[...] = tops_of([cn[i, x0 + x] if i < 3 else cj[x0 + x] * (1.0 / 12.0) for i in range(4) for x in range(2)])
 
 
-def pack_x(fn, fp, fj, cn, cp, cj, fo, co, fe, fb, ce, cb, an, am, af):
+def pack_x(fn, fp, fj, cn, cp, cj, ix, wt, fo, co, fe, fb, ce, cb, an, am, af):
     for half in (slice(0, 8), slice(16, 24)):
         ce[:, :, half] = jnp.zeros((4, 16, 8, NL), F32)
         cb[:, :, half] = jnp.zeros((5, 12, 8, NL), F32)
         fb[:, :, half] = jnp.zeros((6, 12, 8, NL), F32)
+    mix = one_hot_rows(ix[...].reshape(128, 16), wt[...].reshape(128, 16))
+    for x in range(8):
+        fb[5, 2 + x, 4:20] = mix[x * 16 : x * 16 + 16]
     for x in range(8):
         for i in range(3):
             fe[i, 4 + x, 4:20] = fn[i, x]
             fb[i, 2 + x, 4:20] = fp[i, x]
+        for i in range(2):
             fb[3 + i, 2 + x, 4:20] = fo[i, x]
         fe[3, 4 + x, 4:20] = fj[x] * (1.0 / 12.0)
     for x in range(4):
@@ -542,20 +554,20 @@
 PACK_ORDER = (12, 13, 0, 1, 5, 2, 3, 4, 6, 7, 11, 8, 9, 10)
 
 
-KEPT = (0, 1, 5, 6, 7, 11)
+KEPT = (0, 1, 5, 6, 7, 11, 12, 13)
 BLOCKS = [(4, 16, 24, NL), (6, 12, 24, NL), (4, 16, 24, NL), (5, 12, 24, NL)]
 
 
 def pack_call(*operands):
-    shapes = [operands[k].shape for k in KEPT]
-    shapes += [(3, 8, 16, NL), (2, 4, 8, NL), (Y_ROWS + 8, NL), (Y_ROWS, NL), (O_ROWS, NL)]
+    shapes = [(2, 8, 16, NL), (2, 4, 8, NL), (Y_ROWS + 8, NL), (Y_ROWS, NL), (O_ROWS, NL)]
     return pl.pallas_call(
         pack_y,
-        out_shape=[pltpu.VMEM(s, F32) for s in shapes],
+        out_shape=[pltpu.VMEM(operands[k].shape, operands[k].dtype) for k in KEPT] + [pltpu.VMEM(s, F32) for s in shapes],
         in_specs=[pl.BlockSpec(memory_space=pl.ANY)] * len(operands),
-        out_specs=[pl.BlockSpec(memory_space=pltpu.VMEM)] * len(shapes),
+        out_specs=[pl.BlockSpec(memory_space=pltpu.VMEM)] * (len(KEPT) + len(shapes)),
         scratch_shapes=[pltpu.VMEM(o.shape, o.dtype) for k, o in enumerate(operands) if k not in KEPT]
-        + [pltpu.SemaphoreType.DMA((len(operands),)), pltpu.VMEM((72, NL), F32)],
+        + [pltpu.SemaphoreType.DMA((len(operands),)), pltpu.VMEM((72, NL), F32)]
+        + [pltpu.VMEM((32, NL), F32), pltpu.VMEM((32, 16), jnp.int32), pltpu.VMEM((32, 16), F32)],
         compiler_params=pltpu.CompilerParams(vmem_limit_bytes=56 << 20),
         interpret=INTERPRET,
     )(*operands)

time: 49.1 us -> 48.7 us (level)
  waiting for transfers between devices: 3.21 us -> 2.57 us
    pallas_call x6, Pallas kernels: 5.43 us -> 6.04 us  [call(): pl.pallas_call(body, out_shape=[jax.ShapeDtypeStruct(s, F32) if k < away...]
    ppermute x1, waiting for transfers between devices: 0.67 us -> 0.08 us  [on_device(): yn = keep(lax.ppermute(yn, 'gy', near_y))]
  transfers between devices with their start and end apart: 6 -> 6, of which waited for: 2 -> 2; matrix products, arithmetic and copies ran while one was open for 0% -> 0% of each run, Pallas kernels for 1% -> 3%
where the time goes in v7:
time: 48.7 us; the launch traced here: 48.4 us
  starting transfers between devices  32.1 us (66%)
  Pallas kernels  7.58 us (16%)
  blocking collectives  5.43 us (11%)
  waiting for transfers between devices  2.57 us (5%)
  between operations  0.73 us (1%)
    ppermute x1, starting transfers between devices, on_device(): yf = keep(lax.ppermute(yf, 'gy', far_y))  14.1 us
    ppermute x1, starting transfers between devices, on_device(): bf = keep(lax.ppermute(bp, 'gx', far_x))  7.82 us
    pallas_call x6, Pallas kernels, call(): pl.pallas_call(body, out_shape=[jax.ShapeDtypeStruct(s, F32) if k < away...  6.04 us
    ppermute x1, starting transfers between devices, on_device(): af = keep(lax.ppermute(af, 'gx', far_x))  3.94 us
    all_gather x1, blocking collectives, on_device(): gn = keep(lax.all_gather(cn, 'gx', axis_index_groups=groups))  3.6 us
    ppermute x1, waiting for transfers between devices, on_device(): bf = keep(lax.ppermute(bp, 'gx', far_x))  2.48 us
    ppermute x1, starting transfers between devices, on_device(): an = keep(lax.ppermute(an, 'gx', near_x))  2.41 us
    ppermute x1, starting transfers between devices, on_device(): yn = keep(lax.ppermute(yn, 'gy', near_y))  1.92 us
  transfers between devices with their start and end apart: 6, of which 2 were waited for; matrix products, arithmetic and copies ran while one was open for 0% of the time, Pallas kernels for 3%

profile of v7, /device:TPU:57, one launch (start us, length us, event | category | flops | bytes accessed | tf_op | source)
XLA Modules:
  0.0 48.4 jit_solution(4540367331571678355)
XLA Ops:
  0.6 1.5 %shard_map.158 = (f32[3,8,16,128]{3,2,1,0:T(8,128)S(1)}, f32[3,8,16,128]{3,2,1,0:T(8,128)S(1)}, f32[8,16,128]{2,1,0:T(8,128)S(1)}, f32[3,4,8,128]{3,2,1,0:T(8,12...) custom-call(f32[3,8,16,128]{3,2,1,0:T(8,128)} %refs_0_.1, ...), custom_call_target="tpu_custom_call" | custom-call | tf_op jit(solution)/shard_map/pallas_call | solution.py:563
  2.2 14.1 %collective-permute-start.1 = (f32[344,128]{1,0:T(8,128)S(1)}, f32[344,128]{1,0:T(8,128)S(1)}, u32[]{:S(2)}, u32[]{:S(2)}) collective-permute-start(f32[344,128]{1,0:T(8,128)S(1)} %get-tuple-element.43), channel_id=1, source_target_pairs={{1,2},{2,1},{3,4},{4,3},{5,6},{6,5},{7,8},{8,7},{9,10},{10,9},{11,... | collective-permute-start | bytes 528392 | tf_op jit(solution)/shard_map/ppermute | solution.py:602
  16.3 1.9 %collective-permute-start = (f32[336,128]{1,0:T(8,128)S(1)}, f32[336,128]{1,0:T(8,128)S(1)}, u32[]{:S(2)}, u32[]{:S(2)}) collective-permute-start(f32[336,128]{1,0:T(8,128)S(1)} %get-tuple-element.42), channel_id=1, source_target_pairs={{0,1},{1,0},{2,3},{3,2},{4,5},{5,4},{6,7},{7,6},{8,9},{9,8},{10,11... | collective-permute-start | bytes 516104 | tf_op jit(solution)/shard_map/ppermute | solution.py:603
  18.2 0.9 %shard_map.159 = (f32[4,16,24,128]{3,2,1,0:T(8,128)S(1)}, f32[6,12,24,128]{3,2,1,0:T(8,128)S(1)}, f32[4,16,24,128]{3,2,1,0:T(8,128)S(1)}, f32[5,12,24,128]{3,2,1...) custom-call(f32[3,8,16,128]{3,2,1,0:T(8,128)S(1)} %get-tuple-element.28.fn, ...), custom_call_target="tpu_custom_call" | custom-call | tf_op jit(solution)/shard_map/pallas_call | solution.py:538
  19.1 3.9 %collective-permute-start.4 = (f32[664,128]{1,0:T(8,128)S(1)}, f32[664,128]{1,0:T(8,128)S(1)}, u32[]{:S(2)}, u32[]{:S(2)}) collective-permute-start(f32[664,128]{1,0:T(8,128)S(1)} %get-tuple-element.51), channel_id=1, source_target_pairs={{16,32},{32,16},{48,64},{64,48},{80,96},{96,80},{112,128},{128,112... | collective-permute-start | bytes 1019912 | tf_op jit(solution)/shard_map/ppermute | solution.py:606
  23.0 0.1 collective-permute-done.rn.yn
  23.1 0.0 collective-permute-done.1.rf.yf
  23.1 3.6 %all-gather = f32[816,128]{1,0:T(8,128)S(1)} all-gather(f32[408,128]{1,0:T(8,128)S(1)} %shard_map.160), channel_id=2, replica_groups={{0,16},{32,48},{64,80},{96,112},{128,144},{160,176},{192,208},{224,240}..., dimensions={0}, use_global_device_ids=true | all-gather | bytes 626688 | tf_op jit(solution)/shard_map/all_gather | solution.py:610
  26.7 0.1 shard_map.161._____
  26.8 7.8 %collective-permute-start.5 = (f32[424,128]{1,0:T(8,128)S(1)}, f32[424,128]{1,0:T(8,128)S(1)}, u32[]{:S(2)}, u32[]{:S(2)}) collective-permute-start(f32[424,128]{1,0:T(8,128)S(1)} %shard_map.161._____), channel_id=1, source_target_pairs={{16,32},{32,16},{48,64},{64,48},{80,96},{96,80},{112,128},{128,112... | collective-permute-start | bytes 651272 | tf_op jit(solution)/shard_map/ppermute | solution.py:613
  34.6 1.9 %collective-permute-start.3 = (f32[408,128]{1,0:T(8,128)S(1)}, f32[408,128]{1,0:T(8,128)S(1)}, u32[]{:S(2)}, u32[]{:S(2)}) collective-permute-start(f32[408,128]{1,0:T(8,128)S(1)} %get-tuple-element.50), channel_id=1, source_target_pairs={{0,16},{16,0},{32,48},{48,32},{64,80},{80,64},{96,112},{112,96},{1... | collective-permute-start | bytes 626696 | tf_op jit(solution)/shard_map/ppermute | solution.py:608
  36.5 2.4 %collective-permute-start.2 = (f32[256,128]{1,0:T(8,128)S(1)}, f32[256,128]{1,0:T(8,128)S(1)}, u32[]{:S(2)}, u32[]{:S(2)}) collective-permute-start(f32[256,128]{1,0:T(8,128)S(1)} %get-tuple-element.49), channel_id=1, source_target_pairs={{0,16},{16,0},{32,48},{48,32},{64,80},{80,64},{96,112},{112,96},{1... | collective-permute-start | bytes 393224 | tf_op jit(solution)/shard_map/ppermute | solution.py:607
  39.0 0.2 shard_map.162
  39.2 0.0 collective-permute-done.4.a.af
  39.2 2.5 %collective-permute-done.5.c.bf = f32[424,128]{1,0:T(8,128)S(1)} collective-permute-done((f32[424,128]{1,0:T(8,128)S(1)}, f32[424,128]{1,0:T(8,128)S(1)}, u32[]{:S(2)}, u32[]{:S(2)}) %collective-permute-start.5) | collective-permute-done | bytes 217120 | tf_op jit(solution)/shard_map/ppermute | solution.py:613
  41.6 0.0 copy-start
  41.6 0.1 shard_map.163
  41.7 1.8 %all-gather.1 = f32[48,128]{1,0:T(8,128)S(1)} all-gather(f32[24,128]{1,0:T(8,128)S(1)} %shard_map.163), channel_id=3, replica_groups={{0,16},{32,48},{64,80},{96,112},{128,144},{160,176},{192,208},{224,240}..., dimensions={0}, use_global_device_ids=true | all-gather | bytes 36864 | tf_op jit(solution)/shard_map/all_gather | solution.py:617
  43.6 0.0 collective-permute-done.2.an
  43.6 0.0 collective-permute-done.3.am
  43.6 0.0 copy-done
  43.6 4.8 %shard_map.164 = (f32[3,8,16,128]{3,2,1,0:T(8,128)}, f32[3,4,8,128]{3,2,1,0:T(8,128)}, f32[4,16,24,128]{3,2,1,0:T(8,128)S(1)}, f32[6,12,24,128]{3,2,1,0:T(8,128)...) custom-call(f32[4,16,24,128]{3,2,1,0:T(8,128)S(1)} %get-tuple-elemen, ...), custom_call_target="tpu_custom_call", output_to_operand_aliasing={{2}: (0, {}), {3}: (1, {}), {4}: (2, {}), {5}: (3, {})} | custom-call | tf_op jit(solution)/shard_map/pallas_call | solution.py:538
  (1 shorter events, 0.0 us)
Async XLA Ops:
  2.2 20.9 %collective-permute-start.1 = (f32[344,128]{1,0:T(8,128)S(1)}, f32[344,128]{1,0:T(8,128)S(1)}, u32[]{:S(2)}, u32[]{:S(2)}) collective-permute-start(f32[344,128]{1,0:T(8,128)S(1)} %get-tuple-element.43), channel_id=1, source_target_pairs={{1,2},{2,1},{3,4},{4,3},{5,6},{6,5},{7,8},{8,7},{9,10},{10,9},{11,... | collective-permute-start | bytes 528392 | tf_op jit(solution)/shard_map/ppermute | solution.py:602
  16.3 6.8 %collective-permute-start = (f32[336,128]{1,0:T(8,128)S(1)}, f32[336,128]{1,0:T(8,128)S(1)}, u32[]{:S(2)}, u32[]{:S(2)}) collective-permute-start(f32[336,128]{1,0:T(8,128)S(1)} %get-tuple-element.42), channel_id=1, source_target_pairs={{0,1},{1,0},{2,3},{3,2},{4,5},{5,4},{6,7},{7,6},{8,9},{9,8},{10,11... | collective-permute-start | bytes 516104 | tf_op jit(solution)/shard_map/ppermute | solution.py:603
  19.1 20.1 %collective-permute-start.4 = (f32[664,128]{1,0:T(8,128)S(1)}, f32[664,128]{1,0:T(8,128)S(1)}, u32[]{:S(2)}, u32[]{:S(2)}) collective-permute-start(f32[664,128]{1,0:T(8,128)S(1)} %get-tuple-element.51), channel_id=1, source_target_pairs={{16,32},{32,16},{48,64},{64,48},{80,96},{96,80},{112,128},{128,112... | collective-permute-start | bytes 1019912 | tf_op jit(solution)/shard_map/ppermute | solution.py:606
  26.8 14.9 %collective-permute-start.5 = (f32[424,128]{1,0:T(8,128)S(1)}, f32[424,128]{1,0:T(8,128)S(1)}, u32[]{:S(2)}, u32[]{:S(2)}) collective-permute-start(f32[424,128]{1,0:T(8,128)S(1)} %shard_map.161._____), channel_id=1, source_target_pairs={{16,32},{32,16},{48,64},{64,48},{80,96},{96,80},{112,128},{128,112... | collective-permute-start | bytes 651272 | tf_op jit(solution)/shard_map/ppermute | solution.py:613
  34.6 8.9 %collective-permute-start.3 = (f32[408,128]{1,0:T(8,128)S(1)}, f32[408,128]{1,0:T(8,128)S(1)}, u32[]{:S(2)}, u32[]{:S(2)}) collective-permute-start(f32[408,128]{1,0:T(8,128)S(1)} %get-tuple-element.50), channel_id=1, source_target_pairs={{0,16},{16,0},{32,48},{48,32},{64,80},{80,64},{96,112},{112,96},{1... | collective-permute-start | bytes 626696 | tf_op jit(solution)/shard_map/ppermute | solution.py:608
  36.5 7.0 %collective-permute-start.2 = (f32[256,128]{1,0:T(8,128)S(1)}, f32[256,128]{1,0:T(8,128)S(1)}, u32[]{:S(2)}, u32[]{:S(2)}) collective-permute-start(f32[256,128]{1,0:T(8,128)S(1)} %get-tuple-element.49), channel_id=1, source_target_pairs={{0,16},{16,0},{32,48},{48,32},{64,80},{80,64},{96,112},{112,96},{1... | collective-permute-start | bytes 393224 | tf_op jit(solution)/shard_map/ppermute | solution.py:607
  41.6 1.9 %copy-start = (bf16[256,128]{1,0:T(8,128)(2,1)S(1)}, bf16[256,128]{1,0:T(8,128)(2,1)}, u32[]{:S(2)}) copy-start(bf16[256,128]{1,0:T(8,128)(2,1)} %constant.2.clone.table_ref) | copy-start | bytes 196612

commit v8 on v7

--- a/solution.py
+++ b/solution.py
@@ -9,10 +9,10 @@
 
 DT2 = 0.0625
 NL = 128
-Y_ROWS, A_ROWS, C_ROWS, R_ROWS, O_ROWS = 336, 664, 400, 24, 8
-YB, YC, YD, YT = 128, 224, 288, 328
+Y_ROWS, A_ROWS, C_ROWS, R_ROWS, O_ROWS = 328, 664, 400, 24, 8
+YB, YW, YC, YD, YT = 128, 208, 216, 280, 320
 AB, AC, AD, AT = 256, 448, 576, 656
-CB_, CC, CD, CT, CS = 64, 88, 152, 192, 200
+CB_, CW, CC, CD, CT, CS = 64, 84, 88, 152, 192, 200
 F32 = jnp.float32
 
 
@@ -80,15 +80,14 @@
         for x in range(8):
             v = fn[i, x] if i < 3 else fj[x] * (1.0 / 12.0)
             out[i * 32 + x * 4 : i * 32 + x * 4 + 4] = v[0:4] if low else v[12:16]
-    for i in range(6):
+    for i in range(5):
         for x in range(8):
-            if i < 5:
-                v = fp[i, x] if i < 3 else fo[i - 3, x]
-                v = v[0:2] if low else v[14:16]
-            else:
-                v = edge[x * 4 : x * 4 + 2] if low else edge[x * 4 + 2 : x * 4 + 4]
-                v = pltpu.roll(v, 8 if low else 120, 1)
-            out[YB + i * 16 + x * 2 : YB + i * 16 + x * 2 + 2] = v
+            v = fp[i, x] if i < 3 else fo[i - 3, x]
+            out[YB + i * 16 + x * 2 : YB + i * 16 + x * 2 + 2] = v[0:2] if low else v[14:16]
+    for x in range(8):
+        o = x * 4 if low else x * 4 + 2
+        one, two = edge[o : o + 1], edge[o + 1 : o + 2]
+        out[YW + x : YW + x + 1] = one + pltpu.roll(two, 8, 1) if low else pltpu.roll(one, NL - 8, 1) + two
     for i in range(4):
         for x in range(4):
             v = cn[i, x] if i < 3 else cj[x] * (1.0 / 12.0)
@@ -199,9 +198,11 @@
     for i in range(4):
         o = i * 32 + (0 if low else 16)
         out[base + i * 16 : base + i * 16 + 16] = src[o : o + 16]
-    for i in range(6):
+    for i in range(5):
         o = YB + i * 16 + (0 if low else 12)
         out[base + CB_ + i * 4 : base + CB_ + i * 4 + 4] = src[o : o + 4]
+    o = YW + (0 if low else 6)
+    out[base + CW : base + CC] = jnp.concatenate([src[o : o + 2]] * 2, 0)
     out[base + CC : base + CS] = src[YC:Y_ROWS]
 
 
@@ -328,6 +329,14 @@
     return (20, 20, 16, 20, 16, 18) if high else (0, 2, 4, 2, 6, 4)
 
 
+def mixing_rows(row, high):
+    first_half = lax.broadcasted_iota(jnp.int32, (1, NL), 1) % 16 < 8
+    one, two = jnp.where(first_half, row, 0.0), jnp.where(first_half, 0.0, row)
+    if high:
+        return pltpu.roll(one, 8, 1), two
+    return one, pltpu.roll(two, NL - 8, 1)
+
+
 def unpack_y(src, high, fe, fb, ce, cb):
     t4, t2, k4, k2, k1, k3 = y_places(high)
     top = src[YT:Y_ROWS]
@@ -339,10 +348,12 @@
             o = YC + i * 16 + x * 4
             ce[i, 6 + x, k4 : k4 + 4] = src[o : o + 4]
             ce[i, 6 + x, k2 : k2 + 2] = v[x * 2 : x * 2 + 2]
-    for i in range(6):
-        for x in range(8):
+    for x in range(8):
+        for i in range(5):
             o = YB + i * 16 + x * 2
             fb[i, 2 + x, t2 : t2 + 2] = src[o : o + 2]
+        for y, v in enumerate(mixing_rows(src[YW + x : YW + x + 1], high)):
+            fb[5, 2 + x, t2 + y : t2 + y + 1] = v
     for i in range(5):
         v = top_of(top, 4 + i)
         for x in range(4):
@@ -364,10 +375,12 @@
             o = q + CC + i * 16 + x * 4
             ce[i, c4 + x, k4 : k4 + 4] = c[o : o + 4]
             ce[i, c4 + x, k2 : k2 + 2] = v[x * 2 : x * 2 + 2]
-    for i in range(6):
-        for x in range(2):
+    for x in range(2):
+        for i in range(5):
             o = q + CB_ + i * 4 + x * 2
             fb[i, f2 + x, t2 : t2 + 2] = c[o : o + 2]
+        for y, v in enumerate(mixing_rows(c[q + CW + x : q + CW + x + 1], high)):
+            fb[5, f2 + x, t2 + y : t2 + y + 1] = v
     for i in range(5):
         v = top_of(top, 4 + i)
         for x in range(4):

time: 48.7 us -> 48.7 us (level)
  transfers between devices with their start and end apart: 6 -> 6, of which waited for: 2 -> 1; matrix products, arithmetic and copies ran while one was open for 0% -> 0% of each run, Pallas kernels for 3% -> 3%
where the time goes in v8:
time: 48.7 us; the launch traced here: 48.1 us
  starting transfers between devices  31.9 us (66%)
  Pallas kernels  7.62 us (16%)
  blocking collectives  5.38 us (11%)
  waiting for transfers between devices  2.5 us (5%)
  between operations  0.75 us (2%)
    ppermute x1, starting transfers between devices, on_device(): yf = keep(lax.ppermute(yf, 'gy', far_y))  14.1 us
    ppermute x1, starting transfers between devices, on_device(): bf = keep(lax.ppermute(bp, 'gx', far_x))  7.63 us
    pallas_call x6, Pallas kernels, call(): pl.pallas_call(body, out_shape=[jax.ShapeDtypeStruct(s, F32) if k < away...  6.08 us
    ppermute x1, starting transfers between devices, on_device(): af = keep(lax.ppermute(af, 'gx', far_x))  3.94 us
    all_gather x1, blocking collectives, on_device(): gn = keep(lax.all_gather(cn, 'gx', axis_index_groups=groups))  3.55 us
    ppermute x1, waiting for transfers between devices, on_device(): bf = keep(lax.ppermute(bp, 'gx', far_x))  2.49 us
    ppermute x1, starting transfers between devices, on_device(): an = keep(lax.ppermute(an, 'gx', near_x))  2.41 us
    ppermute x1, starting transfers between devices, on_device(): yn = keep(lax.ppermute(yn, 'gy', near_y))  1.92 us
  transfers between devices with their start and end apart: 6, of which 1 were waited for; matrix products, arithmetic and copies ran while one was open for 0% of the time, Pallas kernels for 3%

profile of v8, /device:TPU:57, one launch (start us, length us, event | category | flops | bytes accessed | tf_op | source)
XLA Modules:
  0.0 48.1 jit_solution(1084371728140522070)
XLA Ops:
  0.6 1.5 %shard_map.158 = (f32[3,8,16,128]{3,2,1,0:T(8,128)S(1)}, f32[3,8,16,128]{3,2,1,0:T(8,128)S(1)}, f32[8,16,128]{2,1,0:T(8,128)S(1)}, f32[3,4,8,128]{3,2,1,0:T(8,12...) custom-call(f32[3,8,16,128]{3,2,1,0:T(8,128)} %refs_0_.1, ...), custom_call_target="tpu_custom_call" | custom-call | tf_op jit(solution)/shard_map/pallas_call | solution.py:576
  2.2 14.1 %collective-permute-start.1 = (f32[336,128]{1,0:T(8,128)S(1)}, f32[336,128]{1,0:T(8,128)S(1)}, u32[]{:S(2)}, u32[]{:S(2)}) collective-permute-start(f32[336,128]{1,0:T(8,128)S(1)} %get-tuple-element.43), channel_id=1, source_target_pairs={{1,2},{2,1},{3,4},{4,3},{5,6},{6,5},{7,8},{8,7},{9,10},{10,9},{11,... | collective-permute-start | bytes 516104 | tf_op jit(solution)/shard_map/ppermute | solution.py:615
  16.3 1.9 %collective-permute-start = (f32[328,128]{1,0:T(8,128)S(1)}, f32[328,128]{1,0:T(8,128)S(1)}, u32[]{:S(2)}, u32[]{:S(2)}) collective-permute-start(f32[328,128]{1,0:T(8,128)S(1)} %get-tuple-element.42), channel_id=1, source_target_pairs={{0,1},{1,0},{2,3},{3,2},{4,5},{5,4},{6,7},{7,6},{8,9},{9,8},{10,11... | collective-permute-start | bytes 503816 | tf_op jit(solution)/shard_map/ppermute | solution.py:616
  18.2 0.9 %shard_map.159 = (f32[4,16,24,128]{3,2,1,0:T(8,128)S(1)}, f32[6,12,24,128]{3,2,1,0:T(8,128)S(1)}, f32[4,16,24,128]{3,2,1,0:T(8,128)S(1)}, f32[5,12,24,128]{3,2,1...) custom-call(f32[3,8,16,128]{3,2,1,0:T(8,128)S(1)} %get-tuple-element.28.fn, ...), custom_call_target="tpu_custom_call" | custom-call | tf_op jit(solution)/shard_map/pallas_call | solution.py:551
  19.1 3.9 %collective-permute-start.4 = (f32[664,128]{1,0:T(8,128)S(1)}, f32[664,128]{1,0:T(8,128)S(1)}, u32[]{:S(2)}, u32[]{:S(2)}) collective-permute-start(f32[664,128]{1,0:T(8,128)S(1)} %get-tuple-element.51), channel_id=1, source_target_pairs={{16,32},{32,16},{48,64},{64,48},{80,96},{96,80},{112,128},{128,112... | collective-permute-start | bytes 1019912 | tf_op jit(solution)/shard_map/ppermute | solution.py:619
  23.0 0.0 collective-permute-done.rn.yn
  23.0 0.0 collective-permute-done.1.rf.yf
  23.1 3.6 %all-gather = f32[816,128]{1,0:T(8,128)S(1)} all-gather(f32[408,128]{1,0:T(8,128)S(1)} %shard_map.160), channel_id=2, replica_groups={{0,16},{32,48},{64,80},{96,112},{128,144},{160,176},{192,208},{224,240}..., dimensions={0}, use_global_device_ids=true | all-gather | bytes 626688 | tf_op jit(solution)/shard_map/all_gather | solution.py:623
  26.6 0.1 shard_map.161._____
  26.7 7.6 %collective-permute-start.5 = (f32[424,128]{1,0:T(8,128)S(1)}, f32[424,128]{1,0:T(8,128)S(1)}, u32[]{:S(2)}, u32[]{:S(2)}) collective-permute-start(f32[424,128]{1,0:T(8,128)S(1)} %shard_map.161._____), channel_id=1, source_target_pairs={{16,32},{32,16},{48,64},{64,48},{80,96},{96,80},{112,128},{128,112... | collective-permute-start | bytes 651272 | tf_op jit(solution)/shard_map/ppermute | solution.py:626
  34.3 1.9 %collective-permute-start.3 = (f32[408,128]{1,0:T(8,128)S(1)}, f32[408,128]{1,0:T(8,128)S(1)}, u32[]{:S(2)}, u32[]{:S(2)}) collective-permute-start(f32[408,128]{1,0:T(8,128)S(1)} %get-tuple-element.50), channel_id=1, source_target_pairs={{0,16},{16,0},{32,48},{48,32},{64,80},{80,64},{96,112},{112,96},{1... | collective-permute-start | bytes 626696 | tf_op jit(solution)/shard_map/ppermute | solution.py:621
  36.3 2.4 %collective-permute-start.2 = (f32[256,128]{1,0:T(8,128)S(1)}, f32[256,128]{1,0:T(8,128)S(1)}, u32[]{:S(2)}, u32[]{:S(2)}) collective-permute-start(f32[256,128]{1,0:T(8,128)S(1)} %get-tuple-element.49), channel_id=1, source_target_pairs={{0,16},{16,0},{32,48},{48,32},{64,80},{80,64},{96,112},{112,96},{1... | collective-permute-start | bytes 393224 | tf_op jit(solution)/shard_map/ppermute | solution.py:620
  38.7 0.2 shard_map.162
  38.9 0.0 collective-permute-done.4.a.af
  38.9 2.5 %collective-permute-done.5.c.bf = f32[424,128]{1,0:T(8,128)S(1)} collective-permute-done((f32[424,128]{1,0:T(8,128)S(1)}, f32[424,128]{1,0:T(8,128)S(1)}, u32[]{:S(2)}, u32[]{:S(2)}) %collective-permute-start.5) | collective-permute-done | bytes 217120 | tf_op jit(solution)/shard_map/ppermute | solution.py:626
  41.4 0.0 copy-start
  41.4 0.1 shard_map.163
  41.5 1.8 %all-gather.1 = f32[48,128]{1,0:T(8,128)S(1)} all-gather(f32[24,128]{1,0:T(8,128)S(1)} %shard_map.163), channel_id=3, replica_groups={{0,16},{32,48},{64,80},{96,112},{128,144},{160,176},{192,208},{224,240}..., dimensions={0}, use_global_device_ids=true | all-gather | bytes 36864 | tf_op jit(solution)/shard_map/all_gather | solution.py:630
  43.3 0.0 collective-permute-done.2.an
  43.3 0.0 collective-permute-done.3.am
  43.3 0.0 copy-done
  43.3 4.8 %shard_map.164 = (f32[3,8,16,128]{3,2,1,0:T(8,128)}, f32[3,4,8,128]{3,2,1,0:T(8,128)}, f32[4,16,24,128]{3,2,1,0:T(8,128)S(1)}, f32[6,12,24,128]{3,2,1,0:T(8,128)...) custom-call(f32[4,16,24,128]{3,2,1,0:T(8,128)S(1)} %get-tuple-elemen, ...), custom_call_target="tpu_custom_call", output_to_operand_aliasing={{2}: (0, {}), {3}: (1, {}), {4}: (2, {}), {5}: (3, {})} | custom-call | tf_op jit(solution)/shard_map/pallas_call | solution.py:551
  (1 shorter events, 0.0 us)
Async XLA Ops:
  2.2 20.8 %collective-permute-start.1 = (f32[336,128]{1,0:T(8,128)S(1)}, f32[336,128]{1,0:T(8,128)S(1)}, u32[]{:S(2)}, u32[]{:S(2)}) collective-permute-start(f32[336,128]{1,0:T(8,128)S(1)} %get-tuple-element.43), channel_id=1, source_target_pairs={{1,2},{2,1},{3,4},{4,3},{5,6},{6,5},{7,8},{8,7},{9,10},{10,9},{11,... | collective-permute-start | bytes 516104 | tf_op jit(solution)/shard_map/ppermute | solution.py:615
  16.3 6.7 %collective-permute-start = (f32[328,128]{1,0:T(8,128)S(1)}, f32[328,128]{1,0:T(8,128)S(1)}, u32[]{:S(2)}, u32[]{:S(2)}) collective-permute-start(f32[328,128]{1,0:T(8,128)S(1)} %get-tuple-element.42), channel_id=1, source_target_pairs={{0,1},{1,0},{2,3},{3,2},{4,5},{5,4},{6,7},{7,6},{8,9},{9,8},{10,11... | collective-permute-start | bytes 503816 | tf_op jit(solution)/shard_map/ppermute | solution.py:616
  19.1 19.8 %collective-permute-start.4 = (f32[664,128]{1,0:T(8,128)S(1)}, f32[664,128]{1,0:T(8,128)S(1)}, u32[]{:S(2)}, u32[]{:S(2)}) collective-permute-start(f32[664,128]{1,0:T(8,128)S(1)} %get-tuple-element.51), channel_id=1, source_target_pairs={{16,32},{32,16},{48,64},{64,48},{80,96},{96,80},{112,128},{128,112... | collective-permute-start | bytes 1019912 | tf_op jit(solution)/shard_map/ppermute | solution.py:619
  26.7 14.7 %collective-permute-start.5 = (f32[424,128]{1,0:T(8,128)S(1)}, f32[424,128]{1,0:T(8,128)S(1)}, u32[]{:S(2)}, u32[]{:S(2)}) collective-permute-start(f32[424,128]{1,0:T(8,128)S(1)} %shard_map.161._____), channel_id=1, source_target_pairs={{16,32},{32,16},{48,64},{64,48},{80,96},{96,80},{112,128},{128,112... | collective-permute-start | bytes 651272 | tf_op jit(solution)/shard_map/ppermute | solution.py:626
  34.3 9.0 %collective-permute-start.3 = (f32[408,128]{1,0:T(8,128)S(1)}, f32[408,128]{1,0:T(8,128)S(1)}, u32[]{:S(2)}, u32[]{:S(2)}) collective-permute-start(f32[408,128]{1,0:T(8,128)S(1)} %get-tuple-element.50), channel_id=1, source_target_pairs={{0,16},{16,0},{32,48},{48,32},{64,80},{80,64},{96,112},{112,96},{1... | collective-permute-start | bytes 626696 | tf_op jit(solution)/shard_map/ppermute | solution.py:621
  36.3 7.0 %collective-permute-start.2 = (f32[256,128]{1,0:T(8,128)S(1)}, f32[256,128]{1,0:T(8,128)S(1)}, u32[]{:S(2)}, u32[]{:S(2)}) collective-permute-start(f32[256,128]{1,0:T(8,128)S(1)} %get-tuple-element.49), channel_id=1, source_target_pairs={{0,16},{16,0},{32,48},{48,32},{64,80},{80,64},{96,112},{112,96},{1... | collective-permute-start | bytes 393224 | tf_op jit(solution)/shard_map/ppermute | solution.py:620
  41.4 1.9 %copy-start = (bf16[256,128]{1,0:T(8,128)(2,1)S(1)}, bf16[256,128]{1,0:T(8,128)(2,1)}, u32[]{:S(2)}) copy-start(bf16[256,128]{1,0:T(8,128)(2,1)} %constant.2.clone.table_ref) | copy-start | bytes 196612

commit v9 on v8

--- a/solution.py
+++ b/solution.py
@@ -296,9 +296,8 @@
         yy1 = second(m2, m1, v, p1, p2, s2)
         work[4, x] = yy1
         work[5, x] = yy1 + first(*shifted(t), s1)
-    work[2, 0:n] = lift[2 : 2 + n]
     for c in range(4):
-        g = vertical(rows(work[c, 0:n]), table)
+        g = vertical(rows(lift[2 : 2 + n] if c == 2 else work[c, 0:n]), table)
         work[c, 0:n] = (rows(j(2, n)) * g).reshape(n, 24, NL)
     for x in range(n):
         col = [[u(c, x + k, None) for k in range(5)] for c in range(3)]

time: 48.7 us -> 48.7 us (level)
  no operation moved by 1% of the time
where the time goes in v9:
time: 48.7 us; the launch traced here: 48.1 us
  starting transfers between devices  31.9 us (66%)
  Pallas kernels  7.62 us (16%)
  blocking collectives  5.38 us (11%)
  waiting for transfers between devices  2.5 us (5%)
  between operations  0.75 us (2%)
    ppermute x1, starting transfers between devices, on_device(): yf = keep(lax.ppermute(yf, 'gy', far_y))  14.1 us
    ppermute x1, starting transfers between devices, on_device(): bf = keep(lax.ppermute(bp, 'gx', far_x))  7.63 us
    pallas_call x6, Pallas kernels, call(): pl.pallas_call(body, out_shape=[jax.ShapeDtypeStruct(s, F32) if k < away...  6.08 us
    ppermute x1, starting transfers between devices, on_device(): af = keep(lax.ppermute(af, 'gx', far_x))  3.94 us
    all_gather x1, blocking collectives, on_device(): gn = keep(lax.all_gather(cn, 'gx', axis_index_groups=groups))  3.55 us
    ppermute x1, waiting for transfers between devices, on_device(): bf = keep(lax.ppermute(bp, 'gx', far_x))  2.49 us
    ppermute x1, starting transfers between devices, on_device(): an = keep(lax.ppermute(an, 'gx', near_x))  2.41 us
    ppermute x1, starting transfers between devices, on_device(): yn = keep(lax.ppermute(yn, 'gy', near_y))  1.92 us
  transfers between devices with their start and end apart: 6, of which 1 were waited for; matrix products, arithmetic and copies ran while one was open for 0% of the time, Pallas kernels for 3%

profile of v9, /device:TPU:57, one launch (start us, length us, event | category | flops | bytes accessed | tf_op | source)
XLA Modules:
  0.0 48.1 jit_solution(1084371728140522070)
XLA Ops:
  0.6 1.5 %shard_map.158 = (f32[3,8,16,128]{3,2,1,0:T(8,128)S(1)}, f32[3,8,16,128]{3,2,1,0:T(8,128)S(1)}, f32[8,16,128]{2,1,0:T(8,128)S(1)}, f32[3,4,8,128]{3,2,1,0:T(8,12...) custom-call(f32[3,8,16,128]{3,2,1,0:T(8,128)} %refs_0_.1, ...), custom_call_target="tpu_custom_call" | custom-call | tf_op jit(solution)/shard_map/pallas_call | solution.py:575
  2.2 14.1 %collective-permute-start.1 = (f32[336,128]{1,0:T(8,128)S(1)}, f32[336,128]{1,0:T(8,128)S(1)}, u32[]{:S(2)}, u32[]{:S(2)}) collective-permute-start(f32[336,128]{1,0:T(8,128)S(1)} %get-tuple-element.43), channel_id=1, source_target_pairs={{1,2},{2,1},{3,4},{4,3},{5,6},{6,5},{7,8},{8,7},{9,10},{10,9},{11,... | collective-permute-start | bytes 516104 | tf_op jit(solution)/shard_map/ppermute | solution.py:614
  16.3 1.9 %collective-permute-start = (f32[328,128]{1,0:T(8,128)S(1)}, f32[328,128]{1,0:T(8,128)S(1)}, u32[]{:S(2)}, u32[]{:S(2)}) collective-permute-start(f32[328,128]{1,0:T(8,128)S(1)} %get-tuple-element.42), channel_id=1, source_target_pairs={{0,1},{1,0},{2,3},{3,2},{4,5},{5,4},{6,7},{7,6},{8,9},{9,8},{10,11... | collective-permute-start | bytes 503816 | tf_op jit(solution)/shard_map/ppermute | solution.py:615
  18.2 0.9 %shard_map.159 = (f32[4,16,24,128]{3,2,1,0:T(8,128)S(1)}, f32[6,12,24,128]{3,2,1,0:T(8,128)S(1)}, f32[4,16,24,128]{3,2,1,0:T(8,128)S(1)}, f32[5,12,24,128]{3,2,1...) custom-call(f32[3,8,16,128]{3,2,1,0:T(8,128)S(1)} %get-tuple-element.28.fn, ...), custom_call_target="tpu_custom_call" | custom-call | tf_op jit(solution)/shard_map/pallas_call | solution.py:550
  19.1 3.9 %collective-permute-start.4 = (f32[664,128]{1,0:T(8,128)S(1)}, f32[664,128]{1,0:T(8,128)S(1)}, u32[]{:S(2)}, u32[]{:S(2)}) collective-permute-start(f32[664,128]{1,0:T(8,128)S(1)} %get-tuple-element.51), channel_id=1, source_target_pairs={{16,32},{32,16},{48,64},{64,48},{80,96},{96,80},{112,128},{128,112... | collective-permute-start | bytes 1019912 | tf_op jit(solution)/shard_map/ppermute | solution.py:618
  23.0 0.0 collective-permute-done.rn.yn
  23.0 0.0 collective-permute-done.1.rf.yf
  23.1 3.6 %all-gather = f32[816,128]{1,0:T(8,128)S(1)} all-gather(f32[408,128]{1,0:T(8,128)S(1)} %shard_map.160), channel_id=2, replica_groups={{0,16},{32,48},{64,80},{96,112},{128,144},{160,176},{192,208},{224,240}..., dimensions={0}, use_global_device_ids=true | all-gather | bytes 626688 | tf_op jit(solution)/shard_map/all_gather | solution.py:622
  26.6 0.1 shard_map.161._____
  26.7 7.6 %collective-permute-start.5 = (f32[424,128]{1,0:T(8,128)S(1)}, f32[424,128]{1,0:T(8,128)S(1)}, u32[]{:S(2)}, u32[]{:S(2)}) collective-permute-start(f32[424,128]{1,0:T(8,128)S(1)} %shard_map.161._____), channel_id=1, source_target_pairs={{16,32},{32,16},{48,64},{64,48},{80,96},{96,80},{112,128},{128,112... | collective-permute-start | bytes 651272 | tf_op jit(solution)/shard_map/ppermute | solution.py:625
  34.3 1.9 %collective-permute-start.3 = (f32[408,128]{1,0:T(8,128)S(1)}, f32[408,128]{1,0:T(8,128)S(1)}, u32[]{:S(2)}, u32[]{:S(2)}) collective-permute-start(f32[408,128]{1,0:T(8,128)S(1)} %get-tuple-element.50), channel_id=1, source_target_pairs={{0,16},{16,0},{32,48},{48,32},{64,80},{80,64},{96,112},{112,96},{1... | collective-permute-start | bytes 626696 | tf_op jit(solution)/shard_map/ppermute | solution.py:620
  36.3 2.4 %collective-permute-start.2 = (f32[256,128]{1,0:T(8,128)S(1)}, f32[256,128]{1,0:T(8,128)S(1)}, u32[]{:S(2)}, u32[]{:S(2)}) collective-permute-start(f32[256,128]{1,0:T(8,128)S(1)} %get-tuple-element.49), channel_id=1, source_target_pairs={{0,16},{16,0},{32,48},{48,32},{64,80},{80,64},{96,112},{112,96},{1... | collective-permute-start | bytes 393224 | tf_op jit(solution)/shard_map/ppermute | solution.py:619
  38.7 0.2 shard_map.162
  38.9 0.0 collective-permute-done.4.a.af
  38.9 2.5 %collective-permute-done.5.c.bf = f32[424,128]{1,0:T(8,128)S(1)} collective-permute-done((f32[424,128]{1,0:T(8,128)S(1)}, f32[424,128]{1,0:T(8,128)S(1)}, u32[]{:S(2)}, u32[]{:S(2)}) %collective-permute-start.5) | collective-permute-done | bytes 217120 | tf_op jit(solution)/shard_map/ppermute | solution.py:625
  41.4 0.0 copy-start
  41.4 0.1 shard_map.163
  41.5 1.8 %all-gather.1 = f32[48,128]{1,0:T(8,128)S(1)} all-gather(f32[24,128]{1,0:T(8,128)S(1)} %shard_map.163), channel_id=3, replica_groups={{0,16},{32,48},{64,80},{96,112},{128,144},{160,176},{192,208},{224,240}..., dimensions={0}, use_global_device_ids=true | all-gather | bytes 36864 | tf_op jit(solution)/shard_map/all_gather | solution.py:629
  43.3 0.0 collective-permute-done.2.an
  43.3 0.0 collective-permute-done.3.am
  43.3 0.0 copy-done
  43.3 4.8 %shard_map.164 = (f32[3,8,16,128]{3,2,1,0:T(8,128)}, f32[3,4,8,128]{3,2,1,0:T(8,128)}, f32[4,16,24,128]{3,2,1,0:T(8,128)S(1)}, f32[6,12,24,128]{3,2,1,0:T(8,128)...) custom-call(f32[4,16,24,128]{3,2,1,0:T(8,128)S(1)} %get-tuple-elemen, ...), custom_call_target="tpu_custom_call", output_to_operand_aliasing={{2}: (0, {}), {3}: (1, {}), {4}: (2, {}), {5}: (3, {})} | custom-call | tf_op jit(solution)/shard_map/pallas_call | solution.py:550
  (1 shorter events, 0.0 us)
Async XLA Ops:
  2.2 20.8 %collective-permute-start.1 = (f32[336,128]{1,0:T(8,128)S(1)}, f32[336,128]{1,0:T(8,128)S(1)}, u32[]{:S(2)}, u32[]{:S(2)}) collective-permute-start(f32[336,128]{1,0:T(8,128)S(1)} %get-tuple-element.43), channel_id=1, source_target_pairs={{1,2},{2,1},{3,4},{4,3},{5,6},{6,5},{7,8},{8,7},{9,10},{10,9},{11,... | collective-permute-start | bytes 516104 | tf_op jit(solution)/shard_map/ppermute | solution.py:614
  16.3 6.7 %collective-permute-start = (f32[328,128]{1,0:T(8,128)S(1)}, f32[328,128]{1,0:T(8,128)S(1)}, u32[]{:S(2)}, u32[]{:S(2)}) collective-permute-start(f32[328,128]{1,0:T(8,128)S(1)} %get-tuple-element.42), channel_id=1, source_target_pairs={{0,1},{1,0},{2,3},{3,2},{4,5},{5,4},{6,7},{7,6},{8,9},{9,8},{10,11... | collective-permute-start | bytes 503816 | tf_op jit(solution)/shard_map/ppermute | solution.py:615
  19.1 19.8 %collective-permute-start.4 = (f32[664,128]{1,0:T(8,128)S(1)}, f32[664,128]{1,0:T(8,128)S(1)}, u32[]{:S(2)}, u32[]{:S(2)}) collective-permute-start(f32[664,128]{1,0:T(8,128)S(1)} %get-tuple-element.51), channel_id=1, source_target_pairs={{16,32},{32,16},{48,64},{64,48},{80,96},{96,80},{112,128},{128,112... | collective-permute-start | bytes 1019912 | tf_op jit(solution)/shard_map/ppermute | solution.py:618
  26.7 14.7 %collective-permute-start.5 = (f32[424,128]{1,0:T(8,128)S(1)}, f32[424,128]{1,0:T(8,128)S(1)}, u32[]{:S(2)}, u32[]{:S(2)}) collective-permute-start(f32[424,128]{1,0:T(8,128)S(1)} %shard_map.161._____), channel_id=1, source_target_pairs={{16,32},{32,16},{48,64},{64,48},{80,96},{96,80},{112,128},{128,112... | collective-permute-start | bytes 651272 | tf_op jit(solution)/shard_map/ppermute | solution.py:625
  34.3 9.0 %collective-permute-start.3 = (f32[408,128]{1,0:T(8,128)S(1)}, f32[408,128]{1,0:T(8,128)S(1)}, u32[]{:S(2)}, u32[]{:S(2)}) collective-permute-start(f32[408,128]{1,0:T(8,128)S(1)} %get-tuple-element.50), channel_id=1, source_target_pairs={{0,16},{16,0},{32,48},{48,32},{64,80},{80,64},{96,112},{112,96},{1... | collective-permute-start | bytes 626696 | tf_op jit(solution)/shard_map/ppermute | solution.py:620
  36.3 7.0 %collective-permute-start.2 = (f32[256,128]{1,0:T(8,128)S(1)}, f32[256,128]{1,0:T(8,128)S(1)}, u32[]{:S(2)}, u32[]{:S(2)}) collective-permute-start(f32[256,128]{1,0:T(8,128)S(1)} %get-tuple-element.49), channel_id=1, source_target_pairs={{0,16},{16,0},{32,48},{48,32},{64,80},{80,64},{96,112},{112,96},{1... | collective-permute-start | bytes 393224 | tf_op jit(solution)/shard_map/ppermute | solution.py:619
  41.4 1.9 %copy-start = (bf16[256,128]{1,0:T(8,128)(2,1)S(1)}, bf16[256,128]{1,0:T(8,128)(2,1)}, u32[]{:S(2)}) copy-start(bf16[256,128]{1,0:T(8,128)(2,1)} %constant.2.clone.table_ref) | copy-start | bytes 196612
